TPU v7x, 32 devices: a whole 2x2x4 slice. The times are simulated.
32 devices in a mesh: slab: 4 (over x, core), weight: 8 (over z, y).
Axes of the slice: x: 2, y: 2, z: 4, core: 2. Of those that a mesh axis runs over, the one named last changes fastest.
Arguments:
- tokens: bfloat16 [8192, 1536], P(('slab', 'weight')), may hold values from -6 to 6
- w_qkv: bfloat16 [1536, 384], P('weight', 'slab'), may hold values from -0.1875 to 0.1875
- w_proj: bfloat16 [128, 1536], P('slab', 'weight'), may hold values from -1.5 to 1.5
- grad_out: bfloat16 [8192, 1536], P(('slab', 'weight')), may hold values from -0.59765625 to 0.59765625
Outputs:
- mixed: bfloat16 [8192, 1536], P(('slab', 'weight'))
- grad_tokens: bfloat16 [8192, 1536], P(('slab', 'weight'))
- grad_qkv: float32 [1536, 384], P('weight', 'slab')
- grad_proj: float32 [128, 1536], P('slab', 'weight')
All inputs are finite; a program needn't handle non-finite values.
Results may differ from a plain program's by a relative error of at most 0.013.
Values may be sent and summed in bfloat16 or wider, within the bound.
No kernel may reach another device: no remote copies, remote signals or barrier semaphores. Data moves between devices by JAX's collectives and lax.ppermute only.
A program may use at most 64 MiB of HBM per device.

v0:
```python
import jax
import jax.numpy as jnp
from jax import lax
from jax.sharding import PartitionSpec as P

HD = 128
HT = 2


def padded_2(shard, sides, width):
    for axis, dim in sides:
        size, length = (lax.axis_size(axis), shard.shape[dim])
        up = [(i, (i + 1) % size) for i in range(size - 1)]
        down = [(j, i) for i, j in up]
        last = lax.slice_in_dim(shard, length - width, length, axis=dim)
        leading = lax.slice_in_dim(shard, 0, width, axis=dim)
        before = lax.ppermute(last, axis, up)
        after = lax.ppermute(leading, axis, down)
        shard = jnp.concatenate([before, shard, after], axis=dim)
    return shard


def shifted(block, axis, distance):
    devices = range(lax.axis_size(axis))
    route = [(i - distance, i) for i in devices if i - distance in devices]
    return lax.ppermute(block, axis, route)


def rounded_copy(values):
    return lax.optimization_barrier(values.astype(jnp.bfloat16)).astype(jnp.float32)


def local(tokens, w_qkv, w_proj, grad_out):
    slab_count = lax.axis_size("slab")
    weight_count = lax.axis_size("weight")
    slab_index = lax.axis_index("slab")
    weight_index = lax.axis_index("weight")
    inverse_root = HD ** (-0.5)
    tile_rows = tokens.shape[0] // HT
    qkv_block, proj_block = (
        lax.all_gather(w_qkv, "slab", axis=1, tiled=True),
        lax.all_gather(w_proj, "slab", axis=0, tiled=True),
    )
    full_qkv, full_proj = (
        lax.all_gather(qkv_block, "weight", axis=0, tiled=True),
        lax.all_gather(proj_block, "weight", axis=1, tiled=True),
    )
    projected = jnp.dot(tokens, full_qkv, preferred_element_type=jnp.float32).astype(jnp.bfloat16)
    queries = projected[:, :HD].reshape(HT, tile_rows, HD)
    key_value = projected[:, HD:].reshape(HT, tile_rows, 2 * HD)
    grad_attended = jnp.dot(grad_out, full_proj.T, preferred_element_type=jnp.float32).astype(
        jnp.bfloat16
    )
    cotangent = grad_attended.reshape(HT, tile_rows, HD)
    in_time = padded_2(key_value[None], (("slab", 0),), 1)
    neighbours = padded_2(in_time[:, None], (("weight", 1),), 1)
    padded = jnp.pad(neighbours, ((0, 0), (0, 0), (1, 1), (0, 0), (0, 0)))
    window = jnp.stack([padded[:, :, row_start : row_start + 3] for row_start in range(HT)], 0)
    window = window.reshape(HT, 27, tile_rows, 2 * HD)
    offset_codes = jnp.arange(27, dtype=jnp.int32)
    time_offset = offset_codes // 9 - 1
    column_offset = offset_codes // 3 % 3 - 1
    row_offset = offset_codes % 3 - 1
    local_rows = jnp.arange(HT, dtype=jnp.int32)[:, None]
    inside = (
        (slab_index + time_offset >= 0)
        & (slab_index + time_offset < slab_count)
        & (weight_index + column_offset >= 0)
        & (weight_index + column_offset < weight_count)
    )[None, :]
    inside = (
        inside & (local_rows + row_offset[None, :] >= 0) & (local_rows + row_offset[None, :] < HT)
    )
    window_keys = window[..., :HD]
    window_values = window[..., HD:]
    scores = (
        jnp.einsum("rqd,rjkd->rqjk", queries, window_keys, preferred_element_type=jnp.float32)
        * inverse_root
    )
    scores = jnp.where(inside[:, None, :, None], scores, -jnp.inf)
    highest = jnp.max(scores, axis=(2, 3), keepdims=True)
    log_total = highest + jnp.log(jnp.sum(jnp.exp(scores - highest), axis=(2, 3), keepdims=True))
    weights = jnp.exp(scores - log_total)
    weights_half = weights.astype(jnp.bfloat16)
    attended = jnp.einsum(
        "rqjk,rjkd->rqd", weights_half, window_values, preferred_element_type=jnp.float32
    ).astype(jnp.bfloat16)
    attended_rows = attended.reshape(HT * tile_rows, HD)
    mixed = jnp.dot(attended_rows, full_proj, preferred_element_type=jnp.float32).astype(
        jnp.bfloat16
    )
    row_delta = jnp.sum(cotangent.astype(jnp.float32) * attended.astype(jnp.float32), axis=2)
    grad_weights = jnp.einsum(
        "rqd,rjkd->rqjk", cotangent, window_values, preferred_element_type=jnp.float32
    )
    grad_scores = (weights * (grad_weights - row_delta[:, :, None, None])).astype(jnp.bfloat16)
    grad_queries = (
        jnp.einsum("rqjk,rjkd->rqd", grad_scores, window_keys, preferred_element_type=jnp.float32)
        * inverse_root
    ).astype(jnp.bfloat16)
    grad_keys = (
        jnp.einsum("rqjk,rqd->rjkd", grad_scores, queries, preferred_element_type=jnp.float32)
        * inverse_root
    )
    grad_values = jnp.einsum(
        "rqjk,rqd->rjkd", weights_half, cotangent, preferred_element_type=jnp.float32
    )
    key_parts = jnp.concatenate([grad_keys, grad_values], axis=3).astype(jnp.bfloat16)
    key_parts = key_parts.reshape(HT, 3, 3, 3, tile_rows, 2 * HD)
    pair_total = jnp.zeros((HT + 2, tile_rows, 2 * HD), jnp.float32)
    for time_step in (-1, 0, 1):
        for column_step in (-1, 0, 1):
            parts = key_parts[:, time_step + 1, column_step + 1]
            if time_step == 0 and column_step == 0:
                received = parts
            else:
                received = shifted(
                    parts, ("slab", "weight"), time_step * weight_count + column_step
                )
            for row_place in range(3):
                pair_total = pair_total.at[row_place : row_place + HT].add(
                    received[:, row_place].astype(jnp.float32)
                )
    grad_pairs = pair_total[1 : HT + 1].astype(jnp.bfloat16).reshape(HT * tile_rows, 2 * HD)
    grad_rows = jnp.concatenate([grad_queries.reshape(HT * tile_rows, HD), grad_pairs], axis=1)
    grad_tokens = jnp.dot(grad_rows, full_qkv.T, preferred_element_type=jnp.float32).astype(
        jnp.bfloat16
    )
    first_part = jnp.dot(tokens.T, grad_rows, preferred_element_type=jnp.float32)
    second_part = jnp.dot(grad_out.T, attended_rows, preferred_element_type=jnp.float32)
    summed = lax.psum_scatter(
        rounded_copy(jnp.concatenate([first_part, second_part], axis=1)).astype(jnp.bfloat16),
        "weight",
        scatter_dimension=0,
        tiled=True,
    ).astype(jnp.float32)
    grad_qkv, proj_part = (
        lax.psum_scatter(summed[:, : 3 * HD], "slab", scatter_dimension=1, tiled=True),
        lax.psum_scatter(summed[:, 3 * HD :], "slab", scatter_dimension=1, tiled=True),
    )
    grad_proj = proj_part.T
    return (mixed, grad_tokens, grad_qkv, grad_proj)


def solution(mesh):
    in_specs = (
        P(("slab", "weight"), None),
        P("weight", "slab"),
        P("slab", "weight"),
        P(("slab", "weight"), None),
    )
    out_specs = (
        P(("slab", "weight"), None),
        P(("slab", "weight"), None),
        P("weight", "slab"),
        P("slab", "weight"),
    )
    return jax.shard_map(local, mesh=mesh, in_specs=in_specs, out_specs=out_specs, check_vma=False)
```

profile of v0, /device:TPU:0, one launch (start us, length us, event | category | flops | bytes accessed | tf_op | source)
XLA Modules:
  0.0 299.1 jit_solution(11361830387973733529)
XLA Ops:
  8.2 6.9 %all_gather.12 = bf16[192,384]{0,1:T(8,128)(2,1)S(1)} all-gather(bf16[192,96]{0,1:T(8,128)(2,1)S(1)} %copy.54), channel_id=1, replica_groups=mesh['slab'=4,'weight'=8] {'slab'}, dimensions={1}, use_global_device_ids=true | all-gather | bytes 184320 | tf_op jit(solution)/shard_map/all_gather | solution.py:41
  16.0 5.4 %all_gather.14 = bf16[128,192]{1,0:T(8,128)(2,1)S(1)} all-gather(bf16[32,192]{1,0:T(8,128)(2,1)} %param.60), channel_id=1, replica_groups=mesh['slab'=4,'weight'=8] {'slab'}, dimensions={0}, use_global_device_ids=true | all-gather | bytes 61440 | tf_op jit(solution)/shard_map/all_gather | solution.py:42
  21.6 37.1 %all-gather.2.cloned.1.call-done = bf16[1536,384]{1,0:T(8,128)(2,1)} async-done(((bf16[192,384]{1,0:T(8,128)(2,1)}), bf16[1536,384]{1,0:T(8,128)(2,1)}) %all-gather.2.cloned.1.call-update) | async-done | bytes 1179664 | tf_op jit(solution)/shard_map/all_gather | solution.py:45
  58.6 1.8 convolution_convert_fusion.5
  60.5 1.3 collective-permute-start.1
  61.8 3.0 %collective-permute-start = (bf16[1,2,128,256]{3,2,1,0:T(8,128)(2,1)S(1)}, bf16[1,2,128,256]{3,2,1,0:T(8,128)(2,1)S(1)}, u32[]{:S(2)}, u32[]{:S(2)}) collective-permute-start(bf16[1,2,128,256]{3,2,1,0:T(8,128)(2,1)S(1)} %bitcast.223), channel_id=1, source_target_pairs={{0,8},{8,16},{16,24},{1,9},{9,17},{17,25},{2,10},{10,18},{18,26},{... | collective-permute-start | bytes 393224 | tf_op jit(solution)/shard_map/ppermute | solution.py:17
  65.9 1.3 collective-permute-start.3
  67.2 4.6 %collective-permute-start.2 = (bf16[3,1,2,128,256]{4,3,2,0,1:T(8,128)(2,1)S(1)}, bf16[3,1,2,128,256]{4,3,2,0,1:T(8,128)(2,1)S(1)}, u32[]{:S(2)}, u32[]{:S(2)}) collective-permute-start(bf16[3,1,2,128,256]{4,3,2,0,1:T(8,128)(2,1)S(1)} %maximum_bitcast_fusion), channel_id=1, source_target_pairs={{0,1},{1,2},{2,3},{3,4},{4,5},{5,6},{6,7},{8,9},{9,10},{10,11},{11... | collective-permute-start | bytes 1179656 | tf_op jit(solution)/shard_map/ppermute | solution.py:17
  71.7 39.0 %all_gather.15 = bf16[128,1536]{0,1:T(8,128)(2,1)S(1)} all-gather(bf16[128,192]{0,1:T(8,128)(2,1)S(1)} %copy.59), channel_id=1, replica_groups=mesh['slab'=4,'weight'=8] {'weight'}, dimensions={1}, use_global_device_ids=true | all-gather | bytes 442368 | tf_op jit(solution)/shard_map/all_gather | solution.py:46
  113.8 1.3 multiply_reduce_fusion
  115.1 2.5 convolution_convert_fusion.4
  118.7 2.0 multiply_convert_fusion
  120.7 2.8 copy.66
  123.4 3.9 %copy.67 = bf16[2,3,3,3,128,128]{5,4,0,3,2,1:T(8,128)(2,1)} copy(bf16[2,3,3,3,128,128]{4,5,3,2,1,0:T(8,128)(2,1)} %bitcast.210) | data formatting | bytes 3538944 | tf_op jit(solution)/shard_map/concatenate | solution.py:108
  127.3 1.9 fusion.22
  129.3 1.4 collective-permute-start.4
  131.0 4.3 %collective-permute-start.11 = (bf16[2,3,128,256]{3,2,0,1:T(8,128)(2,1)S(1)}, bf16[2,3,128,256]{3,2,0,1:T(8,128)(2,1)S(1)}, u32[]{:S(2)}, u32[]{:S(2)}) collective-permute-start(bf16[2,3,128,256]{3,2,0,1:T(8,128)(2,1)S(1)} %get-tuple-element.344), channel_id=1, source_target_pairs={{0,9},{1,10},{2,11},{3,12},{4,13},{5,14},{6,15},{7,16},{8,17},{9,1... | collective-permute-start | bytes 1179656 | tf_op jit(solution)/shard_map/ppermute | solution.py:26
  135.3 1.3 collective-permute-start.5
  136.6 1.3 collective-permute-start.6
  137.9 1.3 collective-permute-start.7
  140.0 2.7 collective-permute-done.4
  142.7 2.7 collective-permute-start.8
  145.7 11.8 %collective-permute-start.9 = (bf16[2,3,128,256]{3,2,0,1:T(8,128)(2,1)S(1)}, bf16[2,3,128,256]{3,2,0,1:T(8,128)(2,1)S(1)}, u32[]{:S(2)}, u32[]{:S(2)}) collective-permute-start(bf16[2,3,128,256]{3,2,0,1:T(8,128)(2,1)S(1)} %get-tuple-element.351), channel_id=1, source_target_pairs={{0,7},{1,8},{2,9},{3,10},{4,11},{5,12},{6,13},{7,14},{8,15},{9,16}... | collective-permute-start | bytes 1179656 | tf_op jit(solution)/shard_map/ppermute | solution.py:26
  157.6 10.9 %collective-permute-start.10 = (bf16[2,3,128,256]{3,2,0,1:T(8,128)(2,1)S(1)}, bf16[2,3,128,256]{3,2,0,1:T(8,128)(2,1)S(1)}, u32[]{:S(2)}, u32[]{:S(2)}) collective-permute-start(bf16[2,3,128,256]{3,2,0,1:T(8,128)(2,1)S(1)} %get-tuple-element.352), channel_id=1, source_target_pairs={{0,8},{1,9},{2,10},{3,11},{4,12},{5,13},{6,14},{7,15},{8,16},{9,17... | collective-permute-start | bytes 1179656 | tf_op jit(solution)/shard_map/ppermute | solution.py:26
  169.1 5.4 %collective-permute-done.8 = bf16[2,3,128,256]{3,2,0,1:T(8,128)(2,1)S(1)} collective-permute-done((bf16[2,3,128,256]{3,2,0,1:T(8,128)(2,1)S(1)}, bf16[2,3,128,256]{3,2,0,1:T(8,128)(2,1)S(1)}, u32[]{:S(2)}, u32[]{:S(2)}) %collective-permute-start.8) | collective-permute-done | bytes 393248 | tf_op jit(solution)/shard_map/ppermute | solution.py:26
  176.0 1.6 copy.84
  177.7 70.2 %reduce-scatter.10.cloned.1.call-done = bf16[192,512]{1,0:T(8,128)(2,1)} async-done(((bf16[1536,512]{1,0:T(8,128)(2,1)}), bf16[192,512]{1,0:T(8,128)(2,1)}) %reduce-scatter.10.cloned.1.call-update) | async-done | bytes 196624
  249.8 1.3 convolution_convert_fusion.2
  252.6 1.5 convolution_convert_fusion.1
  254.1 15.9 %reduce-scatter.6.cloned.1.call-done = f32[192,96]{0,1:T(8,128)} async-done(((f32[192,384]{0,1:T(8,128)}), f32[192,96]{0,1:T(8,128)}) %reduce-scatter.6.cloned.1.call-update) | async-done | bytes 73744 | tf_op jit(solution)/shard_map/reduce_scatter | solution.py:138
  270.1 1.6 copy.68
  271.7 20.9 %reduce-scatter.8.cloned.1.call-done = f32[192,32]{0,1:T(8,128)} async-done(((f32[192,128]{0,1:T(8,128)}), f32[192,32]{0,1:T(8,128)}) %reduce-scatter.8.cloned.1.call-update) | async-done | bytes 24592 | tf_op jit(solution)/shard_map/reduce_scatter | solution.py:139
  (93 shorter events, 13.9 us)
Async XLA Ops:
  7.2 51.5 %copy-start = (bf16[256,1536]{1,0:T(8,128)(2,1)S(1)}, bf16[256,1536]{1,0:T(8,128)(2,1)}, u32[]{:S(2)}) copy-start(bf16[256,1536]{1,0:T(8,128)(2,1)} %param.58) | copy-start | bytes 2359300
  7.2 103.5 %copy-start.1 = (bf16[256,1536]{1,0:T(8,128)(2,1)S(1)}, bf16[256,1536]{1,0:T(8,128)(2,1)}, u32[]{:S(2)}) copy-start(bf16[256,1536]{1,0:T(8,128)(2,1)} %param.61) | copy-start | bytes 2359300
  7.2 51.5 %all-gather.2.cloned.1.call-start = ((), (), s32[]{:S(2)}) async-start(), calls=%async_computation.3 | async-start | bytes 1327104 | tf_op jit(solution)/shard_map/all_gather | solution.py:45
  15.9 231.9 %reduce-scatter.10.cloned.1.call-start = ((), (), s32[]{:S(2)}) async-start(), calls=%async_computation.6 | async-start | bytes 1769472
  60.5 4.4 %collective-permute-start.1 = (bf16[1,2,128,256]{3,2,1,0:T(8,128)(2,1)S(1)}, bf16[1,2,128,256]{3,2,1,0:T(8,128)(2,1)S(1)}, u32[]{:S(2)}, u32[]{:S(2)}) collective-permute-start(bf16[1,2,128,256]{3,2,1,0:T(8,128)(2,1)S(1)} %bitcast.222), channel_id=1, source_target_pairs={{8,0},{16,8},{24,16},{9,1},{17,9},{25,17},{10,2},{18,10},{26,18},{... | collective-permute-start | bytes 393224 | tf_op jit(solution)/shard_map/ppermute | solution.py:18
  61.8 4.0 %collective-permute-start = (bf16[1,2,128,256]{3,2,1,0:T(8,128)(2,1)S(1)}, bf16[1,2,128,256]{3,2,1,0:T(8,128)(2,1)S(1)}, u32[]{:S(2)}, u32[]{:S(2)}) collective-permute-start(bf16[1,2,128,256]{3,2,1,0:T(8,128)(2,1)S(1)} %bitcast.223), channel_id=1, source_target_pairs={{0,8},{8,16},{16,24},{1,9},{9,17},{17,25},{2,10},{10,18},{18,26},{... | collective-permute-start | bytes 393224 | tf_op jit(solution)/shard_map/ppermute | solution.py:17
  65.9 45.2 %collective-permute-start.3 = (bf16[3,1,2,128,256]{4,3,2,0,1:T(8,128)(2,1)S(1)}, bf16[3,1,2,128,256]{4,3,2,0,1:T(8,128)(2,1)S(1)}, u32[]{:S(2)}, u32[]{:S(2)}) collective-permute-start(bf16[3,1,2,128,256]{4,3,2,0,1:T(8,128)(2,1)S(1)} %maximum_bitcast_fusion), channel_id=1, source_target_pairs={{1,0},{2,1},{3,2},{4,3},{5,4},{6,5},{7,6},{9,8},{10,9},{11,10},{12... | collective-permute-start | bytes 1179656 | tf_op jit(solution)/shard_map/ppermute | solution.py:18
  67.2 43.9 %collective-permute-start.2 = (bf16[3,1,2,128,256]{4,3,2,0,1:T(8,128)(2,1)S(1)}, bf16[3,1,2,128,256]{4,3,2,0,1:T(8,128)(2,1)S(1)}, u32[]{:S(2)}, u32[]{:S(2)}) collective-permute-start(bf16[3,1,2,128,256]{4,3,2,0,1:T(8,128)(2,1)S(1)} %maximum_bitcast_fusion), channel_id=1, source_target_pairs={{0,1},{1,2},{2,3},{3,4},{4,5},{5,6},{6,7},{8,9},{9,10},{10,11},{11... | collective-permute-start | bytes 1179656 | tf_op jit(solution)/shard_map/ppermute | solution.py:17
  112.0 5.6 %copy-start.3 = (bf16[3,3,3,128,256]{4,3,2,1,0:T(8,128)(2,1)}, bf16[3,3,3,128,256]{4,3,2,1,0:T(8,128)(2,1)S(1)}, u32[]{:S(2)}) copy-start(bf16[3,3,3,128,256]{4,3,2,1,0:T(8,128)(2,1)S(1)} %copy.56) | copy-start | bytes 5308420
  112.2 5.4 %copy-start.5 = (bf16[3,3,3,128,256]{4,3,2,1,0:T(8,128)(2,1)}, bf16[3,3,3,128,256]{4,3,2,1,0:T(8,128)(2,1)S(1)}, u32[]{:S(2)}) copy-start(bf16[3,3,3,128,256]{4,3,2,1,0:T(8,128)(2,1)S(1)} %copy.57) | copy-start | bytes 5308420
  118.7 2.0 copy-start.7
  127.3 3.4 %copy-start.2 = (bf16[256,1536]{1,0:T(8,128)(2,1)S(1)}, bf16[256,1536]{1,0:T(8,128)(2,1)}, u32[]{:S(2)}) copy-start(bf16[256,1536]{1,0:T(8,128)(2,1)} %param.61) | copy-start | bytes 2359300
  127.3 11.9 %copy-start.4 = (bf16[3,3,3,128,256]{4,3,2,1,0:T(8,128)(2,1)S(1)}, bf16[3,3,3,128,256]{4,3,2,1,0:T(8,128)(2,1)}, u32[]{:S(2)}) copy-start(bf16[3,3,3,128,256]{4,3,2,1,0:T(8,128)(2,1)} %copy-done.3) | copy-start | bytes 5308420
  127.3 11.9 %copy-start.6 = (bf16[3,3,3,128,256]{4,3,2,1,0:T(8,128)(2,1)S(1)}, bf16[3,3,3,128,256]{4,3,2,1,0:T(8,128)(2,1)}, u32[]{:S(2)}) copy-start(bf16[3,3,3,128,256]{4,3,2,1,0:T(8,128)(2,1)} %copy-done.5) | copy-start | bytes 5308420
  127.3 11.9 %copy-start.8 = (bf16[2,128,27,128]{1,3,2,0:T(8,128)(2,1)S(1)}, bf16[2,128,27,128]{1,3,2,0:T(8,128)(2,1)}, u32[]{:S(2)}) copy-start(bf16[2,128,27,128]{1,3,2,0:T(8,128)(2,1)} %copy-done.7) | copy-start | bytes 5308420
  129.3 13.4 %collective-permute-start.4 = (bf16[2,3,128,256]{3,2,0,1:T(8,128)(2,1)S(1)}, bf16[2,3,128,256]{3,2,0,1:T(8,128)(2,1)S(1)}, u32[]{:S(2)}, u32[]{:S(2)}) collective-permute-start(bf16[2,3,128,256]{3,2,0,1:T(8,128)(2,1)S(1)} %get-tuple-element.345), channel_id=1, source_target_pairs={{9,0},{10,1},{11,2},{12,3},{13,4},{14,5},{15,6},{16,7},{17,8},{18,... | collective-permute-start | bytes 1179656 | tf_op jit(solution)/shard_map/ppermute | solution.py:26
  131.0 44.1 %collective-permute-start.11 = (bf16[2,3,128,256]{3,2,0,1:T(8,128)(2,1)S(1)}, bf16[2,3,128,256]{3,2,0,1:T(8,128)(2,1)S(1)}, u32[]{:S(2)}, u32[]{:S(2)}) collective-permute-start(bf16[2,3,128,256]{3,2,0,1:T(8,128)(2,1)S(1)} %get-tuple-element.344), channel_id=1, source_target_pairs={{0,9},{1,10},{2,11},{3,12},{4,13},{5,14},{6,15},{7,16},{8,17},{9,1... | collective-permute-start | bytes 1179656 | tf_op jit(solution)/shard_map/ppermute | solution.py:26
  135.3 10.3 %collective-permute-start.5 = (bf16[2,3,128,256]{3,2,0,1:T(8,128)(2,1)S(1)}, bf16[2,3,128,256]{3,2,0,1:T(8,128)(2,1)S(1)}, u32[]{:S(2)}, u32[]{:S(2)}) collective-permute-start(bf16[2,3,128,256]{3,2,0,1:T(8,128)(2,1)S(1)} %get-tuple-element.346), channel_id=1, source_target_pairs={{8,0},{9,1},{10,2},{11,3},{12,4},{13,5},{14,6},{15,7},{16,8},{17,9... | collective-permute-start | bytes 1179656 | tf_op jit(solution)/shard_map/ppermute | solution.py:26
  136.6 21.0 %collective-permute-start.6 = (bf16[2,3,128,256]{3,2,0,1:T(8,128)(2,1)S(1)}, bf16[2,3,128,256]{3,2,0,1:T(8,128)(2,1)S(1)}, u32[]{:S(2)}, u32[]{:S(2)}) collective-permute-start(bf16[2,3,128,256]{3,2,0,1:T(8,128)(2,1)S(1)} %get-tuple-element.347), channel_id=1, source_target_pairs={{7,0},{8,1},{9,2},{10,3},{11,4},{12,5},{13,6},{14,7},{15,8},{16,9}... | collective-permute-start | bytes 1179656 | tf_op jit(solution)/shard_map/ppermute | solution.py:26
  137.9 30.8 %collective-permute-start.7 = (bf16[2,3,128,256]{3,2,0,1:T(8,128)(2,1)S(1)}, bf16[2,3,128,256]{3,2,0,1:T(8,128)(2,1)S(1)}, u32[]{:S(2)}, u32[]{:S(2)}) collective-permute-start(bf16[2,3,128,256]{3,2,0,1:T(8,128)(2,1)S(1)} %get-tuple-element.348), channel_id=1, source_target_pairs={{1,0},{2,1},{3,2},{4,3},{5,4},{6,5},{7,6},{8,7},{9,8},{10,9},{11,1... | collective-permute-start | bytes 1179656 | tf_op jit(solution)/shard_map/ppermute | solution.py:26
  142.7 31.8 %collective-permute-start.8 = (bf16[2,3,128,256]{3,2,0,1:T(8,128)(2,1)S(1)}, bf16[2,3,128,256]{3,2,0,1:T(8,128)(2,1)S(1)}, u32[]{:S(2)}, u32[]{:S(2)}) collective-permute-start(bf16[2,3,128,256]{3,2,0,1:T(8,128)(2,1)S(1)} %get-tuple-element.350), channel_id=1, source_target_pairs={{0,1},{1,2},{2,3},{3,4},{4,5},{5,6},{6,7},{7,8},{8,9},{9,10},{10,1... | collective-permute-start | bytes 1179656 | tf_op jit(solution)/shard_map/ppermute | solution.py:26
  145.7 29.1 %collective-permute-start.9 = (bf16[2,3,128,256]{3,2,0,1:T(8,128)(2,1)S(1)}, bf16[2,3,128,256]{3,2,0,1:T(8,128)(2,1)S(1)}, u32[]{:S(2)}, u32[]{:S(2)}) collective-permute-start(bf16[2,3,128,256]{3,2,0,1:T(8,128)(2,1)S(1)} %get-tuple-element.351), channel_id=1, source_target_pairs={{0,7},{1,8},{2,9},{3,10},{4,11},{5,12},{6,13},{7,14},{8,15},{9,16}... | collective-permute-start | bytes 1179656 | tf_op jit(solution)/shard_map/ppermute | solution.py:26
  157.6 17.3 %collective-permute-start.10 = (bf16[2,3,128,256]{3,2,0,1:T(8,128)(2,1)S(1)}, bf16[2,3,128,256]{3,2,0,1:T(8,128)(2,1)S(1)}, u32[]{:S(2)}, u32[]{:S(2)}) collective-permute-start(bf16[2,3,128,256]{3,2,0,1:T(8,128)(2,1)S(1)} %get-tuple-element.352), channel_id=1, source_target_pairs={{0,8},{1,9},{2,10},{3,11},{4,12},{5,13},{6,14},{7,15},{8,16},{9,17... | collective-permute-start | bytes 1179656 | tf_op jit(solution)/shard_map/ppermute | solution.py:26
  177.6 75.0 %copy-start.9 = (bf16[1536,384]{1,0:T(8,128)(2,1)S(1)}, bf16[1536,384]{1,0:T(8,128)(2,1)}, u32[]{:S(2)}) copy-start(bf16[1536,384]{1,0:T(8,128)(2,1)} %all-gather.2.cloned.1.call-done) | copy-start | bytes 3538948
  177.6 92.4 %reduce-scatter.6.cloned.1.call-start = ((), (), s32[]{:S(2)}) async-start(), calls=%async_computation.4 | async-start | bytes 491520 | tf_op jit(solution)/shard_map/reduce_scatter | solution.py:138
  249.7 42.9 %reduce-scatter.8.cloned.1.call-start = ((), (), s32[]{:S(2)}) async-start(), calls=%async_computation.5 | async-start | bytes 163840 | tf_op jit(solution)/shard_map/reduce_scatter | solution.py:139
Sparse Core Ops, SparseCore 0:
  16.0 42.5 all-gather.1
  177.7 70.0 reduce-scatter.9
  250.3 19.6 reduce-scatter.5
  272.9 19.6 reduce-scatter.7
where the time goes:
time: 300 us; the launch traced here: 299 us
  waiting for transfers between devices  153 us (51%)
  blocking collectives  51.3 us (17%)
  starting transfers between devices  45.4 us (15%)
  local copies, waits for them, and re-layouts  16.1 us (5%)
  between operations  14.4 us (5%)
  matrix products  13.9 us (5%)
  other arithmetic  4.85 us (2%)
    unnamed x5, waiting for transfers between devices  70.2 us
    all_gather x1, blocking collectives, local(): lax.all_gather(proj_block, 'weight', axis=1, tiled=True)  39 us
    all_gather x1, waiting for transfers between devices, local(): lax.all_gather(qkv_block, 'weight', axis=0, tiled=True)  37.1 us
    ppermute x8, starting transfers between devices, shifted(): return lax.ppermute(block, axis, route)  35 us
    reduce_scatter x1, waiting for transfers between devices, local(): lax.psum_scatter(summed[:, 3 * HD:], 'slab', scatter_dimension=1, tiled=T...  20.9 us
    reduce_scatter x1, waiting for transfers between devices, local(): lax.psum_scatter(summed[:, :3 * HD], 'slab', scatter_dimension=1, tiled=T...  15.9 us
    ppermute x8, waiting for transfers between devices, shifted(): return lax.ppermute(block, axis, route)  8.16 us
    ppermute x2, starting transfers between devices, padded_2(): before = lax.ppermute(last, axis, up)  7.61 us
  transfers between devices with their start and end apart: 16, of which 7 were waited for; matrix products, arithmetic and copies ran while one was open for 3% of the time, Pallas kernels for 0%

commit v1 on v0

v1 whole, which is shorter than its diff:
```python
import functools

import jax
import jax.numpy as jnp
from jax import lax
from jax.experimental import pallas as pl
from jax.experimental.pallas import tpu as pltpu
from jax.sharding import PartitionSpec as P

HD = 128
AXES = ("slab", "weight")
BF = jnp.bfloat16
F32 = jnp.float32
VMEM = pl.BlockSpec(memory_space=pltpu.VMEM)
SMEM = pl.BlockSpec(memory_space=pltpu.SMEM)


def bits_of(size):
    return size.bit_length() - 1


def exchange_steps(slabs, weights):
    steps = [("weight", bit) for bit in reversed(range(1, bits_of(weights)))]
    steps += [("slab", bit) for bit in reversed(range(2, bits_of(slabs)))]
    return steps + [("first", 0), ("second", 0)]


def step_mask(step, odd):
    kind, bit = step
    if kind == "weight":
        return 0, 1 << bit
    if kind == "slab":
        return 1 << bit, 0
    along_slab = 1 - odd if kind == "first" else odd
    return 2 * along_slab, 1 - along_slab


def block_owner(block, steps, slab, weight, odd):
    for place, step in enumerate(steps):
        if block >> place & 1:
            slab_mask, weight_mask = step_mask(step, odd)
            slab, weight = slab ^ slab_mask, weight ^ weight_mask
    return slab, weight


def step_pairs(step, slabs, weights):
    pairs = []
    for s in range(slabs):
        for w in range(weights):
            slab_mask, weight_mask = step_mask(step, s & 1)
            pairs.append((s * weights + w, (s ^ slab_mask) * weights + (w ^ weight_mask)))
    return pairs


def core_pairs(slabs, weights):
    return [(s * weights + w, (s ^ 1) * weights + w) for s in range(slabs) for w in range(weights)]


def paired(index, size, odd):
    other = ((index + odd) ^ 1) - odd
    return other if 0 <= other < size else None


def slab_pairs(odd, slabs, weights):
    return [
        (s * weights + w, paired(s, slabs, odd) * weights + w)
        for s in range(slabs)
        for w in range(weights)
        if paired(s, slabs, odd) is not None
    ]


def weight_pairs(odd, slabs, weights):
    return [
        (s * weights + w, s * weights + paired(w, weights, odd))
        for s in range(slabs)
        for w in range(weights)
        if paired(w, weights, odd) is not None
    ]


def dot(a, b, dims=((1,), (0,))):
    return lax.dot_general(a, b, (dims, ((), ())), preferred_element_type=F32)


def pack_kernel(qkv_ref, proj_ref, out_ref):
    out_ref[0] = jnp.concatenate([qkv_ref[...], proj_ref[...].T], axis=1)


def project_kernel(steps, split, index, own, got, tokens, grad_out, q_ref, kv_ref, co_ref, full):
    slab, weight = index[0], index[1]
    odd = slab & 1
    rows = own.shape[1]
    for half, (source, where, parity) in enumerate(((own, slab, odd), (got, slab ^ 1, 1 - odd))):
        for block in range(own.shape[0]):
            s, w = block_owner(block, steps, where, weight, parity)
            full[s, pl.ds(pl.multiple_of(w * rows, rows), rows), :] = source[block]
    slabs = full.shape[0]
    projected = [dot(tokens[...], full[s])[:, :split].astype(BF) for s in range(slabs)]
    cotangent = [dot(grad_out[...], full[s])[:, split:].astype(BF) for s in range(slabs)]
    projected = jnp.concatenate(projected, axis=1)
    q_ref[...] = projected[:, :HD]
    kv_ref[...] = projected[:, HD:]
    co_ref[...] = jnp.concatenate(cotangent, axis=1)


def attention_kernel(
    sizes, index, q_ref, co_ref, own, even, odd, slab_even, slab_odd,
    att_ref, dq_ref, parts_own, parts_even, parts_odd, scores,
):
    slab, weight = index[0], index[1]
    slabs, weights = sizes
    root = HD ** (-0.5)
    slab_inside = (slab > 0) & (slab < slabs - 1)
    weight_inside = (weight > 0) & (weight < weights - 1)
    blocks = [own, even, odd]
    blocks += [slab_even.at[i] for i in range(3)] + [slab_odd.at[i] for i in range(3)]
    outs = [parts.at[i] for parts in (parts_own, parts_even, parts_odd) for i in range(3)]
    query, cotangent = q_ref[...], co_ref[...]
    highest = None
    for j, block in enumerate(blocks):
        part = dot(query, block[:, :HD], ((1,), (1,))) * root
        present = None
        if j % 3 == 2:
            present = weight_inside
        if j >= 6:
            present = slab_inside if present is None else present & slab_inside
        if present is not None:
            part = part + jnp.where(present, 0.0, -jnp.inf)
        scores[j] = part
        highest = part if highest is None else jnp.maximum(highest, part)
    highest = jnp.max(highest, axis=1, keepdims=True)
    total = None
    for j in range(9):
        part = jnp.exp(scores[j] - highest)
        scores[j] = part
        total = part if total is None else total + part
    scale = 1.0 / jnp.sum(total, axis=1, keepdims=True)
    attended = None
    for j, block in enumerate(blocks):
        weighted = dot((scores[j] * scale).astype(BF), block[:, HD:])
        attended = weighted if attended is None else attended + weighted
    attended = attended.astype(BF)
    att_ref[...] = attended
    delta = jnp.sum(cotangent.astype(F32) * attended.astype(F32), axis=1, keepdims=True)
    grad_query = None
    for j, (block, out) in enumerate(zip(blocks, outs)):
        grad = dot(cotangent, block[:, HD:], ((1,), (1,)))
        part = scores[j] * scale
        grad = (part * (grad - delta)).astype(BF)
        step = dot(grad, block[:, :HD])
        grad_query = step if grad_query is None else grad_query + step
        out[:, :HD] = (dot(grad, query, ((0,), (0,))) * root).astype(BF)
        out[:, HD:] = dot(part.astype(BF), cotangent, ((0,), (0,))).astype(BF)
    dq_ref[...] = (grad_query * root).astype(BF)


def mixed_kernel(split, att_ref, full, out_ref):
    slabs = full.shape[0]
    width = HD // slabs
    attended = att_ref[...]
    zeros = jnp.zeros((attended.shape[0], split), BF)
    total = None
    for s in range(slabs):
        part = jnp.concatenate([zeros, attended[:, s * width : (s + 1) * width]], axis=1)
        part = dot(part, full[s], ((1,), (1,)))
        total = part if total is None else total + part
    out_ref[...] = total.astype(BF)


def weight_grads_kernel(
    steps, slabs, split, index, tokens, grad_out, dq, own, even, odd, att_ref,
    rows_ref, keep, send, full,
):
    slab, weight = index[0], index[1]
    parity = slab & 1
    pairs = own[...] + even[...].astype(F32) + odd[...].astype(F32)
    rows = jnp.concatenate([dq[...], pairs.astype(BF)], axis=1)
    rows_ref[...] = rows
    attended = att_ref[...]
    width = HD // slabs
    count = rows.shape[0]
    left_zeros = jnp.zeros((count, width), BF)
    right_zeros = jnp.zeros((count, split), BF)
    left, right = [], []
    for s in range(slabs):
        left += [rows[:, s * split : (s + 1) * split], left_zeros]
        right += [right_zeros, attended[:, s * width : (s + 1) * width]]
    grads = dot(tokens[...], jnp.concatenate(left, axis=1), ((0,), (0,)))
    grads = grads + dot(grad_out[...], jnp.concatenate(right, axis=1), ((0,), (0,)))
    lanes = split + width
    for s in range(slabs):
        full[s] = grads[:, s * lanes : (s + 1) * lanes].astype(BF)
    size = keep.shape[1]
    for target, where, odd_core in ((send, slab ^ 1, 1 - parity), (keep, slab, parity)):
        for block in range(keep.shape[0]):
            s, w = block_owner(block, steps, where, weight, odd_core)
            target[block] = full[s, pl.ds(pl.multiple_of(w * size, size), size), :]


def grad_tokens_kernel(split, rows_ref, full, out_ref):
    slabs = full.shape[0]
    rows = rows_ref[...]
    zeros = jnp.zeros((rows.shape[0], HD // slabs), BF)
    total = None
    for s in range(slabs):
        part = jnp.concatenate([rows[:, s * split : (s + 1) * split], zeros], axis=1)
        part = dot(part, full[s], ((1,), (1,)))
        total = part if total is None else total + part
    out_ref[...] = total.astype(BF)


def unpack_kernel(split, keep, got, qkv_ref, proj_ref):
    total = keep[0] + got[0].astype(F32)
    qkv_ref[...] = total[:, :split]
    proj_ref[...] = total[:, split:].T


def call(kernel, outs, args, scratch=(), scalars=0):
    shapes = [jax.ShapeDtypeStruct(shape, kind) for shape, kind in outs]
    return pl.pallas_call(
        kernel,
        out_shape=shapes,
        in_specs=[SMEM] * scalars + [VMEM] * (len(args) - scalars),
        out_specs=[VMEM] * len(outs),
        scratch_shapes=list(scratch),
    )(*args)


def local(slabs, weights, tokens, w_qkv, w_proj, grad_out):
    steps = exchange_steps(slabs, weights)
    index = jnp.stack([lax.axis_index("slab"), lax.axis_index("weight")]).astype(jnp.int32)
    count, features = tokens.shape
    rows, split = w_qkv.shape
    lanes = split + HD // slabs

    def swap(values, pairs):
        return lax.ppermute(values, AXES, pairs)

    (held,) = call(pack_kernel, [((1, rows, lanes), BF)], [w_qkv, w_proj])
    for step in steps:
        held = jnp.concatenate([held, swap(held, step_pairs(step, slabs, weights))], axis=0)
    got = swap(held, core_pairs(slabs, weights))
    query, key_value, cotangent, full = call(
        functools.partial(project_kernel, steps, split),
        [((count, HD), BF), ((count, 2 * HD), BF), ((count, HD), BF), ((slabs, features, lanes), BF)],
        [index, held, got, tokens, grad_out],
        scalars=1,
    )

    weight_even, weight_odd = (weight_pairs(odd, slabs, weights) for odd in (0, 1))
    slab_even, slab_odd = (slab_pairs(odd, slabs, weights) for odd in (0, 1))
    even, odd = swap(key_value, weight_even), swap(key_value, weight_odd)
    columns = jnp.stack([key_value, even, odd])
    across_even, across_odd = swap(columns, slab_even), swap(columns, slab_odd)
    pair = (3, count, 2 * HD)
    attended, grad_query, parts_own, parts_even, parts_odd = call(
        functools.partial(attention_kernel, (slabs, weights)),
        [((count, HD), BF), ((count, HD), BF), (pair, BF), (pair, BF), (pair, BF)],
        [index, query, cotangent, key_value, even, odd, across_even, across_odd],
        scratch=[pltpu.VMEM((9, count, count), F32)],
        scalars=1,
    )
    parts_even, parts_odd = swap(parts_even, slab_even), swap(parts_odd, slab_odd)
    (mixed,) = call(
        functools.partial(mixed_kernel, split), [((count, features), BF)], [attended, full]
    )

    def summed(column):
        return (
            parts_own[column].astype(F32)
            + parts_even[column].astype(F32)
            + parts_odd[column].astype(F32)
        )

    even = swap(summed(1).astype(BF), weight_even)
    odd = swap(summed(2).astype(BF), weight_odd)
    half = (1 << len(steps), rows, lanes)
    grad_rows, keep, send = call(
        functools.partial(weight_grads_kernel, steps, slabs, split),
        [((count, 3 * HD), BF), (half, BF), (half, BF)],
        [index, tokens, grad_out, grad_query, summed(0), even, odd, attended],
        scratch=[pltpu.VMEM((slabs, features, lanes), BF)],
        scalars=1,
    )
    got = swap(send, core_pairs(slabs, weights))
    (grad_tokens,) = call(
        functools.partial(grad_tokens_kernel, split), [((count, features), BF)], [grad_rows, full]
    )
    for step in reversed(steps):
        near = keep.shape[0] // 2
        send = (keep[near:].astype(F32) + got[near:].astype(F32)).astype(BF)
        keep = keep[:near].astype(F32) + got[:near].astype(F32)
        got = swap(send, step_pairs(step, slabs, weights))
    grad_qkv, grad_proj = call(
        functools.partial(unpack_kernel, split),
        [((rows, split), F32), ((HD // slabs, rows), F32)],
        [keep, got],
    )
    return mixed, grad_tokens, grad_qkv, grad_proj


def solution(mesh):
    in_specs = (
        P(AXES, None),
        P("weight", "slab"),
        P("slab", "weight"),
        P(AXES, None),
    )
    out_specs = (
        P(AXES, None),
        P(AXES, None),
        P("weight", "slab"),
        P("slab", "weight"),
    )
    body = functools.partial(local, mesh.shape["slab"], mesh.shape["weight"])
    return jax.shard_map(body, mesh=mesh, in_specs=in_specs, out_specs=out_specs, check_vma=False)
```

time: 300 us -> 123 us (0.41)
  waiting for transfers between devices: 153 us -> 39.3 us
  blocking collectives: 51.3 us -> 0 us
  Pallas kernels: 0 us -> 24.4 us
  matrix products: 13.9 us -> 0 us
  between operations: 14.4 us -> 0.78 us
  local copies, waits for them, and re-layouts: 16.1 us -> 3.98 us
  other arithmetic: 4.85 us -> 8.14 us
    unnamed x5 -> x0, waiting for transfers between devices: 70.2 us -> none
    all_gather x3 -> x0, blocking collectives: 51.3 us -> none  [the longest x1 39 us: local(): lax.all_gather(proj_block, 'weight', axis=1, tiled=True)]
    all_gather x1 -> x0, waiting for transfers between devices: 37.1 us -> none  [local(): lax.all_gather(qkv_block, 'weight', axis=0, tiled=True)]
    reduce_scatter x2 -> x0, waiting for transfers between devices: 36.8 us -> none  [the longest x1 20.9 us: local(): lax.psum_scatter(summed[:, 3 * HD:], 'slab', scatter_dimension=1, tiled=T...]
    ppermute x12 -> x18, waiting for transfers between devices: 9.11 us -> 39.3 us  [swap(): return lax.ppermute(values, AXES, pairs)]
    pallas_call x0 -> x7, Pallas kernels: none -> 24.4 us  [call(): pl.pallas_call(kernel, out_shape=shapes, in_specs=[SMEM] * scalars + [VME...]
    dot_general x12 -> x0, matrix products: 13.9 us -> none  [the longest x1 2.46 us: local(): jnp.einsum('rqjk,rqd->rjkd', weights_half, cotangent, preferred_element_t...]
    concatenate x2 -> x1, local copies, waits for them, and re-layouts: 6.66 us -> 0.05 us  [local(): jnp.concatenate([held, swap(held, step_pairs(step, slabs, weights))], axi...]
  transfers between devices with their start and end apart: 16 -> 18, of which waited for: 7 -> 13; matrix products, arithmetic and copies ran while one was open for 3% -> 1% of each run, Pallas kernels for 0% -> 6%
where the time goes in v1:
time: 123 us
  starting transfers between devices  45.9 us (37%)
  waiting for transfers between devices  39.3 us (32%)
  Pallas kernels  24.4 us (20%)
  other arithmetic  8.14 us (7%)
  local copies, waits for them, and re-layouts  3.98 us (3%)
    ppermute x18, starting transfers between devices, swap(): return lax.ppermute(values, AXES, pairs)  45.9 us
    ppermute x18, waiting for transfers between devices, swap(): return lax.ppermute(values, AXES, pairs)  39.3 us
    pallas_call x7, Pallas kernels, call(): pl.pallas_call(kernel, out_shape=shapes, in_specs=[SMEM] * scalars + [VME...  24.4 us
    unnamed x22, local copies, waits for them, and re-layouts  3.93 us
    concatenate x3, other arithmetic, local(): jnp.concatenate([held, swap(held, step_pairs(step, slabs, weights))], axi...  2.47 us
  transfers between devices with their start and end apart: 18, of which 13 were waited for; matrix products, arithmetic and copies ran while one was open for 1% of the time, Pallas kernels for 6%

profile of v1, /device:TPU:0, one launch (start us, length us, event | category | flops | bytes accessed | tf_op | source)
XLA Modules:
  0.0 122.5 jit_solution(6679860531132257285)
XLA Ops:
  0.6 1.6 %shard_map.75 = bf16[1,192,128]{2,1,0:T(8,128)(2,1)} custom-call(bf16[192,96]{1,0:T(8,128)(2,1)} %qkv_ref.1, bf16[32,192]{1,0:T(8,128)(2,1)} %proj_ref.1), custom_call_target="tpu_custom_call" | custom-call | tf_op jit(solution)/shard_map/pallas_call | solution.py:221
  2.2 4.1 %collective-permute-start = (bf16[1,192,128]{2,1,0:T(8,128)(2,1)}, bf16[1,192,128]{2,1,0:T(8,128)(2,1)S(1)}, u32[]{:S(2)}, u32[]{:S(2)}) collective-permute-start(bf16[1,192,128]{2,1,0:T(8,128)(2,1)} %shard_map.75), channel_id=1, source_target_pairs={{0,4},{1,5},{2,6},{3,7},{4,0},{5,1},{6,2},{7,3},{8,12},{9,13},{10,... | collective-permute-start | bytes 147464 | tf_op jit(solution)/shard_map/ppermute | solution.py:238
  6.3 2.8 %collective-permute-done = bf16[1,192,128]{2,1,0:T(8,128)(2,1)S(1)} collective-permute-done((bf16[1,192,128]{2,1,0:T(8,128)(2,1)}, bf16[1,192,128]{2,1,0:T(8,128)(2,1)S(1)}, u32[]{:S(2)}, u32[]{:S(2)}) %collective-permute-start) | collective-permute-done | bytes 49184 | tf_op jit(solution)/shard_map/ppermute | solution.py:238
  9.9 1.4 %collective-permute-start.1 = (bf16[2,192,128]{2,1,0:T(8,128)(2,1)S(1)}, bf16[2,192,128]{2,1,0:T(8,128)(2,1)S(1)}, u32[]{:S(2)}, u32[]{:S(2)}) collective-permute-start(bf16[2,192,128]{2,1,0:T(8,128)(2,1)S(1)} %pad_maximum_fusion.3), channel_id=1, source_target_pairs={{0,2},{1,3},{2,0},{3,1},{4,6},{5,7},{6,4},{7,5},{8,10},{9,11},{10,... | collective-permute-start | bytes 294920 | tf_op jit(solution)/shard_map/ppermute | solution.py:238
  11.3 3.2 %collective-permute-done.1 = bf16[2,192,128]{2,1,0:T(8,128)(2,1)S(1)} collective-permute-done((bf16[2,192,128]{2,1,0:T(8,128)(2,1)S(1)}, bf16[2,192,128]{2,1,0:T(8,128)(2,1)S(1)}, u32[]{:S(2)}, u32[]{:S(2)}) %collective-permute-start.1) | collective-permute-done | bytes 98336 | tf_op jit(solution)/shard_map/ppermute | solution.py:238
  15.4 1.8 %collective-permute-start.2 = (bf16[4,192,128]{2,1,0:T(8,128)(2,1)S(1)}, bf16[4,192,128]{2,1,0:T(8,128)(2,1)S(1)}, u32[]{:S(2)}, u32[]{:S(2)}) collective-permute-start(bf16[4,192,128]{2,1,0:T(8,128)(2,1)S(1)} %pad_maximum_fusion.2), channel_id=1, source_target_pairs={{0,16},{1,17},{2,18},{3,19},{4,20},{5,21},{6,22},{7,23},{8,9},{9,8... | collective-permute-start | bytes 589832 | tf_op jit(solution)/shard_map/ppermute | solution.py:238
  17.1 4.3 %collective-permute-done.2 = bf16[4,192,128]{2,1,0:T(8,128)(2,1)S(1)} collective-permute-done((bf16[4,192,128]{2,1,0:T(8,128)(2,1)S(1)}, bf16[4,192,128]{2,1,0:T(8,128)(2,1)S(1)}, u32[]{:S(2)}, u32[]{:S(2)}) %collective-permute-start.2) | collective-permute-done | bytes 196640 | tf_op jit(solution)/shard_map/ppermute | solution.py:238
  22.3 2.0 %collective-permute-start.3 = (bf16[8,192,128]{2,1,0:T(8,128)(2,1)S(1)}, bf16[8,192,128]{2,1,0:T(8,128)(2,1)S(1)}, u32[]{:S(2)}, u32[]{:S(2)}) collective-permute-start(bf16[8,192,128]{2,1,0:T(8,128)(2,1)S(1)} %pad_maximum_fusion), channel_id=1, source_target_pairs={{0,1},{1,0},{2,3},{3,2},{4,5},{5,4},{6,7},{7,6},{8,24},{9,25},{10,... | collective-permute-start | bytes 1179656 | tf_op jit(solution)/shard_map/ppermute | solution.py:238
  25.1 5.0 %collective-permute-done.3 = bf16[8,192,128]{2,1,0:T(8,128)(2,1)S(1)} collective-permute-done((bf16[8,192,128]{2,1,0:T(8,128)(2,1)S(1)}, bf16[8,192,128]{2,1,0:T(8,128)(2,1)S(1)}, u32[]{:S(2)}, u32[]{:S(2)}) %collective-permute-start.3) | collective-permute-done | bytes 393248 | tf_op jit(solution)/shard_map/ppermute | solution.py:238
  31.0 1.6 %collective-permute-done.4.got = bf16[16,192,128]{2,1,0:T(8,128)(2,1)S(1)} collective-permute-done((bf16[16,192,128]{2,1,0:T(8,128)(2,1)S(1)}, bf16[16,192,128]{2,1,0:T(8,128)(2,1)S(1)}, u32[]{:S(2)}, u32[]{:S(2)}) %collective-permute-start.4) | collective-permute-done | bytes 786464 | tf_op jit(solution)/shard_map/ppermute | solution.py:238
  33.5 4.4 %shard_map.76 = (bf16[256,128]{1,0:T(8,128)(2,1)}, bf16[256,256]{1,0:T(8,128)(2,1)}, bf16[256,128]{1,0:T(8,128)(2,1)}, bf16[4,1536,128]{2,1,0:T(8,128)(2,1)}) custom-call(s32[2]{0:T(128)} %pad_add_fusion.index, bf16[16,192,128]{2,1,0:T(8,128)(2,1)} %copy-done, bf16[16,192,128]{2,1,0:T(8,128)(2,1)} %copy-done.1, bf16[256,1536]{1,0:T(8,128)(2,1)} %tokens.3, ...), custom_call_target="tpu_custom_call" | custom-call | tf_op jit(solution)/shard_map/pallas_call | solution.py:221
  37.8 1.9 %collective-permute-start.5 = (bf16[256,256]{1,0:T(8,128)(2,1)}, bf16[256,256]{1,0:T(8,128)(2,1)S(1)}, u32[]{:S(2)}, u32[]{:S(2)}) collective-permute-start(bf16[256,256]{1,0:T(8,128)(2,1)} %get-tuple-element.20.own), channel_id=1, source_target_pairs={{0,1},{1,0},{2,3},{3,2},{4,5},{5,4},{6,7},{7,6},{8,9},{9,8},{10,11... | collective-permute-start | bytes 393224 | tf_op jit(solution)/shard_map/ppermute | solution.py:238
  40.4 3.3 %collective-permute-done.5.even = bf16[256,256]{1,0:T(8,128)(2,1)S(1)} collective-permute-done((bf16[256,256]{1,0:T(8,128)(2,1)}, bf16[256,256]{1,0:T(8,128)(2,1)S(1)}, u32[]{:S(2)}, u32[]{:S(2)}) %collective-permute-start.5) | collective-permute-done | bytes 131104 | tf_op jit(solution)/shard_map/ppermute | solution.py:238
  47.4 6.3 %shard_map.77 = (bf16[256,128]{1,0:T(8,128)(2,1)}, bf16[256,128]{1,0:T(8,128)(2,1)}, bf16[3,256,256]{2,1,0:T(8,128)(2,1)}, bf16[3,256,256]{2,1,0:T(8,128)(2,1)}, bf16[3,256,256]{2,1,0:T(8,128)(2,1)}) custom-call(s32[2]{0:T(128)} %pad_add_fusion.index, bf16[256,128]{1,0:T(8,128)(2,1)} %get-tuple-element.18.q_ref, bf16[256,128]{1,0:T(8,128)(2,1)} %get-tuple-element.19.co_ref, ...), custom_call_target="tpu_custom_call" | custom-call | tf_op jit(solution)/shard_map/pallas_call | solution.py:221
  54.4 10.4 %collective-permute-start.9 = (bf16[3,256,256]{2,1,0:T(8,128)(2,1)}, bf16[3,256,256]{2,1,0:T(8,128)(2,1)S(1)}, u32[]{:S(2)}, u32[]{:S(2)}) collective-permute-start(bf16[3,256,256]{2,1,0:T(8,128)(2,1)} %get-tuple-element.25), channel_id=1, source_target_pairs={{0,8},{1,9},{2,10},{3,11},{4,12},{5,13},{6,14},{7,15},{8,0},{9,1},... | collective-permute-start | bytes 1179656 | tf_op jit(solution)/shard_map/ppermute | solution.py:238
  64.8 1.6 %collective-permute-done.9 = bf16[3,256,256]{2,1,0:T(8,128)(2,1)S(1)} collective-permute-done((bf16[3,256,256]{2,1,0:T(8,128)(2,1)}, bf16[3,256,256]{2,1,0:T(8,128)(2,1)S(1)}, u32[]{:S(2)}, u32[]{:S(2)}) %collective-permute-start.9) | collective-permute-done | bytes 393248 | tf_op jit(solution)/shard_map/ppermute | solution.py:238
  66.4 1.9 %fusion.3 = (bf16[256,256]{1,0:T(8,128)(2,1)S(1)}, bf16[256,256]{1,0:T(8,128)(2,1)S(1)}, f32[256,256]{1,0:T(8,128)}) fusion(bf16[3,256,256]{2,1,0:T(8,128)(2,1)S(1)} %collective-permute-done.10, bf16[3,256,256]{2,1,0:T(8,128)(2,1)S(1)} %collective-permute-done.9, bf16[3,256,256]{2,1,0:T(8,128)(2,1)} %get-tuple-element.24), kind=kLoop, calls=%fused_computation.15 | loop fusion | flops 1114112 | bytes 1703936 | tf_op jit(solution)/shard_map/convert_element_type | solution.py:277
  68.2 4.5 %collective-permute-start.11 = (bf16[256,256]{1,0:T(8,128)(2,1)S(1)}, bf16[256,256]{1,0:T(8,128)(2,1)S(1)}, u32[]{:S(2)}, u32[]{:S(2)}) collective-permute-start(bf16[256,256]{1,0:T(8,128)(2,1)S(1)} %get-tuple-element.37), channel_id=1, source_target_pairs={{0,1},{1,0},{2,3},{3,2},{4,5},{5,4},{6,7},{7,6},{8,9},{9,8},{10,11... | collective-permute-start | bytes 393224 | tf_op jit(solution)/shard_map/ppermute | solution.py:238
  73.4 2.3 %collective-permute-done.11.even = bf16[256,256]{1,0:T(8,128)(2,1)S(1)} collective-permute-done((bf16[256,256]{1,0:T(8,128)(2,1)S(1)}, bf16[256,256]{1,0:T(8,128)(2,1)S(1)}, u32[]{:S(2)}, u32[]{:S(2)}) %collective-permute-start.11) | collective-permute-done | bytes 131104 | tf_op jit(solution)/shard_map/ppermute | solution.py:238
  76.4 3.8 %shard_map.79 = (bf16[256,384]{1,0:T(8,128)(2,1)}, bf16[16,192,128]{2,1,0:T(8,128)(2,1)}, bf16[16,192,128]{2,1,0:T(8,128)(2,1)}) custom-call(s32[2]{0:T(128)} %pad_add_fusion.index, bf16[256,1536]{1,0:T(8,128)(2,1)} %tokens.3, bf16[256,1536]{1,0:T(8,128)(2,1)} %grad_out.3, bf16[256,128]{1,0:T(8,128)(2,1)} %get-tuple-element.23.dq, ...), custom_call_target="tpu_custom_call" | custom-call | tf_op jit(solution)/shard_map/pallas_call | solution.py:221
  80.1 3.8 %collective-permute-start.13 = (bf16[16,192,128]{2,1,0:T(8,128)(2,1)}, bf16[16,192,128]{2,1,0:T(8,128)(2,1)S(1)}, u32[]{:S(2)}, u32[]{:S(2)}) collective-permute-start(bf16[16,192,128]{2,1,0:T(8,128)(2,1)} %get-tuple-element.29), channel_id=1, source_target_pairs={{0,8},{1,9},{2,10},{3,11},{4,12},{5,13},{6,14},{7,15},{8,0},{9,1},... | collective-permute-start | bytes 2359304 | tf_op jit(solution)/shard_map/ppermute | solution.py:238
  84.0 2.1 %collective-permute-done.13 = bf16[16,192,128]{2,1,0:T(8,128)(2,1)S(1)} collective-permute-done((bf16[16,192,128]{2,1,0:T(8,128)(2,1)}, bf16[16,192,128]{2,1,0:T(8,128)(2,1)S(1)}, u32[]{:S(2)}, u32[]{:S(2)}) %collective-permute-start.13) | collective-permute-done | bytes 786464 | tf_op jit(solution)/shard_map/ppermute | solution.py:238
  87.4 4.3 %collective-permute-start.14 = (bf16[8,192,128]{2,1,0:T(8,128)(2,1)S(1)}, bf16[8,192,128]{2,1,0:T(8,128)(2,1)S(1)}, u32[]{:S(2)}, u32[]{:S(2)}) collective-permute-start(bf16[8,192,128]{2,1,0:T(8,128)(2,1)S(1)} %get-tuple-element.32), channel_id=1, source_target_pairs={{0,1},{1,0},{2,3},{3,2},{4,5},{5,4},{6,7},{7,6},{8,24},{9,25},{10,... | collective-permute-start | bytes 1179656 | tf_op jit(solution)/shard_map/ppermute | solution.py:238
  91.7 5.8 %collective-permute-done.14 = bf16[8,192,128]{2,1,0:T(8,128)(2,1)S(1)} collective-permute-done((bf16[8,192,128]{2,1,0:T(8,128)(2,1)S(1)}, bf16[8,192,128]{2,1,0:T(8,128)(2,1)S(1)}, u32[]{:S(2)}, u32[]{:S(2)}) %collective-permute-start.14) | collective-permute-done | bytes 393248 | tf_op jit(solution)/shard_map/ppermute | solution.py:238
  97.5 2.8 %collective-permute-start.15 = (bf16[4,192,128]{2,1,0:T(8,128)(2,1)S(1)}, bf16[4,192,128]{2,1,0:T(8,128)(2,1)S(1)}, u32[]{:S(2)}, u32[]{:S(2)}) collective-permute-start(bf16[4,192,128]{2,1,0:T(8,128)(2,1)S(1)} %get-tuple-element.34), channel_id=1, source_target_pairs={{0,16},{1,17},{2,18},{3,19},{4,20},{5,21},{6,22},{7,23},{8,9},{9,8... | collective-permute-start | bytes 589832 | tf_op jit(solution)/shard_map/ppermute | solution.py:238
  100.3 3.6 %collective-permute-done.15 = bf16[4,192,128]{2,1,0:T(8,128)(2,1)S(1)} collective-permute-done((bf16[4,192,128]{2,1,0:T(8,128)(2,1)S(1)}, bf16[4,192,128]{2,1,0:T(8,128)(2,1)S(1)}, u32[]{:S(2)}, u32[]{:S(2)}) %collective-permute-start.15) | collective-permute-done | bytes 196640 | tf_op jit(solution)/shard_map/ppermute | solution.py:238
  104.0 2.8 %collective-permute-start.16 = (bf16[2,192,128]{2,1,0:T(8,128)(2,1)S(1)}, bf16[2,192,128]{2,1,0:T(8,128)(2,1)S(1)}, u32[]{:S(2)}, u32[]{:S(2)}) collective-permute-start(bf16[2,192,128]{2,1,0:T(8,128)(2,1)S(1)} %get-tuple-element.39), channel_id=1, source_target_pairs={{0,2},{1,3},{2,0},{3,1},{4,6},{5,7},{6,4},{7,5},{8,10},{9,11},{10,... | collective-permute-start | bytes 294920 | tf_op jit(solution)/shard_map/ppermute | solution.py:238
  106.8 2.6 %collective-permute-done.16 = bf16[2,192,128]{2,1,0:T(8,128)(2,1)S(1)} collective-permute-done((bf16[2,192,128]{2,1,0:T(8,128)(2,1)S(1)}, bf16[2,192,128]{2,1,0:T(8,128)(2,1)S(1)}, u32[]{:S(2)}, u32[]{:S(2)}) %collective-permute-start.16) | collective-permute-done | bytes 98336 | tf_op jit(solution)/shard_map/ppermute | solution.py:238
  110.1 3.4 %collective-permute-start.17 = (bf16[1,192,128]{2,1,0:T(8,128)(2,1)S(1)}, bf16[1,192,128]{2,1,0:T(8,128)(2,1)S(1)}, u32[]{:S(2)}, u32[]{:S(2)}) collective-permute-start(bf16[1,192,128]{2,1,0:T(8,128)(2,1)S(1)} %get-tuple-element.41), channel_id=1, source_target_pairs={{0,4},{1,5},{2,6},{3,7},{4,0},{5,1},{6,2},{7,3},{8,12},{9,13},{10,... | collective-permute-start | bytes 147464 | tf_op jit(solution)/shard_map/ppermute | solution.py:238
  113.5 3.3 %shard_map.78 = bf16[256,1536]{1,0:T(8,128)(2,1)} custom-call(bf16[256,128]{1,0:T(8,128)(2,1)} %get-tuple-element.21.att_ref, bf16[4,1536,128]{2,1,0:T(8,128)(2,1)} %get-tuple-element.22.full), custom_call_target="tpu_custom_call" | custom-call | tf_op jit(solution)/shard_map/pallas_call | solution.py:221
  116.8 3.4 %shard_map.80 = bf16[256,1536]{1,0:T(8,128)(2,1)} custom-call(bf16[256,384]{1,0:T(8,128)(2,1)} %get-tuple-element.27.rows_ref, bf16[4,1536,128]{2,1,0:T(8,128)(2,1)} %get-tuple-element.22.full), custom_call_target="tpu_custom_call" | custom-call | tf_op jit(solution)/shard_map/pallas_call | solution.py:221
  120.8 1.7 %shard_map.81 = (f32[192,96]{1,0:T(8,128)}, f32[32,192]{1,0:T(8,128)}) custom-call(f32[1,192,128]{2,1,0:T(8,128)} %get-tuple-element.42.keep, bf16[1,192,128]{2,1,0:T(8,128)(2,1)} %copy-done.8), custom_call_target="tpu_custom_call" | custom-call | tf_op jit(solution)/shard_map/pallas_call | solution.py:221
  (44 shorter events, 14.1 us)
Async XLA Ops:
  2.2 6.9 %collective-permute-start = (bf16[1,192,128]{2,1,0:T(8,128)(2,1)}, bf16[1,192,128]{2,1,0:T(8,128)(2,1)S(1)}, u32[]{:S(2)}, u32[]{:S(2)}) collective-permute-start(bf16[1,192,128]{2,1,0:T(8,128)(2,1)} %shard_map.75), channel_id=1, source_target_pairs={{0,4},{1,5},{2,6},{3,7},{4,0},{5,1},{6,2},{7,3},{8,12},{9,13},{10,... | collective-permute-start | bytes 147464 | tf_op jit(solution)/shard_map/ppermute | solution.py:238
  9.9 4.7 %collective-permute-start.1 = (bf16[2,192,128]{2,1,0:T(8,128)(2,1)S(1)}, bf16[2,192,128]{2,1,0:T(8,128)(2,1)S(1)}, u32[]{:S(2)}, u32[]{:S(2)}) collective-permute-start(bf16[2,192,128]{2,1,0:T(8,128)(2,1)S(1)} %pad_maximum_fusion.3), channel_id=1, source_target_pairs={{0,2},{1,3},{2,0},{3,1},{4,6},{5,7},{6,4},{7,5},{8,10},{9,11},{10,... | collective-permute-start | bytes 294920 | tf_op jit(solution)/shard_map/ppermute | solution.py:238
  15.4 6.1 %collective-permute-start.2 = (bf16[4,192,128]{2,1,0:T(8,128)(2,1)S(1)}, bf16[4,192,128]{2,1,0:T(8,128)(2,1)S(1)}, u32[]{:S(2)}, u32[]{:S(2)}) collective-permute-start(bf16[4,192,128]{2,1,0:T(8,128)(2,1)S(1)} %pad_maximum_fusion.2), channel_id=1, source_target_pairs={{0,16},{1,17},{2,18},{3,19},{4,20},{5,21},{6,22},{7,23},{8,9},{9,8... | collective-permute-start | bytes 589832 | tf_op jit(solution)/shard_map/ppermute | solution.py:238
  22.3 7.8 %collective-permute-start.3 = (bf16[8,192,128]{2,1,0:T(8,128)(2,1)S(1)}, bf16[8,192,128]{2,1,0:T(8,128)(2,1)S(1)}, u32[]{:S(2)}, u32[]{:S(2)}) collective-permute-start(bf16[8,192,128]{2,1,0:T(8,128)(2,1)S(1)} %pad_maximum_fusion), channel_id=1, source_target_pairs={{0,1},{1,0},{2,3},{3,2},{4,5},{5,4},{6,7},{7,6},{8,24},{9,25},{10,... | collective-permute-start | bytes 1179656 | tf_op jit(solution)/shard_map/ppermute | solution.py:238
  30.2 2.4 %copy-start = (bf16[16,192,128]{2,1,0:T(8,128)(2,1)}, bf16[16,192,128]{2,1,0:T(8,128)(2,1)S(1)}, u32[]{:S(2)}) copy-start(bf16[16,192,128]{2,1,0:T(8,128)(2,1)S(1)} %constant_dynamic-update-slice_fusion.own) | copy-start | bytes 2359300
  30.2 2.4 %collective-permute-start.4 = (bf16[16,192,128]{2,1,0:T(8,128)(2,1)S(1)}, bf16[16,192,128]{2,1,0:T(8,128)(2,1)S(1)}, u32[]{:S(2)}, u32[]{:S(2)}) collective-permute-start(bf16[16,192,128]{2,1,0:T(8,128)(2,1)S(1)} %constant_dynamic-update-slice_fusion.own), channel_id=1, source_target_pairs={{0,8},{1,9},{2,10},{3,11},{4,12},{5,13},{6,14},{7,15},{8,0},{9,1},... | collective-permute-start | bytes 2359304 | tf_op jit(solution)/shard_map/ppermute | solution.py:238
  32.6 0.9 copy-start.1
  37.8 5.9 %collective-permute-start.5 = (bf16[256,256]{1,0:T(8,128)(2,1)}, bf16[256,256]{1,0:T(8,128)(2,1)S(1)}, u32[]{:S(2)}, u32[]{:S(2)}) collective-permute-start(bf16[256,256]{1,0:T(8,128)(2,1)} %get-tuple-element.20.own), channel_id=1, source_target_pairs={{0,1},{1,0},{2,3},{3,2},{4,5},{5,4},{6,7},{7,6},{8,9},{9,8},{10,11... | collective-permute-start | bytes 393224 | tf_op jit(solution)/shard_map/ppermute | solution.py:238
  39.7 4.0 %collective-permute-start.6 = (bf16[256,256]{1,0:T(8,128)(2,1)}, bf16[256,256]{1,0:T(8,128)(2,1)S(1)}, u32[]{:S(2)}, u32[]{:S(2)}) collective-permute-start(bf16[256,256]{1,0:T(8,128)(2,1)} %get-tuple-element.20.own), channel_id=1, source_target_pairs={{1,2},{2,1},{3,4},{4,3},{5,6},{6,5},{9,10},{10,9},{11,12},{12,11},... | collective-permute-start | bytes 393224 | tf_op jit(solution)/shard_map/ppermute | solution.py:238
  43.7 2.9 %copy-start.2 = (bf16[256,256]{1,0:T(8,128)(2,1)}, bf16[256,256]{1,0:T(8,128)(2,1)S(1)}, u32[]{:S(2)}) copy-start(bf16[256,256]{1,0:T(8,128)(2,1)S(1)} %collective-permute-done.5.even) | copy-start | bytes 393220
  43.7 2.9 %copy-start.3 = (bf16[256,256]{1,0:T(8,128)(2,1)}, bf16[256,256]{1,0:T(8,128)(2,1)S(1)}, u32[]{:S(2)}) copy-start(bf16[256,256]{1,0:T(8,128)(2,1)S(1)} %collective-permute-done.6.odd) | copy-start | bytes 393220
  44.8 1.8 %collective-permute-start.7 = (bf16[3,256,256]{2,1,0:T(8,128)(2,1)S(1)}, bf16[3,256,256]{2,1,0:T(8,128)(2,1)S(1)}, u32[]{:S(2)}, u32[]{:S(2)}) collective-permute-start(bf16[3,256,256]{2,1,0:T(8,128)(2,1)S(1)} %pad_maximum_fusion.1), channel_id=1, source_target_pairs={{0,8},{1,9},{2,10},{3,11},{4,12},{5,13},{6,14},{7,15},{8,0},{9,1},... | collective-permute-start | bytes 1179656 | tf_op jit(solution)/shard_map/ppermute | solution.py:238
  44.9 1.7 %collective-permute-start.8 = (bf16[3,256,256]{2,1,0:T(8,128)(2,1)S(1)}, bf16[3,256,256]{2,1,0:T(8,128)(2,1)S(1)}, u32[]{:S(2)}, u32[]{:S(2)}) collective-permute-start(bf16[3,256,256]{2,1,0:T(8,128)(2,1)S(1)} %pad_maximum_fusion.1), channel_id=1, source_target_pairs={{8,16},{9,17},{10,18},{11,19},{12,20},{13,21},{14,22},{15,23},{16,... | collective-permute-start | bytes 1179656 | tf_op jit(solution)/shard_map/ppermute | solution.py:238
  46.6 0.7 copy-start.4
  46.6 0.9 copy-start.5
  53.8 11.1 %collective-permute-start.10 = (bf16[3,256,256]{2,1,0:T(8,128)(2,1)}, bf16[3,256,256]{2,1,0:T(8,128)(2,1)S(1)}, u32[]{:S(2)}, u32[]{:S(2)}) collective-permute-start(bf16[3,256,256]{2,1,0:T(8,128)(2,1)} %get-tuple-element.26), channel_id=1, source_target_pairs={{8,16},{9,17},{10,18},{11,19},{12,20},{13,21},{14,22},{15,23},{16,... | collective-permute-start | bytes 1179656 | tf_op jit(solution)/shard_map/ppermute | solution.py:238
  54.4 11.9 %collective-permute-start.9 = (bf16[3,256,256]{2,1,0:T(8,128)(2,1)}, bf16[3,256,256]{2,1,0:T(8,128)(2,1)S(1)}, u32[]{:S(2)}, u32[]{:S(2)}) collective-permute-start(bf16[3,256,256]{2,1,0:T(8,128)(2,1)} %get-tuple-element.25), channel_id=1, source_target_pairs={{0,8},{1,9},{2,10},{3,11},{4,12},{5,13},{6,14},{7,15},{8,0},{9,1},... | collective-permute-start | bytes 1179656 | tf_op jit(solution)/shard_map/ppermute | solution.py:238
  68.2 7.4 %collective-permute-start.11 = (bf16[256,256]{1,0:T(8,128)(2,1)S(1)}, bf16[256,256]{1,0:T(8,128)(2,1)S(1)}, u32[]{:S(2)}, u32[]{:S(2)}) collective-permute-start(bf16[256,256]{1,0:T(8,128)(2,1)S(1)} %get-tuple-element.37), channel_id=1, source_target_pairs={{0,1},{1,0},{2,3},{3,2},{4,5},{5,4},{6,7},{7,6},{8,9},{9,8},{10,11... | collective-permute-start | bytes 393224 | tf_op jit(solution)/shard_map/ppermute | solution.py:238
  72.7 2.9 %collective-permute-start.12 = (bf16[256,256]{1,0:T(8,128)(2,1)S(1)}, bf16[256,256]{1,0:T(8,128)(2,1)S(1)}, u32[]{:S(2)}, u32[]{:S(2)}) collective-permute-start(bf16[256,256]{1,0:T(8,128)(2,1)S(1)} %get-tuple-element.36), channel_id=1, source_target_pairs={{1,2},{2,1},{3,4},{4,3},{5,6},{6,5},{9,10},{10,9},{11,12},{12,11},... | collective-permute-start | bytes 393224 | tf_op jit(solution)/shard_map/ppermute | solution.py:238
  75.6 0.6 copy-start.6
  75.7 0.7 copy-start.7
  80.1 6.0 %collective-permute-start.13 = (bf16[16,192,128]{2,1,0:T(8,128)(2,1)}, bf16[16,192,128]{2,1,0:T(8,128)(2,1)S(1)}, u32[]{:S(2)}, u32[]{:S(2)}) collective-permute-start(bf16[16,192,128]{2,1,0:T(8,128)(2,1)} %get-tuple-element.29), channel_id=1, source_target_pairs={{0,8},{1,9},{2,10},{3,11},{4,12},{5,13},{6,14},{7,15},{8,0},{9,1},... | collective-permute-start | bytes 2359304 | tf_op jit(solution)/shard_map/ppermute | solution.py:238
  87.4 10.0 %collective-permute-start.14 = (bf16[8,192,128]{2,1,0:T(8,128)(2,1)S(1)}, bf16[8,192,128]{2,1,0:T(8,128)(2,1)S(1)}, u32[]{:S(2)}, u32[]{:S(2)}) collective-permute-start(bf16[8,192,128]{2,1,0:T(8,128)(2,1)S(1)} %get-tuple-element.32), channel_id=1, source_target_pairs={{0,1},{1,0},{2,3},{3,2},{4,5},{5,4},{6,7},{7,6},{8,24},{9,25},{10,... | collective-permute-start | bytes 1179656 | tf_op jit(solution)/shard_map/ppermute | solution.py:238
  97.5 6.4 %collective-permute-start.15 = (bf16[4,192,128]{2,1,0:T(8,128)(2,1)S(1)}, bf16[4,192,128]{2,1,0:T(8,128)(2,1)S(1)}, u32[]{:S(2)}, u32[]{:S(2)}) collective-permute-start(bf16[4,192,128]{2,1,0:T(8,128)(2,1)S(1)} %get-tuple-element.34), channel_id=1, source_target_pairs={{0,16},{1,17},{2,18},{3,19},{4,20},{5,21},{6,22},{7,23},{8,9},{9,8... | collective-permute-start | bytes 589832 | tf_op jit(solution)/shard_map/ppermute | solution.py:238
  104.0 5.4 %collective-permute-start.16 = (bf16[2,192,128]{2,1,0:T(8,128)(2,1)S(1)}, bf16[2,192,128]{2,1,0:T(8,128)(2,1)S(1)}, u32[]{:S(2)}, u32[]{:S(2)}) collective-permute-start(bf16[2,192,128]{2,1,0:T(8,128)(2,1)S(1)} %get-tuple-element.39), channel_id=1, source_target_pairs={{0,2},{1,3},{2,0},{3,1},{4,6},{5,7},{6,4},{7,5},{8,10},{9,11},{10,... | collective-permute-start | bytes 294920 | tf_op jit(solution)/shard_map/ppermute | solution.py:238
  110.1 10.2 %collective-permute-start.17 = (bf16[1,192,128]{2,1,0:T(8,128)(2,1)S(1)}, bf16[1,192,128]{2,1,0:T(8,128)(2,1)S(1)}, u32[]{:S(2)}, u32[]{:S(2)}) collective-permute-start(bf16[1,192,128]{2,1,0:T(8,128)(2,1)S(1)} %get-tuple-element.41), channel_id=1, source_target_pairs={{0,4},{1,5},{2,6},{3,7},{4,0},{5,1},{6,2},{7,3},{8,12},{9,13},{10,... | collective-permute-start | bytes 147464 | tf_op jit(solution)/shard_map/ppermute | solution.py:238
  120.2 0.6 copy-start.8

commit v2 on v1

--- a/solution.py
+++ b/solution.py
@@ -216,14 +216,19 @@
     proj_ref[...] = total[:, split:].T
 
 
-def call(kernel, outs, args, scratch=(), scalars=0):
-    shapes = [jax.ShapeDtypeStruct(shape, kind) for shape, kind in outs]
+def call(kernel, outs, args, scratch=(), scalars=0, final=False):
+    make = jax.ShapeDtypeStruct if final else pltpu.VMEM
+    args = [
+        value if i < scalars else pltpu.with_memory_space_constraint(value, pltpu.VMEM)
+        for i, value in enumerate(args)
+    ]
     return pl.pallas_call(
         kernel,
-        out_shape=shapes,
+        out_shape=[make(shape, kind) for shape, kind in outs],
         in_specs=[SMEM] * scalars + [VMEM] * (len(args) - scalars),
         out_specs=[VMEM] * len(outs),
         scratch_shapes=list(scratch),
+        compiler_params=pltpu.CompilerParams(vmem_limit_bytes=32 << 20),
     )(*args)
 
 
@@ -263,8 +268,12 @@
     )
     parts_even, parts_odd = swap(parts_even, slab_even), swap(parts_odd, slab_odd)
     (mixed,) = call(
-        functools.partial(mixed_kernel, split), [((count, features), BF)], [attended, full]
-    )
+        functools.partial(mixed_kernel, split),
+        [((count, features), BF)],
+        [attended, full],
+        final=True,
+    )
+    parts_even, parts_odd, mixed = lax.optimization_barrier((parts_even, parts_odd, mixed))
 
     def summed(column):
         return (
@@ -284,18 +293,24 @@
         scalars=1,
     )
     got = swap(send, core_pairs(slabs, weights))
-    (grad_tokens,) = call(
-        functools.partial(grad_tokens_kernel, split), [((count, features), BF)], [grad_rows, full]
-    )
     for step in reversed(steps):
         near = keep.shape[0] // 2
         send = (keep[near:].astype(F32) + got[near:].astype(F32)).astype(BF)
         keep = keep[:near].astype(F32) + got[:near].astype(F32)
         got = swap(send, step_pairs(step, slabs, weights))
+        if step == steps[-1]:
+            (grad_tokens,) = call(
+                functools.partial(grad_tokens_kernel, split),
+                [((count, features), BF)],
+                [grad_rows, full],
+                final=True,
+            )
+            got, grad_tokens = lax.optimization_barrier((got, grad_tokens))
     grad_qkv, grad_proj = call(
         functools.partial(unpack_kernel, split),
         [((rows, split), F32), ((HD // slabs, rows), F32)],
         [keep, got],
+        final=True,
     )
     return mixed, grad_tokens, grad_qkv, grad_proj
 

time: 123 us -> 105 us (0.85)
  Pallas kernels: 24.4 us -> 13.6 us
  other arithmetic: 8.14 us -> 0.66 us
  waiting for transfers between devices: 39.3 us -> 44.3 us
  starting transfers between devices: 45.9 us -> 43.4 us
  local copies, waits for them, and re-layouts: 3.98 us -> 1.7 us
    pallas_call x7, Pallas kernels: 24.4 us -> 13.6 us  [call(): pl.pallas_call(kernel, out_shape=[make(shape, kind) for shape, kind in ou...]
    ppermute x18, waiting for transfers between devices: 39.3 us -> 44.3 us  [swap(): return lax.ppermute(values, AXES, pairs)]
    ppermute x18, starting transfers between devices: 45.9 us -> 43.4 us  [swap(): return lax.ppermute(values, AXES, pairs)]
    concatenate x3, other arithmetic: 2.47 us -> 0.07 us  [local(): jnp.concatenate([held, swap(held, step_pairs(step, slabs, weights))], axi...]
    unnamed x22 -> x12, local copies, waits for them, and re-layouts: 3.93 us -> 1.65 us
    convert_element_type x4 -> x3, other arithmetic: 2.07 us -> 0.14 us  [local(): send = (keep[near:].astype(F32) + got[near:].astype(F32)).astype(BF)]
    convert_element_type x1, other arithmetic: 1.86 us -> 0.14 us  [local(): odd = swap(summed(2).astype(BF), weight_odd)]
  transfers between devices with their start and end apart: 18 -> 18, of which waited for: 13 -> 13; matrix products, arithmetic and copies ran while one was open for 1% -> 0% of each run, Pallas kernels for 6% -> 4%
where the time goes in v2:
time: 105 us; the launch traced here: 104 us
  waiting for transfers between devices  44.3 us (42%)
  starting transfers between devices  43.4 us (41%)
  Pallas kernels  13.6 us (13%)
  local copies, waits for them, and re-layouts  1.7 us (2%)
    ppermute x18, waiting for transfers between devices, swap(): return lax.ppermute(values, AXES, pairs)  44.3 us
    ppermute x18, starting transfers between devices, swap(): return lax.ppermute(values, AXES, pairs)  43.4 us
    pallas_call x7, Pallas kernels, call(): pl.pallas_call(kernel, out_shape=[make(shape, kind) for shape, kind in ou...  13.6 us
  transfers between devices with their start and end apart: 18, of which 13 were waited for; matrix products, arithmetic and copies ran while one was open for 0% of the time, Pallas kernels for 4%

profile of v2, /device:TPU:0, one launch (start us, length us, event | category | flops | bytes accessed | tf_op | source)
XLA Modules:
  0.0 104.5 jit_solution(6151451752661580235)
XLA Ops:
  0.7 0.9 copy-done.2
  2.4 4.1 %collective-permute-start = (bf16[1,192,128]{2,1,0:T(8,128)(2,1)S(1)}, bf16[1,192,128]{2,1,0:T(8,128)(2,1)S(1)}, u32[]{:S(2)}, u32[]{:S(2)}) collective-permute-start(bf16[1,192,128]{2,1,0:T(8,128)(2,1)S(1)} %shard_map.75), channel_id=1, source_target_pairs={{0,4},{1,5},{2,6},{3,7},{4,0},{5,1},{6,2},{7,3},{8,12},{9,13},{10,... | collective-permute-start | bytes 147464 | tf_op jit(solution)/shard_map/ppermute | solution.py:243
  6.5 2.6 %collective-permute-done = bf16[1,192,128]{2,1,0:T(8,128)(2,1)S(1)} collective-permute-done((bf16[1,192,128]{2,1,0:T(8,128)(2,1)S(1)}, bf16[1,192,128]{2,1,0:T(8,128)(2,1)S(1)}, u32[]{:S(2)}, u32[]{:S(2)}) %collective-permute-start) | collective-permute-done | bytes 49184 | tf_op jit(solution)/shard_map/ppermute | solution.py:243
  9.1 1.4 %collective-permute-start.1 = (bf16[2,192,128]{2,1,0:T(8,128)(2,1)S(1)}, bf16[2,192,128]{2,1,0:T(8,128)(2,1)S(1)}, u32[]{:S(2)}, u32[]{:S(2)}) collective-permute-start(bf16[2,192,128]{2,1,0:T(8,128)(2,1)S(1)} %pad_maximum_fusion.3), channel_id=1, source_target_pairs={{0,2},{1,3},{2,0},{3,1},{4,6},{5,7},{6,4},{7,5},{8,10},{9,11},{10,... | collective-permute-start | bytes 294920 | tf_op jit(solution)/shard_map/ppermute | solution.py:243
  10.6 3.2 %collective-permute-done.1 = bf16[2,192,128]{2,1,0:T(8,128)(2,1)S(1)} collective-permute-done((bf16[2,192,128]{2,1,0:T(8,128)(2,1)S(1)}, bf16[2,192,128]{2,1,0:T(8,128)(2,1)S(1)}, u32[]{:S(2)}, u32[]{:S(2)}) %collective-permute-start.1) | collective-permute-done | bytes 98336 | tf_op jit(solution)/shard_map/ppermute | solution.py:243
  13.8 1.8 %collective-permute-start.2 = (bf16[4,192,128]{2,1,0:T(8,128)(2,1)S(1)}, bf16[4,192,128]{2,1,0:T(8,128)(2,1)S(1)}, u32[]{:S(2)}, u32[]{:S(2)}) collective-permute-start(bf16[4,192,128]{2,1,0:T(8,128)(2,1)S(1)} %pad_maximum_fusion.2), channel_id=1, source_target_pairs={{0,16},{1,17},{2,18},{3,19},{4,20},{5,21},{6,22},{7,23},{8,9},{9,8... | collective-permute-start | bytes 589832 | tf_op jit(solution)/shard_map/ppermute | solution.py:243
  15.6 5.1 %collective-permute-done.2 = bf16[4,192,128]{2,1,0:T(8,128)(2,1)S(1)} collective-permute-done((bf16[4,192,128]{2,1,0:T(8,128)(2,1)S(1)}, bf16[4,192,128]{2,1,0:T(8,128)(2,1)S(1)}, u32[]{:S(2)}, u32[]{:S(2)}) %collective-permute-start.2) | collective-permute-done | bytes 196640 | tf_op jit(solution)/shard_map/ppermute | solution.py:243
  20.8 2.0 %collective-permute-start.3 = (bf16[8,192,128]{2,1,0:T(8,128)(2,1)S(1)}, bf16[8,192,128]{2,1,0:T(8,128)(2,1)S(1)}, u32[]{:S(2)}, u32[]{:S(2)}) collective-permute-start(bf16[8,192,128]{2,1,0:T(8,128)(2,1)S(1)} %pad_maximum_fusion), channel_id=1, source_target_pairs={{0,1},{1,0},{2,3},{3,2},{4,5},{5,4},{6,7},{7,6},{8,24},{9,25},{10,... | collective-permute-start | bytes 1179656 | tf_op jit(solution)/shard_map/ppermute | solution.py:243
  22.8 5.8 %collective-permute-done.3 = bf16[8,192,128]{2,1,0:T(8,128)(2,1)S(1)} collective-permute-done((bf16[8,192,128]{2,1,0:T(8,128)(2,1)S(1)}, bf16[8,192,128]{2,1,0:T(8,128)(2,1)S(1)}, u32[]{:S(2)}, u32[]{:S(2)}) %collective-permute-start.3) | collective-permute-done | bytes 393248 | tf_op jit(solution)/shard_map/ppermute | solution.py:243
  28.8 2.2 %collective-permute-done.4.got = bf16[16,192,128]{2,1,0:T(8,128)(2,1)S(1)} collective-permute-done((bf16[16,192,128]{2,1,0:T(8,128)(2,1)S(1)}, bf16[16,192,128]{2,1,0:T(8,128)(2,1)S(1)}, u32[]{:S(2)}, u32[]{:S(2)}) %collective-permute-start.4) | collective-permute-done | bytes 786464 | tf_op jit(solution)/shard_map/ppermute | solution.py:243
  31.0 2.5 %shard_map.76 = (bf16[256,128]{1,0:T(8,128)(2,1)S(1)}, bf16[256,256]{1,0:T(8,128)(2,1)S(1)}, bf16[256,128]{1,0:T(8,128)(2,1)S(1)}, bf16[4,1536,128]{2,1,0:T(8,128)(2,1)S(1)}) custom-call(s32[2]{0:T(128)S(1)} %pad_add_fusion.index, bf16[16,192,128]{2,1,0:T(8,128)(2,1)S(1)} %constant_dynamic-update-slice_fusion.own, ...), custom_call_target="tpu_custom_call" | custom-call | tf_op jit(solution)/shard_map/pallas_call | solution.py:225
  34.2 3.8 %collective-permute-start.5 = (bf16[256,256]{1,0:T(8,128)(2,1)S(1)}, bf16[256,256]{1,0:T(8,128)(2,1)S(1)}, u32[]{:S(2)}, u32[]{:S(2)}) collective-permute-start(bf16[256,256]{1,0:T(8,128)(2,1)S(1)} %get-tuple-element.25.own), channel_id=1, source_target_pairs={{0,1},{1,0},{2,3},{3,2},{4,5},{5,4},{6,7},{7,6},{8,9},{9,8},{10,11... | collective-permute-start | bytes 393224 | tf_op jit(solution)/shard_map/ppermute | solution.py:243
  38.0 5.6 %collective-permute-done.5.even = bf16[256,256]{1,0:T(8,128)(2,1)S(1)} collective-permute-done((bf16[256,256]{1,0:T(8,128)(2,1)S(1)}, bf16[256,256]{1,0:T(8,128)(2,1)S(1)}, u32[]{:S(2)}, u32[]{:S(2)}) %collective-permute-start.5) | collective-permute-done | bytes 131104 | tf_op jit(solution)/shard_map/ppermute | solution.py:243
  44.3 3.0 %collective-permute-start.7 = (bf16[3,256,256]{2,1,0:T(8,128)(2,1)S(1)}, bf16[3,256,256]{2,1,0:T(8,128)(2,1)S(1)}, u32[]{:S(2)}, u32[]{:S(2)}) collective-permute-start(bf16[3,256,256]{2,1,0:T(8,128)(2,1)S(1)} %pad_maximum_fusion.1), channel_id=1, source_target_pairs={{0,8},{1,9},{2,10},{3,11},{4,12},{5,13},{6,14},{7,15},{8,0},{9,1},... | collective-permute-start | bytes 1179656 | tf_op jit(solution)/shard_map/ppermute | solution.py:243
  47.3 1.3 %collective-permute-done.7.slab_even = bf16[3,256,256]{2,1,0:T(8,128)(2,1)S(1)} collective-permute-done((bf16[3,256,256]{2,1,0:T(8,128)(2,1)S(1)}, bf16[3,256,256]{2,1,0:T(8,128)(2,1)S(1)}, u32[]{:S(2)}, u32[]{:S(2)}) %collective-permute-start.7) | collective-permute-done | bytes 393248 | tf_op jit(solution)/shard_map/ppermute | solution.py:243
  48.6 4.7 %shard_map.77 = (bf16[256,128]{1,0:T(8,128)(2,1)S(1)}, bf16[256,128]{1,0:T(8,128)(2,1)S(1)}, bf16[3,256,256]{2,1,0:T(8,128)(2,1)S(1)}, bf16[3,256,256]{2,1,0:T(8,128)(2,1)S(1)}, bf16[3,256,256]{2,1,0:T(8,128)(2,1)S(1)}) custom-call(s32[2]{0:T(128)S(1)} %pad_add_fusion.index, bf16[256,128]{1,0:T(8,128)(2,1)S(1)} %get-tuple-element.23.q_ref, ...), custom_call_target="tpu_custom_call" | custom-call | tf_op jit(solution)/shard_map/pallas_call | solution.py:225
  53.4 4.1 %collective-permute-start.9 = (bf16[3,256,256]{2,1,0:T(8,128)(2,1)S(1)}, bf16[3,256,256]{2,1,0:T(8,128)(2,1)S(1)}, u32[]{:S(2)}, u32[]{:S(2)}) collective-permute-start(bf16[3,256,256]{2,1,0:T(8,128)(2,1)S(1)} %get-tuple-element.26), channel_id=1, source_target_pairs={{0,8},{1,9},{2,10},{3,11},{4,12},{5,13},{6,14},{7,15},{8,0},{9,1},... | collective-permute-start | bytes 1179656 | tf_op jit(solution)/shard_map/ppermute | solution.py:243
  58.2 1.9 %shard_map.78 = bf16[256,1536]{1,0:T(8,128)(2,1)} custom-call(bf16[256,128]{1,0:T(8,128)(2,1)S(1)} %get-tuple-element.28.att_ref, bf16[4,1536,128]{2,1,0:T(8,128)(2,1)S(1)} %get-tuple-element.29.full), custom_call_target="tpu_custom_call" | custom-call | tf_op jit(solution)/shard_map/pallas_call | solution.py:225
  60.9 5.0 %collective-permute-start.11 = (bf16[256,256]{1,0:T(8,128)(2,1)S(1)}, bf16[256,256]{1,0:T(8,128)(2,1)S(1)}, u32[]{:S(2)}, u32[]{:S(2)}) collective-permute-start(bf16[256,256]{1,0:T(8,128)(2,1)S(1)} %get-tuple-element.47), channel_id=1, source_target_pairs={{0,1},{1,0},{2,3},{3,2},{4,5},{5,4},{6,7},{7,6},{8,9},{9,8},{10,11... | collective-permute-start | bytes 393224 | tf_op jit(solution)/shard_map/ppermute | solution.py:243
  65.8 3.5 %collective-permute-done.11.even = bf16[256,256]{1,0:T(8,128)(2,1)S(1)} collective-permute-done((bf16[256,256]{1,0:T(8,128)(2,1)S(1)}, bf16[256,256]{1,0:T(8,128)(2,1)S(1)}, u32[]{:S(2)}, u32[]{:S(2)}) %collective-permute-start.11) | collective-permute-done | bytes 131104 | tf_op jit(solution)/shard_map/ppermute | solution.py:243
  69.4 1.7 %shard_map.79 = (bf16[256,384]{1,0:T(8,128)(2,1)S(1)}, bf16[16,192,128]{2,1,0:T(8,128)(2,1)S(1)}, bf16[16,192,128]{2,1,0:T(8,128)(2,1)S(1)}) custom-call(s32[2]{0:T(128)S(1)} %pad_add_fusion.index, bf16[256,1536]{1,0:T(8,128)(2,1)S(1)} %copy-done, bf16[256,1536]{1,0:T(8,128)(2,1)S(1)} %copy-done.1, bf16[256,128]{1,0:T(8,128)(2,1)S(1)} %get-tuple-element.31.dq, ...), custom_call_target="tpu_custom_call" | custom-call | tf_op jit(solution)/shard_map/pallas_call | solution.py:225
  71.1 6.0 %collective-permute-start.13 = (bf16[16,192,128]{2,1,0:T(8,128)(2,1)S(1)}, bf16[16,192,128]{2,1,0:T(8,128)(2,1)S(1)}, u32[]{:S(2)}, u32[]{:S(2)}) collective-permute-start(bf16[16,192,128]{2,1,0:T(8,128)(2,1)S(1)} %get-tuple-element.36), channel_id=1, source_target_pairs={{0,8},{1,9},{2,10},{3,11},{4,12},{5,13},{6,14},{7,15},{8,0},{9,1},... | collective-permute-start | bytes 2359304 | tf_op jit(solution)/shard_map/ppermute | solution.py:243
  77.1 1.9 %collective-permute-done.13 = bf16[16,192,128]{2,1,0:T(8,128)(2,1)S(1)} collective-permute-done((bf16[16,192,128]{2,1,0:T(8,128)(2,1)S(1)}, bf16[16,192,128]{2,1,0:T(8,128)(2,1)S(1)}, u32[]{:S(2)}, u32[]{:S(2)}) %collective-permute-start.13) | collective-permute-done | bytes 786464 | tf_op jit(solution)/shard_map/ppermute | solution.py:243
  79.3 2.2 %collective-permute-start.14 = (bf16[8,192,128]{2,1,0:T(8,128)(2,1)S(1)}, bf16[8,192,128]{2,1,0:T(8,128)(2,1)S(1)}, u32[]{:S(2)}, u32[]{:S(2)}) collective-permute-start(bf16[8,192,128]{2,1,0:T(8,128)(2,1)S(1)} %get-tuple-element.43), channel_id=1, source_target_pairs={{0,1},{1,0},{2,3},{3,2},{4,5},{5,4},{6,7},{7,6},{8,24},{9,25},{10,... | collective-permute-start | bytes 1179656 | tf_op jit(solution)/shard_map/ppermute | solution.py:243
  81.5 1.9 %shard_map.80 = bf16[256,1536]{1,0:T(8,128)(2,1)} custom-call(bf16[256,384]{1,0:T(8,128)(2,1)S(1)} %get-tuple-element.37.rows_ref, bf16[4,1536,128]{2,1,0:T(8,128)(2,1)S(1)} %get-tuple-element.29.full), custom_call_target="tpu_custom_call" | custom-call | tf_op jit(solution)/shard_map/pallas_call | solution.py:225
  83.4 3.9 %collective-permute-done.14 = bf16[8,192,128]{2,1,0:T(8,128)(2,1)S(1)} collective-permute-done((bf16[8,192,128]{2,1,0:T(8,128)(2,1)S(1)}, bf16[8,192,128]{2,1,0:T(8,128)(2,1)S(1)}, u32[]{:S(2)}, u32[]{:S(2)}) %collective-permute-start.14) | collective-permute-done | bytes 393248 | tf_op jit(solution)/shard_map/ppermute | solution.py:243
  87.3 2.9 %collective-permute-start.15 = (bf16[4,192,128]{2,1,0:T(8,128)(2,1)S(1)}, bf16[4,192,128]{2,1,0:T(8,128)(2,1)S(1)}, u32[]{:S(2)}, u32[]{:S(2)}) collective-permute-start(bf16[4,192,128]{2,1,0:T(8,128)(2,1)S(1)} %get-tuple-element.44), channel_id=1, source_target_pairs={{0,16},{1,17},{2,18},{3,19},{4,20},{5,21},{6,22},{7,23},{8,9},{9,8... | collective-permute-start | bytes 589832 | tf_op jit(solution)/shard_map/ppermute | solution.py:243
  90.3 3.6 %collective-permute-done.15 = bf16[4,192,128]{2,1,0:T(8,128)(2,1)S(1)} collective-permute-done((bf16[4,192,128]{2,1,0:T(8,128)(2,1)S(1)}, bf16[4,192,128]{2,1,0:T(8,128)(2,1)S(1)}, u32[]{:S(2)}, u32[]{:S(2)}) %collective-permute-start.15) | collective-permute-done | bytes 196640 | tf_op jit(solution)/shard_map/ppermute | solution.py:243
  94.0 1.7 %collective-permute-start.16 = (bf16[2,192,128]{2,1,0:T(8,128)(2,1)S(1)}, bf16[2,192,128]{2,1,0:T(8,128)(2,1)S(1)}, u32[]{:S(2)}, u32[]{:S(2)}) collective-permute-start(bf16[2,192,128]{2,1,0:T(8,128)(2,1)S(1)} %get-tuple-element.49), channel_id=1, source_target_pairs={{0,2},{1,3},{2,0},{3,1},{4,6},{5,7},{6,4},{7,5},{8,10},{9,11},{10,... | collective-permute-start | bytes 294920 | tf_op jit(solution)/shard_map/ppermute | solution.py:243
  95.7 3.0 %collective-permute-done.16 = bf16[2,192,128]{2,1,0:T(8,128)(2,1)S(1)} collective-permute-done((bf16[2,192,128]{2,1,0:T(8,128)(2,1)S(1)}, bf16[2,192,128]{2,1,0:T(8,128)(2,1)S(1)}, u32[]{:S(2)}, u32[]{:S(2)}) %collective-permute-start.16) | collective-permute-done | bytes 98336 | tf_op jit(solution)/shard_map/ppermute | solution.py:243
  98.7 2.6 %collective-permute-start.17 = (bf16[1,192,128]{2,1,0:T(8,128)(2,1)S(1)}, bf16[1,192,128]{2,1,0:T(8,128)(2,1)S(1)}, u32[]{:S(2)}, u32[]{:S(2)}) collective-permute-start(bf16[1,192,128]{2,1,0:T(8,128)(2,1)S(1)} %get-tuple-element.51), channel_id=1, source_target_pairs={{0,4},{1,5},{2,6},{3,7},{4,0},{5,1},{6,2},{7,3},{8,12},{9,13},{10,... | collective-permute-start | bytes 147464 | tf_op jit(solution)/shard_map/ppermute | solution.py:243
  101.3 2.4 %collective-permute-done.17.got = bf16[1,192,128]{2,1,0:T(8,128)(2,1)S(1)} collective-permute-done((bf16[1,192,128]{2,1,0:T(8,128)(2,1)S(1)}, bf16[1,192,128]{2,1,0:T(8,128)(2,1)S(1)}, u32[]{:S(2)}, u32[]{:S(2)}) %collective-permute-start.17) | collective-permute-done | bytes 49184 | tf_op jit(solution)/shard_map/ppermute | solution.py:243
  (34 shorter events, 5.2 us)
Async XLA Ops:
  0.6 30.4 %copy-start.1 = (bf16[256,1536]{1,0:T(8,128)(2,1)S(1)}, bf16[256,1536]{1,0:T(8,128)(2,1)}, u32[]{:S(2)}) copy-start(bf16[256,1536]{1,0:T(8,128)(2,1)} %grad_out.3) | copy-start | bytes 2359300
  0.6 0.9 copy-start.2
  1.5 0.7 copy-start.3
  2.2 28.8 %copy-start = (bf16[256,1536]{1,0:T(8,128)(2,1)S(1)}, bf16[256,1536]{1,0:T(8,128)(2,1)}, u32[]{:S(2)}) copy-start(bf16[256,1536]{1,0:T(8,128)(2,1)} %tokens.3) | copy-start | bytes 2359300
  2.4 6.7 %collective-permute-start = (bf16[1,192,128]{2,1,0:T(8,128)(2,1)S(1)}, bf16[1,192,128]{2,1,0:T(8,128)(2,1)S(1)}, u32[]{:S(2)}, u32[]{:S(2)}) collective-permute-start(bf16[1,192,128]{2,1,0:T(8,128)(2,1)S(1)} %shard_map.75), channel_id=1, source_target_pairs={{0,4},{1,5},{2,6},{3,7},{4,0},{5,1},{6,2},{7,3},{8,12},{9,13},{10,... | collective-permute-start | bytes 147464 | tf_op jit(solution)/shard_map/ppermute | solution.py:243
  9.1 4.7 %collective-permute-start.1 = (bf16[2,192,128]{2,1,0:T(8,128)(2,1)S(1)}, bf16[2,192,128]{2,1,0:T(8,128)(2,1)S(1)}, u32[]{:S(2)}, u32[]{:S(2)}) collective-permute-start(bf16[2,192,128]{2,1,0:T(8,128)(2,1)S(1)} %pad_maximum_fusion.3), channel_id=1, source_target_pairs={{0,2},{1,3},{2,0},{3,1},{4,6},{5,7},{6,4},{7,5},{8,10},{9,11},{10,... | collective-permute-start | bytes 294920 | tf_op jit(solution)/shard_map/ppermute | solution.py:243
  13.8 6.9 %collective-permute-start.2 = (bf16[4,192,128]{2,1,0:T(8,128)(2,1)S(1)}, bf16[4,192,128]{2,1,0:T(8,128)(2,1)S(1)}, u32[]{:S(2)}, u32[]{:S(2)}) collective-permute-start(bf16[4,192,128]{2,1,0:T(8,128)(2,1)S(1)} %pad_maximum_fusion.2), channel_id=1, source_target_pairs={{0,16},{1,17},{2,18},{3,19},{4,20},{5,21},{6,22},{7,23},{8,9},{9,8... | collective-permute-start | bytes 589832 | tf_op jit(solution)/shard_map/ppermute | solution.py:243
  20.8 7.8 %collective-permute-start.3 = (bf16[8,192,128]{2,1,0:T(8,128)(2,1)S(1)}, bf16[8,192,128]{2,1,0:T(8,128)(2,1)S(1)}, u32[]{:S(2)}, u32[]{:S(2)}) collective-permute-start(bf16[8,192,128]{2,1,0:T(8,128)(2,1)S(1)} %pad_maximum_fusion), channel_id=1, source_target_pairs={{0,1},{1,0},{2,3},{3,2},{4,5},{5,4},{6,7},{7,6},{8,24},{9,25},{10,... | collective-permute-start | bytes 1179656 | tf_op jit(solution)/shard_map/ppermute | solution.py:243
  28.7 2.4 %collective-permute-start.4 = (bf16[16,192,128]{2,1,0:T(8,128)(2,1)S(1)}, bf16[16,192,128]{2,1,0:T(8,128)(2,1)S(1)}, u32[]{:S(2)}, u32[]{:S(2)}) collective-permute-start(bf16[16,192,128]{2,1,0:T(8,128)(2,1)S(1)} %constant_dynamic-update-slice_fusion.own), channel_id=1, source_target_pairs={{0,8},{1,9},{2,10},{3,11},{4,12},{5,13},{6,14},{7,15},{8,0},{9,1},... | collective-permute-start | bytes 2359304 | tf_op jit(solution)/shard_map/ppermute | solution.py:243
  33.5 4.5 %collective-permute-start.6 = (bf16[256,256]{1,0:T(8,128)(2,1)S(1)}, bf16[256,256]{1,0:T(8,128)(2,1)S(1)}, u32[]{:S(2)}, u32[]{:S(2)}) collective-permute-start(bf16[256,256]{1,0:T(8,128)(2,1)S(1)} %get-tuple-element.25.own), channel_id=1, source_target_pairs={{1,2},{2,1},{3,4},{4,3},{5,6},{6,5},{9,10},{10,9},{11,12},{12,11},... | collective-permute-start | bytes 393224 | tf_op jit(solution)/shard_map/ppermute | solution.py:243
  34.2 9.4 %collective-permute-start.5 = (bf16[256,256]{1,0:T(8,128)(2,1)S(1)}, bf16[256,256]{1,0:T(8,128)(2,1)S(1)}, u32[]{:S(2)}, u32[]{:S(2)}) collective-permute-start(bf16[256,256]{1,0:T(8,128)(2,1)S(1)} %get-tuple-element.25.own), channel_id=1, source_target_pairs={{0,1},{1,0},{2,3},{3,2},{4,5},{5,4},{6,7},{7,6},{8,9},{9,8},{10,11... | collective-permute-start | bytes 393224 | tf_op jit(solution)/shard_map/ppermute | solution.py:243
  43.6 3.7 %collective-permute-start.8 = (bf16[3,256,256]{2,1,0:T(8,128)(2,1)S(1)}, bf16[3,256,256]{2,1,0:T(8,128)(2,1)S(1)}, u32[]{:S(2)}, u32[]{:S(2)}) collective-permute-start(bf16[3,256,256]{2,1,0:T(8,128)(2,1)S(1)} %pad_maximum_fusion.1), channel_id=1, source_target_pairs={{8,16},{9,17},{10,18},{11,19},{12,20},{13,21},{14,22},{15,23},{16,... | collective-permute-start | bytes 1179656 | tf_op jit(solution)/shard_map/ppermute | solution.py:243
  44.3 4.3 %collective-permute-start.7 = (bf16[3,256,256]{2,1,0:T(8,128)(2,1)S(1)}, bf16[3,256,256]{2,1,0:T(8,128)(2,1)S(1)}, u32[]{:S(2)}, u32[]{:S(2)}) collective-permute-start(bf16[3,256,256]{2,1,0:T(8,128)(2,1)S(1)} %pad_maximum_fusion.1), channel_id=1, source_target_pairs={{0,8},{1,9},{2,10},{3,11},{4,12},{5,13},{6,14},{7,15},{8,0},{9,1},... | collective-permute-start | bytes 1179656 | tf_op jit(solution)/shard_map/ppermute | solution.py:243
  53.4 6.7 %collective-permute-start.9 = (bf16[3,256,256]{2,1,0:T(8,128)(2,1)S(1)}, bf16[3,256,256]{2,1,0:T(8,128)(2,1)S(1)}, u32[]{:S(2)}, u32[]{:S(2)}) collective-permute-start(bf16[3,256,256]{2,1,0:T(8,128)(2,1)S(1)} %get-tuple-element.26), channel_id=1, source_target_pairs={{0,8},{1,9},{2,10},{3,11},{4,12},{5,13},{6,14},{7,15},{8,0},{9,1},... | collective-permute-start | bytes 1179656 | tf_op jit(solution)/shard_map/ppermute | solution.py:243
  57.5 2.6 %collective-permute-start.10 = (bf16[3,256,256]{2,1,0:T(8,128)(2,1)S(1)}, bf16[3,256,256]{2,1,0:T(8,128)(2,1)S(1)}, u32[]{:S(2)}, u32[]{:S(2)}) collective-permute-start(bf16[3,256,256]{2,1,0:T(8,128)(2,1)S(1)} %get-tuple-element.27), channel_id=1, source_target_pairs={{8,16},{9,17},{10,18},{11,19},{12,20},{13,21},{14,22},{15,23},{16,... | collective-permute-start | bytes 1179656 | tf_op jit(solution)/shard_map/ppermute | solution.py:243
  60.2 5.6 %collective-permute-start.12 = (bf16[256,256]{1,0:T(8,128)(2,1)S(1)}, bf16[256,256]{1,0:T(8,128)(2,1)S(1)}, u32[]{:S(2)}, u32[]{:S(2)}) collective-permute-start(bf16[256,256]{1,0:T(8,128)(2,1)S(1)} %get-tuple-element.46), channel_id=1, source_target_pairs={{1,2},{2,1},{3,4},{4,3},{5,6},{6,5},{9,10},{10,9},{11,12},{12,11},... | collective-permute-start | bytes 393224 | tf_op jit(solution)/shard_map/ppermute | solution.py:243
  60.9 8.5 %collective-permute-start.11 = (bf16[256,256]{1,0:T(8,128)(2,1)S(1)}, bf16[256,256]{1,0:T(8,128)(2,1)S(1)}, u32[]{:S(2)}, u32[]{:S(2)}) collective-permute-start(bf16[256,256]{1,0:T(8,128)(2,1)S(1)} %get-tuple-element.47), channel_id=1, source_target_pairs={{0,1},{1,0},{2,3},{3,2},{4,5},{5,4},{6,7},{7,6},{8,9},{9,8},{10,11... | collective-permute-start | bytes 393224 | tf_op jit(solution)/shard_map/ppermute | solution.py:243
  71.1 8.0 %collective-permute-start.13 = (bf16[16,192,128]{2,1,0:T(8,128)(2,1)S(1)}, bf16[16,192,128]{2,1,0:T(8,128)(2,1)S(1)}, u32[]{:S(2)}, u32[]{:S(2)}) collective-permute-start(bf16[16,192,128]{2,1,0:T(8,128)(2,1)S(1)} %get-tuple-element.36), channel_id=1, source_target_pairs={{0,8},{1,9},{2,10},{3,11},{4,12},{5,13},{6,14},{7,15},{8,0},{9,1},... | collective-permute-start | bytes 2359304 | tf_op jit(solution)/shard_map/ppermute | solution.py:243
  79.3 8.0 %collective-permute-start.14 = (bf16[8,192,128]{2,1,0:T(8,128)(2,1)S(1)}, bf16[8,192,128]{2,1,0:T(8,128)(2,1)S(1)}, u32[]{:S(2)}, u32[]{:S(2)}) collective-permute-start(bf16[8,192,128]{2,1,0:T(8,128)(2,1)S(1)} %get-tuple-element.43), channel_id=1, source_target_pairs={{0,1},{1,0},{2,3},{3,2},{4,5},{5,4},{6,7},{7,6},{8,24},{9,25},{10,... | collective-permute-start | bytes 1179656 | tf_op jit(solution)/shard_map/ppermute | solution.py:243
  87.3 6.6 %collective-permute-start.15 = (bf16[4,192,128]{2,1,0:T(8,128)(2,1)S(1)}, bf16[4,192,128]{2,1,0:T(8,128)(2,1)S(1)}, u32[]{:S(2)}, u32[]{:S(2)}) collective-permute-start(bf16[4,192,128]{2,1,0:T(8,128)(2,1)S(1)} %get-tuple-element.44), channel_id=1, source_target_pairs={{0,16},{1,17},{2,18},{3,19},{4,20},{5,21},{6,22},{7,23},{8,9},{9,8... | collective-permute-start | bytes 589832 | tf_op jit(solution)/shard_map/ppermute | solution.py:243
  94.0 4.7 %collective-permute-start.16 = (bf16[2,192,128]{2,1,0:T(8,128)(2,1)S(1)}, bf16[2,192,128]{2,1,0:T(8,128)(2,1)S(1)}, u32[]{:S(2)}, u32[]{:S(2)}) collective-permute-start(bf16[2,192,128]{2,1,0:T(8,128)(2,1)S(1)} %get-tuple-element.49), channel_id=1, source_target_pairs={{0,2},{1,3},{2,0},{3,1},{4,6},{5,7},{6,4},{7,5},{8,10},{9,11},{10,... | collective-permute-start | bytes 294920 | tf_op jit(solution)/shard_map/ppermute | solution.py:243
  98.7 5.1 %collective-permute-start.17 = (bf16[1,192,128]{2,1,0:T(8,128)(2,1)S(1)}, bf16[1,192,128]{2,1,0:T(8,128)(2,1)S(1)}, u32[]{:S(2)}, u32[]{:S(2)}) collective-permute-start(bf16[1,192,128]{2,1,0:T(8,128)(2,1)S(1)} %get-tuple-element.51), channel_id=1, source_target_pairs={{0,4},{1,5},{2,6},{3,7},{4,0},{5,1},{6,2},{7,3},{8,12},{9,13},{10,... | collective-permute-start | bytes 147464 | tf_op jit(solution)/shard_map/ppermute | solution.py:243

commit v3 on v2

--- a/solution.py
+++ b/solution.py
@@ -1,4 +1,5 @@
 import functools
+import math
 
 import jax
 import jax.numpy as jnp
@@ -20,26 +21,17 @@
 
 
 def exchange_steps(slabs, weights):
-    steps = [("weight", bit) for bit in reversed(range(1, bits_of(weights)))]
-    steps += [("slab", bit) for bit in reversed(range(2, bits_of(slabs)))]
-    return steps + [("first", 0), ("second", 0)]
-
-
-def step_mask(step, odd):
-    kind, bit = step
-    if kind == "weight":
-        return 0, 1 << bit
-    if kind == "slab":
-        return 1 << bit, 0
-    along_slab = 1 - odd if kind == "first" else odd
-    return 2 * along_slab, 1 - along_slab
+    steps = [((0, 1 << bit),) * 2 for bit in reversed(range(2, bits_of(weights)))]
+    steps += [((1 << bit, 0),) * 2 for bit in reversed(range(2, bits_of(slabs)))]
+    first, second, third = (2, 0), (0, 1), (0, 2)
+    return steps + [(first, second), (second, third), (third, first)]
 
 
 def block_owner(block, steps, slab, weight, odd):
-    for place, step in enumerate(steps):
+    for place, (even_mask, odd_mask) in enumerate(steps):
         if block >> place & 1:
-            slab_mask, weight_mask = step_mask(step, odd)
-            slab, weight = slab ^ slab_mask, weight ^ weight_mask
+            slab = slab ^ (even_mask[0] * (1 - odd) + odd_mask[0] * odd)
+            weight = weight ^ (even_mask[1] * (1 - odd) + odd_mask[1] * odd)
     return slab, weight
 
 
@@ -47,7 +39,7 @@
     pairs = []
     for s in range(slabs):
         for w in range(weights):
-            slab_mask, weight_mask = step_mask(step, s & 1)
+            slab_mask, weight_mask = step[s & 1]
             pairs.append((s * weights + w, (s ^ slab_mask) * weights + (w ^ weight_mask)))
     return pairs
 
@@ -83,8 +75,20 @@
     return lax.dot_general(a, b, (dims, ((), ())), preferred_element_type=F32)
 
 
-def pack_kernel(qkv_ref, proj_ref, out_ref):
+def pack_kernel(qkv_hbm, proj_hbm, out_ref, qkv_ref, proj_ref, arrived):
+    first = pltpu.make_async_copy(qkv_hbm, qkv_ref, arrived.at[0])
+    second = pltpu.make_async_copy(proj_hbm, proj_ref, arrived.at[1])
+    first.start()
+    second.start()
+    first.wait()
+    second.wait()
     out_ref[0] = jnp.concatenate([qkv_ref[...], proj_ref[...].T], axis=1)
+
+
+def turn_kernel(tokens, grad_out, out_ref):
+    count = tokens.shape[0]
+    out_ref[:, :count] = tokens[...].T
+    out_ref[:, count:] = grad_out[...].T
 
 
 def project_kernel(steps, split, index, own, got, tokens, grad_out, q_ref, kv_ref, co_ref, full):
@@ -106,11 +110,12 @@
 
 def attention_kernel(
     sizes, index, q_ref, co_ref, own, even, odd, slab_even, slab_odd,
-    att_ref, dq_ref, parts_own, parts_even, parts_odd, scores,
+    att_ref, dq_ref, parts_own, parts_even, parts_odd, scores, halves,
 ):
     slab, weight = index[0], index[1]
     slabs, weights = sizes
     root = HD ** (-0.5)
+    binary = root * math.log2(math.e)
     slab_inside = (slab > 0) & (slab < slabs - 1)
     weight_inside = (weight > 0) & (weight < weights - 1)
     blocks = [own, even, odd]
@@ -119,7 +124,7 @@
     query, cotangent = q_ref[...], co_ref[...]
     highest = None
     for j, block in enumerate(blocks):
-        part = dot(query, block[:, :HD], ((1,), (1,))) * root
+        part = dot(query, block[:, :HD], ((1,), (1,)))
         present = None
         if j % 3 == 2:
             present = weight_inside
@@ -129,29 +134,30 @@
             part = part + jnp.where(present, 0.0, -jnp.inf)
         scores[j] = part
         highest = part if highest is None else jnp.maximum(highest, part)
-    highest = jnp.max(highest, axis=1, keepdims=True)
-    total = None
-    for j in range(9):
-        part = jnp.exp(scores[j] - highest)
+    highest = jnp.max(highest, axis=1, keepdims=True) * binary
+    total, attended = None, None
+    for j, block in enumerate(blocks):
+        part = jnp.exp2(scores[j] * binary - highest)
+        total = part if total is None else total + part
+        half = part.astype(BF)
         scores[j] = part
-        total = part if total is None else total + part
+        halves[j] = half
+        weighted = dot(half, block[:, HD:])
+        attended = weighted if attended is None else attended + weighted
     scale = 1.0 / jnp.sum(total, axis=1, keepdims=True)
-    attended = None
-    for j, block in enumerate(blocks):
-        weighted = dot((scores[j] * scale).astype(BF), block[:, HD:])
-        attended = weighted if attended is None else attended + weighted
-    attended = attended.astype(BF)
+    attended = (attended * scale).astype(BF)
     att_ref[...] = attended
     delta = jnp.sum(cotangent.astype(F32) * attended.astype(F32), axis=1, keepdims=True)
+    turned_query = query.T
+    turned_cotangent = (cotangent.astype(F32) * scale).astype(BF).T
     grad_query = None
     for j, (block, out) in enumerate(zip(blocks, outs)):
         grad = dot(cotangent, block[:, HD:], ((1,), (1,)))
-        part = scores[j] * scale
-        grad = (part * (grad - delta)).astype(BF)
+        grad = (scores[j] * ((grad - delta) * scale)).astype(BF)
         step = dot(grad, block[:, :HD])
         grad_query = step if grad_query is None else grad_query + step
-        out[:, :HD] = (dot(grad, query, ((0,), (0,))) * root).astype(BF)
-        out[:, HD:] = dot(part.astype(BF), cotangent, ((0,), (0,))).astype(BF)
+        out[:HD, :] = (dot(turned_query, grad) * root).astype(BF)
+        out[HD:, :] = dot(turned_cotangent, halves[j]).astype(BF)
     dq_ref[...] = (grad_query * root).astype(BF)
 
 
@@ -169,13 +175,13 @@
 
 
 def weight_grads_kernel(
-    steps, slabs, split, index, tokens, grad_out, dq, own, even, odd, att_ref,
+    steps, slabs, split, index, turned, dq, own, even, odd, att_ref,
     rows_ref, keep, send, full,
 ):
     slab, weight = index[0], index[1]
     parity = slab & 1
     pairs = own[...] + even[...].astype(F32) + odd[...].astype(F32)
-    rows = jnp.concatenate([dq[...], pairs.astype(BF)], axis=1)
+    rows = jnp.concatenate([dq[...], pairs.astype(BF).T], axis=1)
     rows_ref[...] = rows
     attended = att_ref[...]
     width = HD // slabs
@@ -186,8 +192,8 @@
     for s in range(slabs):
         left += [rows[:, s * split : (s + 1) * split], left_zeros]
         right += [right_zeros, attended[:, s * width : (s + 1) * width]]
-    grads = dot(tokens[...], jnp.concatenate(left, axis=1), ((0,), (0,)))
-    grads = grads + dot(grad_out[...], jnp.concatenate(right, axis=1), ((0,), (0,)))
+    left, right = jnp.concatenate(left, axis=1), jnp.concatenate(right, axis=1)
+    grads = dot(turned[...], jnp.concatenate([left, right], axis=0))
     lanes = split + width
     for s in range(slabs):
         full[s] = grads[:, s * lanes : (s + 1) * lanes].astype(BF)
@@ -242,7 +248,19 @@
     def swap(values, pairs):
         return lax.ppermute(values, AXES, pairs)
 
-    (held,) = call(pack_kernel, [((1, rows, lanes), BF)], [w_qkv, w_proj])
+    held = pl.pallas_call(
+        pack_kernel,
+        out_shape=pltpu.VMEM((1, rows, lanes), BF),
+        in_specs=[pl.BlockSpec(memory_space=pltpu.HBM)] * 2,
+        out_specs=VMEM,
+        scratch_shapes=[
+            pltpu.VMEM(w_qkv.shape, BF),
+            pltpu.VMEM(w_proj.shape, BF),
+            pltpu.SemaphoreType.DMA((2,)),
+        ],
+        compiler_params=pltpu.CompilerParams(vmem_limit_bytes=32 << 20),
+    )(*(pltpu.with_memory_space_constraint(value, pltpu.HBM) for value in (w_qkv, w_proj)))
+    (turned,) = call(turn_kernel, [((features, 2 * count), BF)], [tokens, grad_out])
     for step in steps:
         held = jnp.concatenate([held, swap(held, step_pairs(step, slabs, weights))], axis=0)
     got = swap(held, core_pairs(slabs, weights))
@@ -256,6 +274,7 @@
     weight_even, weight_odd = (weight_pairs(odd, slabs, weights) for odd in (0, 1))
     slab_even, slab_odd = (slab_pairs(odd, slabs, weights) for odd in (0, 1))
     even, odd = swap(key_value, weight_even), swap(key_value, weight_odd)
+    even, odd, turned = lax.optimization_barrier((even, odd, turned))
     columns = jnp.stack([key_value, even, odd])
     across_even, across_odd = swap(columns, slab_even), swap(columns, slab_odd)
     pair = (3, count, 2 * HD)
@@ -263,7 +282,7 @@
         functools.partial(attention_kernel, (slabs, weights)),
         [((count, HD), BF), ((count, HD), BF), (pair, BF), (pair, BF), (pair, BF)],
         [index, query, cotangent, key_value, even, odd, across_even, across_odd],
-        scratch=[pltpu.VMEM((9, count, count), F32)],
+        scratch=[pltpu.VMEM((9, count, count), F32), pltpu.VMEM((9, count, count), BF)],
         scalars=1,
     )
     parts_even, parts_odd = swap(parts_even, slab_even), swap(parts_odd, slab_odd)
@@ -288,7 +307,7 @@
     grad_rows, keep, send = call(
         functools.partial(weight_grads_kernel, steps, slabs, split),
         [((count, 3 * HD), BF), (half, BF), (half, BF)],
-        [index, tokens, grad_out, grad_query, summed(0), even, odd, attended],
+        [index, turned, grad_query, summed(0), even, odd, attended],
         scratch=[pltpu.VMEM((slabs, features, lanes), BF)],
         scalars=1,
     )

time: 105 us -> 102 us (0.971)
  waiting for transfers between devices: 44.3 us -> 42.5 us
  local copies, waits for them, and re-layouts: 1.7 us -> 0.12 us
    ppermute x18, waiting for transfers between devices: 44.3 us -> 42.5 us  [swap(): return lax.ppermute(values, AXES, pairs)]
    unnamed x12 -> x8, local copies, waits for them, and re-layouts: 1.65 us -> 0.07 us
    pallas_call x0 -> x1, Pallas kernels: none -> 1.08 us  [local(): pl.pallas_call(pack_kernel, out_shape=pltpu.VMEM((1, rows, lanes), BF), i...]
where the time goes in v3:
time: 102 us
  starting transfers between devices  43.9 us (43%)
  waiting for transfers between devices  42.5 us (42%)
  Pallas kernels  14.1 us (14%)
    ppermute x18, starting transfers between devices, swap(): return lax.ppermute(values, AXES, pairs)  43.9 us
    ppermute x18, waiting for transfers between devices, swap(): return lax.ppermute(values, AXES, pairs)  42.5 us
    pallas_call x7, Pallas kernels, call(): pl.pallas_call(kernel, out_shape=[make(shape, kind) for shape, kind in ou...  13 us
  transfers between devices with their start and end apart: 18, of which 13 were waited for; matrix products, arithmetic and copies ran while one was open for 0% of the time, Pallas kernels for 4%

profile of v3, /device:TPU:0, one launch (start us, length us, event | category | flops | bytes accessed | tf_op | source)
XLA Modules:
  0.0 102.0 jit_solution(9404797250848317812)
XLA Ops:
  0.7 1.1 %shard_map.75 = bf16[1,192,128]{2,1,0:T(8,128)(2,1)S(1)} custom-call(bf16[192,96]{1,0:T(8,128)(2,1)} %qkv_hbm.1, bf16[32,192]{1,0:T(8,128)(2,1)} %proj_hbm.1), custom_call_target="tpu_custom_call" | custom-call | tf_op jit(solution)/shard_map/pallas_call | solution.py:251
  1.7 4.1 %collective-permute-start = (bf16[1,192,128]{2,1,0:T(8,128)(2,1)S(1)}, bf16[1,192,128]{2,1,0:T(8,128)(2,1)S(1)}, u32[]{:S(2)}, u32[]{:S(2)}) collective-permute-start(bf16[1,192,128]{2,1,0:T(8,128)(2,1)S(1)} %shard_map.75), channel_id=1, source_target_pairs={{0,4},{1,5},{2,6},{3,7},{4,0},{5,1},{6,2},{7,3},{8,12},{9,13},{10,... | collective-permute-start | bytes 147464 | tf_op jit(solution)/shard_map/ppermute | solution.py:249
  5.9 2.6 %collective-permute-done = bf16[1,192,128]{2,1,0:T(8,128)(2,1)S(1)} collective-permute-done((bf16[1,192,128]{2,1,0:T(8,128)(2,1)S(1)}, bf16[1,192,128]{2,1,0:T(8,128)(2,1)S(1)}, u32[]{:S(2)}, u32[]{:S(2)}) %collective-permute-start) | collective-permute-done | bytes 49184 | tf_op jit(solution)/shard_map/ppermute | solution.py:249
  8.5 1.8 %collective-permute-start.1 = (bf16[2,192,128]{2,1,0:T(8,128)(2,1)S(1)}, bf16[2,192,128]{2,1,0:T(8,128)(2,1)S(1)}, u32[]{:S(2)}, u32[]{:S(2)}) collective-permute-start(bf16[2,192,128]{2,1,0:T(8,128)(2,1)S(1)} %pad_maximum_fusion.3), channel_id=1, source_target_pairs={{0,16},{1,17},{2,18},{3,19},{4,20},{5,21},{6,22},{7,23},{8,9},{9,8... | collective-permute-start | bytes 294920 | tf_op jit(solution)/shard_map/ppermute | solution.py:249
  10.2 2.9 %collective-permute-done.1 = bf16[2,192,128]{2,1,0:T(8,128)(2,1)S(1)} collective-permute-done((bf16[2,192,128]{2,1,0:T(8,128)(2,1)S(1)}, bf16[2,192,128]{2,1,0:T(8,128)(2,1)S(1)}, u32[]{:S(2)}, u32[]{:S(2)}) %collective-permute-start.1) | collective-permute-done | bytes 98336 | tf_op jit(solution)/shard_map/ppermute | solution.py:249
  13.2 1.8 %collective-permute-start.2 = (bf16[4,192,128]{2,1,0:T(8,128)(2,1)S(1)}, bf16[4,192,128]{2,1,0:T(8,128)(2,1)S(1)}, u32[]{:S(2)}, u32[]{:S(2)}) collective-permute-start(bf16[4,192,128]{2,1,0:T(8,128)(2,1)S(1)} %pad_maximum_fusion.2), channel_id=1, source_target_pairs={{0,1},{1,0},{2,3},{3,2},{4,5},{5,4},{6,7},{7,6},{8,10},{9,11},{10,... | collective-permute-start | bytes 589832 | tf_op jit(solution)/shard_map/ppermute | solution.py:249
  15.0 3.9 %collective-permute-done.2 = bf16[4,192,128]{2,1,0:T(8,128)(2,1)S(1)} collective-permute-done((bf16[4,192,128]{2,1,0:T(8,128)(2,1)S(1)}, bf16[4,192,128]{2,1,0:T(8,128)(2,1)S(1)}, u32[]{:S(2)}, u32[]{:S(2)}) %collective-permute-start.2) | collective-permute-done | bytes 196640 | tf_op jit(solution)/shard_map/ppermute | solution.py:249
  19.0 1.4 %collective-permute-start.3 = (bf16[8,192,128]{2,1,0:T(8,128)(2,1)S(1)}, bf16[8,192,128]{2,1,0:T(8,128)(2,1)S(1)}, u32[]{:S(2)}, u32[]{:S(2)}) collective-permute-start(bf16[8,192,128]{2,1,0:T(8,128)(2,1)S(1)} %pad_maximum_fusion), channel_id=1, source_target_pairs={{0,2},{1,3},{2,0},{3,1},{4,6},{5,7},{6,4},{7,5},{8,24},{9,25},{10,... | collective-permute-start | bytes 1179656 | tf_op jit(solution)/shard_map/ppermute | solution.py:249
  20.5 6.3 %collective-permute-done.3 = bf16[8,192,128]{2,1,0:T(8,128)(2,1)S(1)} collective-permute-done((bf16[8,192,128]{2,1,0:T(8,128)(2,1)S(1)}, bf16[8,192,128]{2,1,0:T(8,128)(2,1)S(1)}, u32[]{:S(2)}, u32[]{:S(2)}) %collective-permute-start.3) | collective-permute-done | bytes 393248 | tf_op jit(solution)/shard_map/ppermute | solution.py:249
  27.0 2.2 %collective-permute-done.4.got = bf16[16,192,128]{2,1,0:T(8,128)(2,1)S(1)} collective-permute-done((bf16[16,192,128]{2,1,0:T(8,128)(2,1)S(1)}, bf16[16,192,128]{2,1,0:T(8,128)(2,1)S(1)}, u32[]{:S(2)}, u32[]{:S(2)}) %collective-permute-start.4) | collective-permute-done | bytes 786464 | tf_op jit(solution)/shard_map/ppermute | solution.py:249
  29.2 2.5 %shard_map.76 = (bf16[256,128]{1,0:T(8,128)(2,1)S(1)}, bf16[256,256]{1,0:T(8,128)(2,1)S(1)}, bf16[256,128]{1,0:T(8,128)(2,1)S(1)}, bf16[4,1536,128]{2,1,0:T(8,128)(2,1)S(1)}) custom-call(s32[2]{0:T(128)S(1)} %pad_add_fusion.index, bf16[16,192,128]{2,1,0:T(8,128)(2,1)S(1)} %constant_dynamic-update-slice_fusion.own, ...), custom_call_target="tpu_custom_call" | custom-call | tf_op jit(solution)/shard_map/pallas_call | solution.py:231
  32.4 4.1 %collective-permute-start.5 = (bf16[256,256]{1,0:T(8,128)(2,1)S(1)}, bf16[256,256]{1,0:T(8,128)(2,1)S(1)}, u32[]{:S(2)}, u32[]{:S(2)}) collective-permute-start(bf16[256,256]{1,0:T(8,128)(2,1)S(1)} %get-tuple-element.28.own), channel_id=1, source_target_pairs={{0,1},{1,0},{2,3},{3,2},{4,5},{5,4},{6,7},{7,6},{8,9},{9,8},{10,11... | collective-permute-start | bytes 393224 | tf_op jit(solution)/shard_map/ppermute | solution.py:249
  37.0 5.1 %collective-permute-done.5.even = bf16[256,256]{1,0:T(8,128)(2,1)S(1)} collective-permute-done((bf16[256,256]{1,0:T(8,128)(2,1)S(1)}, bf16[256,256]{1,0:T(8,128)(2,1)S(1)}, u32[]{:S(2)}, u32[]{:S(2)}) %collective-permute-start.5) | collective-permute-done | bytes 131104 | tf_op jit(solution)/shard_map/ppermute | solution.py:249
  42.9 2.9 %collective-permute-start.7 = (bf16[3,256,256]{2,1,0:T(8,128)(2,1)S(1)}, bf16[3,256,256]{2,1,0:T(8,128)(2,1)S(1)}, u32[]{:S(2)}, u32[]{:S(2)}) collective-permute-start(bf16[3,256,256]{2,1,0:T(8,128)(2,1)S(1)} %pad_maximum_fusion.1), channel_id=1, source_target_pairs={{0,8},{1,9},{2,10},{3,11},{4,12},{5,13},{6,14},{7,15},{8,0},{9,1},... | collective-permute-start | bytes 1179656 | tf_op jit(solution)/shard_map/ppermute | solution.py:249
  45.8 1.3 %collective-permute-done.7.slab_even = bf16[3,256,256]{2,1,0:T(8,128)(2,1)S(1)} collective-permute-done((bf16[3,256,256]{2,1,0:T(8,128)(2,1)S(1)}, bf16[3,256,256]{2,1,0:T(8,128)(2,1)S(1)}, u32[]{:S(2)}, u32[]{:S(2)}) %collective-permute-start.7) | collective-permute-done | bytes 393248 | tf_op jit(solution)/shard_map/ppermute | solution.py:249
  47.1 3.7 %shard_map.78 = (bf16[256,128]{1,0:T(8,128)(2,1)S(1)}, bf16[256,128]{1,0:T(8,128)(2,1)S(1)}, bf16[3,256,256]{2,1,0:T(8,128)(2,1)S(1)}, bf16[3,256,256]{2,1,0:T(8,128)(2,1)S(1)}, bf16[3,256,256]{2,1,0:T(8,128)(2,1)S(1)}) custom-call(s32[2]{0:T(128)S(1)} %pad_add_fusion.index, bf16[256,128]{1,0:T(8,128)(2,1)S(1)} %get-tuple-element.26.q_ref, ...), custom_call_target="tpu_custom_call" | custom-call | tf_op jit(solution)/shard_map/pallas_call | solution.py:231
  50.8 4.2 %collective-permute-start.9 = (bf16[3,256,256]{2,1,0:T(8,128)(2,1)S(1)}, bf16[3,256,256]{2,1,0:T(8,128)(2,1)S(1)}, u32[]{:S(2)}, u32[]{:S(2)}) collective-permute-start(bf16[3,256,256]{2,1,0:T(8,128)(2,1)S(1)} %get-tuple-element.31), channel_id=1, source_target_pairs={{0,8},{1,9},{2,10},{3,11},{4,12},{5,13},{6,14},{7,15},{8,0},{9,1},... | collective-permute-start | bytes 1179656 | tf_op jit(solution)/shard_map/ppermute | solution.py:249
  55.7 1.9 %shard_map.79 = bf16[256,1536]{1,0:T(8,128)(2,1)} custom-call(bf16[256,128]{1,0:T(8,128)(2,1)S(1)} %get-tuple-element.33.att_ref, bf16[4,1536,128]{2,1,0:T(8,128)(2,1)S(1)} %get-tuple-element.34.full), custom_call_target="tpu_custom_call" | custom-call | tf_op jit(solution)/shard_map/pallas_call | solution.py:231
  58.4 4.9 %collective-permute-start.11 = (bf16[256,256]{1,0:T(8,128)(2,1)S(1)}, bf16[256,256]{1,0:T(8,128)(2,1)S(1)}, u32[]{:S(2)}, u32[]{:S(2)}) collective-permute-start(bf16[256,256]{1,0:T(8,128)(2,1)S(1)} %get-tuple-element.53), channel_id=1, source_target_pairs={{0,1},{1,0},{2,3},{3,2},{4,5},{5,4},{6,7},{7,6},{8,9},{9,8},{10,11... | collective-permute-start | bytes 393224 | tf_op jit(solution)/shard_map/ppermute | solution.py:249
  63.3 3.6 %collective-permute-done.11.even = bf16[256,256]{1,0:T(8,128)(2,1)S(1)} collective-permute-done((bf16[256,256]{1,0:T(8,128)(2,1)S(1)}, bf16[256,256]{1,0:T(8,128)(2,1)S(1)}, u32[]{:S(2)}, u32[]{:S(2)}) %collective-permute-start.11) | collective-permute-done | bytes 131104 | tf_op jit(solution)/shard_map/ppermute | solution.py:249
  66.9 1.8 %shard_map.80 = (bf16[256,384]{1,0:T(8,128)(2,1)S(1)}, bf16[16,192,128]{2,1,0:T(8,128)(2,1)S(1)}, bf16[16,192,128]{2,1,0:T(8,128)(2,1)S(1)}) custom-call(s32[2]{0:T(128)S(1)} %pad_add_fusion.index, bf16[1536,512]{1,0:T(8,128)(2,1)S(1)} %shard_map.77.turned, bf16[256,128]{1,0:T(8,128)(2,1)S(1)} %get-tuple-element.37.dq, ...), custom_call_target="tpu_custom_call" | custom-call | tf_op jit(solution)/shard_map/pallas_call | solution.py:231
  68.7 6.0 %collective-permute-start.13 = (bf16[16,192,128]{2,1,0:T(8,128)(2,1)S(1)}, bf16[16,192,128]{2,1,0:T(8,128)(2,1)S(1)}, u32[]{:S(2)}, u32[]{:S(2)}) collective-permute-start(bf16[16,192,128]{2,1,0:T(8,128)(2,1)S(1)} %get-tuple-element.42), channel_id=1, source_target_pairs={{0,8},{1,9},{2,10},{3,11},{4,12},{5,13},{6,14},{7,15},{8,0},{9,1},... | collective-permute-start | bytes 2359304 | tf_op jit(solution)/shard_map/ppermute | solution.py:249
  74.8 1.9 %collective-permute-done.13 = bf16[16,192,128]{2,1,0:T(8,128)(2,1)S(1)} collective-permute-done((bf16[16,192,128]{2,1,0:T(8,128)(2,1)S(1)}, bf16[16,192,128]{2,1,0:T(8,128)(2,1)S(1)}, u32[]{:S(2)}, u32[]{:S(2)}) %collective-permute-start.13) | collective-permute-done | bytes 786464 | tf_op jit(solution)/shard_map/ppermute | solution.py:249
  76.9 1.9 %collective-permute-start.14 = (bf16[8,192,128]{2,1,0:T(8,128)(2,1)S(1)}, bf16[8,192,128]{2,1,0:T(8,128)(2,1)S(1)}, u32[]{:S(2)}, u32[]{:S(2)}) collective-permute-start(bf16[8,192,128]{2,1,0:T(8,128)(2,1)S(1)} %get-tuple-element.49), channel_id=1, source_target_pairs={{0,2},{1,3},{2,0},{3,1},{4,6},{5,7},{6,4},{7,5},{8,24},{9,25},{10,... | collective-permute-start | bytes 1179656 | tf_op jit(solution)/shard_map/ppermute | solution.py:249
  78.8 1.9 %shard_map.81 = bf16[256,1536]{1,0:T(8,128)(2,1)} custom-call(bf16[256,384]{1,0:T(8,128)(2,1)S(1)} %get-tuple-element.43.rows_ref, bf16[4,1536,128]{2,1,0:T(8,128)(2,1)S(1)} %get-tuple-element.34.full), custom_call_target="tpu_custom_call" | custom-call | tf_op jit(solution)/shard_map/pallas_call | solution.py:231
  80.7 4.0 %collective-permute-done.14 = bf16[8,192,128]{2,1,0:T(8,128)(2,1)S(1)} collective-permute-done((bf16[8,192,128]{2,1,0:T(8,128)(2,1)S(1)}, bf16[8,192,128]{2,1,0:T(8,128)(2,1)S(1)}, u32[]{:S(2)}, u32[]{:S(2)}) %collective-permute-start.14) | collective-permute-done | bytes 393248 | tf_op jit(solution)/shard_map/ppermute | solution.py:249
  84.8 2.3 %collective-permute-start.15 = (bf16[4,192,128]{2,1,0:T(8,128)(2,1)S(1)}, bf16[4,192,128]{2,1,0:T(8,128)(2,1)S(1)}, u32[]{:S(2)}, u32[]{:S(2)}) collective-permute-start(bf16[4,192,128]{2,1,0:T(8,128)(2,1)S(1)} %get-tuple-element.50), channel_id=1, source_target_pairs={{0,1},{1,0},{2,3},{3,2},{4,5},{5,4},{6,7},{7,6},{8,10},{9,11},{10,... | collective-permute-start | bytes 589832 | tf_op jit(solution)/shard_map/ppermute | solution.py:249
  87.1 3.6 %collective-permute-done.15 = bf16[4,192,128]{2,1,0:T(8,128)(2,1)S(1)} collective-permute-done((bf16[4,192,128]{2,1,0:T(8,128)(2,1)S(1)}, bf16[4,192,128]{2,1,0:T(8,128)(2,1)S(1)}, u32[]{:S(2)}, u32[]{:S(2)}) %collective-permute-start.15) | collective-permute-done | bytes 196640 | tf_op jit(solution)/shard_map/ppermute | solution.py:249
  90.8 2.8 %collective-permute-start.16 = (bf16[2,192,128]{2,1,0:T(8,128)(2,1)S(1)}, bf16[2,192,128]{2,1,0:T(8,128)(2,1)S(1)}, u32[]{:S(2)}, u32[]{:S(2)}) collective-permute-start(bf16[2,192,128]{2,1,0:T(8,128)(2,1)S(1)} %get-tuple-element.55), channel_id=1, source_target_pairs={{0,16},{1,17},{2,18},{3,19},{4,20},{5,21},{6,22},{7,23},{8,9},{9,8... | collective-permute-start | bytes 294920 | tf_op jit(solution)/shard_map/ppermute | solution.py:249
  93.5 2.6 %collective-permute-done.16 = bf16[2,192,128]{2,1,0:T(8,128)(2,1)S(1)} collective-permute-done((bf16[2,192,128]{2,1,0:T(8,128)(2,1)S(1)}, bf16[2,192,128]{2,1,0:T(8,128)(2,1)S(1)}, u32[]{:S(2)}, u32[]{:S(2)}) %collective-permute-start.16) | collective-permute-done | bytes 98336 | tf_op jit(solution)/shard_map/ppermute | solution.py:249
  96.2 2.8 %collective-permute-start.17 = (bf16[1,192,128]{2,1,0:T(8,128)(2,1)S(1)}, bf16[1,192,128]{2,1,0:T(8,128)(2,1)S(1)}, u32[]{:S(2)}, u32[]{:S(2)}) collective-permute-start(bf16[1,192,128]{2,1,0:T(8,128)(2,1)S(1)} %get-tuple-element.57), channel_id=1, source_target_pairs={{0,4},{1,5},{2,6},{3,7},{4,0},{5,1},{6,2},{7,3},{8,12},{9,13},{10,... | collective-permute-start | bytes 147464 | tf_op jit(solution)/shard_map/ppermute | solution.py:249
  98.9 2.3 %collective-permute-done.17.got = bf16[1,192,128]{2,1,0:T(8,128)(2,1)S(1)} collective-permute-done((bf16[1,192,128]{2,1,0:T(8,128)(2,1)S(1)}, bf16[1,192,128]{2,1,0:T(8,128)(2,1)S(1)}, u32[]{:S(2)}, u32[]{:S(2)}) %collective-permute-start.17) | collective-permute-done | bytes 49184 | tf_op jit(solution)/shard_map/ppermute | solution.py:249
  (31 shorter events, 4.8 us)
Async XLA Ops:
  0.6 28.6 %copy-start.1 = (bf16[256,1536]{1,0:T(8,128)(2,1)S(1)}, bf16[256,1536]{1,0:T(8,128)(2,1)}, u32[]{:S(2)}) copy-start(bf16[256,1536]{1,0:T(8,128)(2,1)} %grad_out.3) | copy-start | bytes 2359300
  0.6 28.6 %copy-start = (bf16[256,1536]{1,0:T(8,128)(2,1)S(1)}, bf16[256,1536]{1,0:T(8,128)(2,1)}, u32[]{:S(2)}) copy-start(bf16[256,1536]{1,0:T(8,128)(2,1)} %tokens.3) | copy-start | bytes 2359300
  1.7 6.7 %collective-permute-start = (bf16[1,192,128]{2,1,0:T(8,128)(2,1)S(1)}, bf16[1,192,128]{2,1,0:T(8,128)(2,1)S(1)}, u32[]{:S(2)}, u32[]{:S(2)}) collective-permute-start(bf16[1,192,128]{2,1,0:T(8,128)(2,1)S(1)} %shard_map.75), channel_id=1, source_target_pairs={{0,4},{1,5},{2,6},{3,7},{4,0},{5,1},{6,2},{7,3},{8,12},{9,13},{10,... | collective-permute-start | bytes 147464 | tf_op jit(solution)/shard_map/ppermute | solution.py:249
  8.5 4.7 %collective-permute-start.1 = (bf16[2,192,128]{2,1,0:T(8,128)(2,1)S(1)}, bf16[2,192,128]{2,1,0:T(8,128)(2,1)S(1)}, u32[]{:S(2)}, u32[]{:S(2)}) collective-permute-start(bf16[2,192,128]{2,1,0:T(8,128)(2,1)S(1)} %pad_maximum_fusion.3), channel_id=1, source_target_pairs={{0,16},{1,17},{2,18},{3,19},{4,20},{5,21},{6,22},{7,23},{8,9},{9,8... | collective-permute-start | bytes 294920 | tf_op jit(solution)/shard_map/ppermute | solution.py:249
  13.2 5.7 %collective-permute-start.2 = (bf16[4,192,128]{2,1,0:T(8,128)(2,1)S(1)}, bf16[4,192,128]{2,1,0:T(8,128)(2,1)S(1)}, u32[]{:S(2)}, u32[]{:S(2)}) collective-permute-start(bf16[4,192,128]{2,1,0:T(8,128)(2,1)S(1)} %pad_maximum_fusion.2), channel_id=1, source_target_pairs={{0,1},{1,0},{2,3},{3,2},{4,5},{5,4},{6,7},{7,6},{8,10},{9,11},{10,... | collective-permute-start | bytes 589832 | tf_op jit(solution)/shard_map/ppermute | solution.py:249
  19.0 7.8 %collective-permute-start.3 = (bf16[8,192,128]{2,1,0:T(8,128)(2,1)S(1)}, bf16[8,192,128]{2,1,0:T(8,128)(2,1)S(1)}, u32[]{:S(2)}, u32[]{:S(2)}) collective-permute-start(bf16[8,192,128]{2,1,0:T(8,128)(2,1)S(1)} %pad_maximum_fusion), channel_id=1, source_target_pairs={{0,2},{1,3},{2,0},{3,1},{4,6},{5,7},{6,4},{7,5},{8,24},{9,25},{10,... | collective-permute-start | bytes 1179656 | tf_op jit(solution)/shard_map/ppermute | solution.py:249
  26.9 2.4 %collective-permute-start.4 = (bf16[16,192,128]{2,1,0:T(8,128)(2,1)S(1)}, bf16[16,192,128]{2,1,0:T(8,128)(2,1)S(1)}, u32[]{:S(2)}, u32[]{:S(2)}) collective-permute-start(bf16[16,192,128]{2,1,0:T(8,128)(2,1)S(1)} %constant_dynamic-update-slice_fusion.own), channel_id=1, source_target_pairs={{0,8},{1,9},{2,10},{3,11},{4,12},{5,13},{6,14},{7,15},{8,0},{9,1},... | collective-permute-start | bytes 2359304 | tf_op jit(solution)/shard_map/ppermute | solution.py:249
  31.7 5.3 %collective-permute-start.6 = (bf16[256,256]{1,0:T(8,128)(2,1)S(1)}, bf16[256,256]{1,0:T(8,128)(2,1)S(1)}, u32[]{:S(2)}, u32[]{:S(2)}) collective-permute-start(bf16[256,256]{1,0:T(8,128)(2,1)S(1)} %get-tuple-element.28.own), channel_id=1, source_target_pairs={{1,2},{2,1},{3,4},{4,3},{5,6},{6,5},{9,10},{10,9},{11,12},{12,11},... | collective-permute-start | bytes 393224 | tf_op jit(solution)/shard_map/ppermute | solution.py:249
  32.4 9.7 %collective-permute-start.5 = (bf16[256,256]{1,0:T(8,128)(2,1)S(1)}, bf16[256,256]{1,0:T(8,128)(2,1)S(1)}, u32[]{:S(2)}, u32[]{:S(2)}) collective-permute-start(bf16[256,256]{1,0:T(8,128)(2,1)S(1)} %get-tuple-element.28.own), channel_id=1, source_target_pairs={{0,1},{1,0},{2,3},{3,2},{4,5},{5,4},{6,7},{7,6},{8,9},{9,8},{10,11... | collective-permute-start | bytes 393224 | tf_op jit(solution)/shard_map/ppermute | solution.py:249
  42.2 3.6 %collective-permute-start.8 = (bf16[3,256,256]{2,1,0:T(8,128)(2,1)S(1)}, bf16[3,256,256]{2,1,0:T(8,128)(2,1)S(1)}, u32[]{:S(2)}, u32[]{:S(2)}) collective-permute-start(bf16[3,256,256]{2,1,0:T(8,128)(2,1)S(1)} %pad_maximum_fusion.1), channel_id=1, source_target_pairs={{8,16},{9,17},{10,18},{11,19},{12,20},{13,21},{14,22},{15,23},{16,... | collective-permute-start | bytes 1179656 | tf_op jit(solution)/shard_map/ppermute | solution.py:249
  42.9 4.2 %collective-permute-start.7 = (bf16[3,256,256]{2,1,0:T(8,128)(2,1)S(1)}, bf16[3,256,256]{2,1,0:T(8,128)(2,1)S(1)}, u32[]{:S(2)}, u32[]{:S(2)}) collective-permute-start(bf16[3,256,256]{2,1,0:T(8,128)(2,1)S(1)} %pad_maximum_fusion.1), channel_id=1, source_target_pairs={{0,8},{1,9},{2,10},{3,11},{4,12},{5,13},{6,14},{7,15},{8,0},{9,1},... | collective-permute-start | bytes 1179656 | tf_op jit(solution)/shard_map/ppermute | solution.py:249
  50.8 6.8 %collective-permute-start.9 = (bf16[3,256,256]{2,1,0:T(8,128)(2,1)S(1)}, bf16[3,256,256]{2,1,0:T(8,128)(2,1)S(1)}, u32[]{:S(2)}, u32[]{:S(2)}) collective-permute-start(bf16[3,256,256]{2,1,0:T(8,128)(2,1)S(1)} %get-tuple-element.31), channel_id=1, source_target_pairs={{0,8},{1,9},{2,10},{3,11},{4,12},{5,13},{6,14},{7,15},{8,0},{9,1},... | collective-permute-start | bytes 1179656 | tf_op jit(solution)/shard_map/ppermute | solution.py:249
  55.0 2.6 %collective-permute-start.10 = (bf16[3,256,256]{2,1,0:T(8,128)(2,1)S(1)}, bf16[3,256,256]{2,1,0:T(8,128)(2,1)S(1)}, u32[]{:S(2)}, u32[]{:S(2)}) collective-permute-start(bf16[3,256,256]{2,1,0:T(8,128)(2,1)S(1)} %get-tuple-element.32), channel_id=1, source_target_pairs={{8,16},{9,17},{10,18},{11,19},{12,20},{13,21},{14,22},{15,23},{16,... | collective-permute-start | bytes 1179656 | tf_op jit(solution)/shard_map/ppermute | solution.py:249
  57.8 5.6 %collective-permute-start.12 = (bf16[256,256]{1,0:T(8,128)(2,1)S(1)}, bf16[256,256]{1,0:T(8,128)(2,1)S(1)}, u32[]{:S(2)}, u32[]{:S(2)}) collective-permute-start(bf16[256,256]{1,0:T(8,128)(2,1)S(1)} %get-tuple-element.52), channel_id=1, source_target_pairs={{1,2},{2,1},{3,4},{4,3},{5,6},{6,5},{9,10},{10,9},{11,12},{12,11},... | collective-permute-start | bytes 393224 | tf_op jit(solution)/shard_map/ppermute | solution.py:249
  58.4 8.5 %collective-permute-start.11 = (bf16[256,256]{1,0:T(8,128)(2,1)S(1)}, bf16[256,256]{1,0:T(8,128)(2,1)S(1)}, u32[]{:S(2)}, u32[]{:S(2)}) collective-permute-start(bf16[256,256]{1,0:T(8,128)(2,1)S(1)} %get-tuple-element.53), channel_id=1, source_target_pairs={{0,1},{1,0},{2,3},{3,2},{4,5},{5,4},{6,7},{7,6},{8,9},{9,8},{10,11... | collective-permute-start | bytes 393224 | tf_op jit(solution)/shard_map/ppermute | solution.py:249
  68.7 8.0 %collective-permute-start.13 = (bf16[16,192,128]{2,1,0:T(8,128)(2,1)S(1)}, bf16[16,192,128]{2,1,0:T(8,128)(2,1)S(1)}, u32[]{:S(2)}, u32[]{:S(2)}) collective-permute-start(bf16[16,192,128]{2,1,0:T(8,128)(2,1)S(1)} %get-tuple-element.42), channel_id=1, source_target_pairs={{0,8},{1,9},{2,10},{3,11},{4,12},{5,13},{6,14},{7,15},{8,0},{9,1},... | collective-permute-start | bytes 2359304 | tf_op jit(solution)/shard_map/ppermute | solution.py:249
  76.9 7.8 %collective-permute-start.14 = (bf16[8,192,128]{2,1,0:T(8,128)(2,1)S(1)}, bf16[8,192,128]{2,1,0:T(8,128)(2,1)S(1)}, u32[]{:S(2)}, u32[]{:S(2)}) collective-permute-start(bf16[8,192,128]{2,1,0:T(8,128)(2,1)S(1)} %get-tuple-element.49), channel_id=1, source_target_pairs={{0,2},{1,3},{2,0},{3,1},{4,6},{5,7},{6,4},{7,5},{8,24},{9,25},{10,... | collective-permute-start | bytes 1179656 | tf_op jit(solution)/shard_map/ppermute | solution.py:249
  84.8 5.9 %collective-permute-start.15 = (bf16[4,192,128]{2,1,0:T(8,128)(2,1)S(1)}, bf16[4,192,128]{2,1,0:T(8,128)(2,1)S(1)}, u32[]{:S(2)}, u32[]{:S(2)}) collective-permute-start(bf16[4,192,128]{2,1,0:T(8,128)(2,1)S(1)} %get-tuple-element.50), channel_id=1, source_target_pairs={{0,1},{1,0},{2,3},{3,2},{4,5},{5,4},{6,7},{7,6},{8,10},{9,11},{10,... | collective-permute-start | bytes 589832 | tf_op jit(solution)/shard_map/ppermute | solution.py:249
  90.8 5.4 %collective-permute-start.16 = (bf16[2,192,128]{2,1,0:T(8,128)(2,1)S(1)}, bf16[2,192,128]{2,1,0:T(8,128)(2,1)S(1)}, u32[]{:S(2)}, u32[]{:S(2)}) collective-permute-start(bf16[2,192,128]{2,1,0:T(8,128)(2,1)S(1)} %get-tuple-element.55), channel_id=1, source_target_pairs={{0,16},{1,17},{2,18},{3,19},{4,20},{5,21},{6,22},{7,23},{8,9},{9,8... | collective-permute-start | bytes 294920 | tf_op jit(solution)/shard_map/ppermute | solution.py:249
  96.2 5.1 %collective-permute-start.17 = (bf16[1,192,128]{2,1,0:T(8,128)(2,1)S(1)}, bf16[1,192,128]{2,1,0:T(8,128)(2,1)S(1)}, u32[]{:S(2)}, u32[]{:S(2)}) collective-permute-start(bf16[1,192,128]{2,1,0:T(8,128)(2,1)S(1)} %get-tuple-element.57), channel_id=1, source_target_pairs={{0,4},{1,5},{2,6},{3,7},{4,0},{5,1},{6,2},{7,3},{8,12},{9,13},{10,... | collective-permute-start | bytes 147464 | tf_op jit(solution)/shard_map/ppermute | solution.py:249

commit v4 on v3

--- a/solution.py
+++ b/solution.py
@@ -91,21 +91,23 @@
     out_ref[:, count:] = grad_out[...].T
 
 
-def project_kernel(steps, split, index, own, got, tokens, grad_out, q_ref, kv_ref, co_ref, full):
+def key_value_kernel(steps, split, index, own, got, tokens, kv_ref, qkv_ref, proj_ref, full):
     slab, weight = index[0], index[1]
     odd = slab & 1
     rows = own.shape[1]
-    for half, (source, where, parity) in enumerate(((own, slab, odd), (got, slab ^ 1, 1 - odd))):
+    for source, where, parity in ((own, slab, odd), (got, slab ^ 1, 1 - odd)):
         for block in range(own.shape[0]):
             s, w = block_owner(block, steps, where, weight, parity)
             full[s, pl.ds(pl.multiple_of(w * rows, rows), rows), :] = source[block]
     slabs = full.shape[0]
-    projected = [dot(tokens[...], full[s])[:, :split].astype(BF) for s in range(slabs)]
-    cotangent = [dot(grad_out[...], full[s])[:, split:].astype(BF) for s in range(slabs)]
-    projected = jnp.concatenate(projected, axis=1)
-    q_ref[...] = projected[:, :HD]
-    kv_ref[...] = projected[:, HD:]
-    co_ref[...] = jnp.concatenate(cotangent, axis=1)
+    qkv_ref[...] = jnp.concatenate([full[s][:, :split] for s in range(slabs)], axis=1)
+    proj_ref[...] = jnp.concatenate([full[s][:, split:] for s in range(slabs)], axis=1)
+    kv_ref[...] = dot(tokens[...], qkv_ref[:, HD:]).astype(BF)
+
+
+def query_kernel(tokens, grad_out, qkv_ref, proj_ref, q_ref, co_ref):
+    q_ref[...] = dot(tokens[...], qkv_ref[:, :HD]).astype(BF)
+    co_ref[...] = dot(grad_out[...], proj_ref[...]).astype(BF)
 
 
 def attention_kernel(
@@ -161,17 +163,8 @@
     dq_ref[...] = (grad_query * root).astype(BF)
 
 
-def mixed_kernel(split, att_ref, full, out_ref):
-    slabs = full.shape[0]
-    width = HD // slabs
-    attended = att_ref[...]
-    zeros = jnp.zeros((attended.shape[0], split), BF)
-    total = None
-    for s in range(slabs):
-        part = jnp.concatenate([zeros, attended[:, s * width : (s + 1) * width]], axis=1)
-        part = dot(part, full[s], ((1,), (1,)))
-        total = part if total is None else total + part
-    out_ref[...] = total.astype(BF)
+def mixed_kernel(att_ref, proj_ref, out_ref):
+    out_ref[...] = dot(att_ref[...], proj_ref[...], ((1,), (1,))).astype(BF)
 
 
 def weight_grads_kernel(
@@ -204,16 +197,8 @@
             target[block] = full[s, pl.ds(pl.multiple_of(w * size, size), size), :]
 
 
-def grad_tokens_kernel(split, rows_ref, full, out_ref):
-    slabs = full.shape[0]
-    rows = rows_ref[...]
-    zeros = jnp.zeros((rows.shape[0], HD // slabs), BF)
-    total = None
-    for s in range(slabs):
-        part = jnp.concatenate([rows[:, s * split : (s + 1) * split], zeros], axis=1)
-        part = dot(part, full[s], ((1,), (1,)))
-        total = part if total is None else total + part
-    out_ref[...] = total.astype(BF)
+def grad_tokens_kernel(rows_ref, qkv_ref, out_ref):
+    out_ref[...] = dot(rows_ref[...], qkv_ref[...], ((1,), (1,))).astype(BF)
 
 
 def unpack_kernel(split, keep, got, qkv_ref, proj_ref):
@@ -264,17 +249,25 @@
     for step in steps:
         held = jnp.concatenate([held, swap(held, step_pairs(step, slabs, weights))], axis=0)
     got = swap(held, core_pairs(slabs, weights))
-    query, key_value, cotangent, full = call(
-        functools.partial(project_kernel, steps, split),
-        [((count, HD), BF), ((count, 2 * HD), BF), ((count, HD), BF), ((slabs, features, lanes), BF)],
-        [index, held, got, tokens, grad_out],
+    key_value, full_qkv, full_proj = call(
+        functools.partial(key_value_kernel, steps, split),
+        [((count, 2 * HD), BF), ((features, 3 * HD), BF), ((features, HD), BF)],
+        [index, held, got, tokens],
+        scratch=[pltpu.VMEM((slabs, features, lanes), BF)],
         scalars=1,
     )
 
     weight_even, weight_odd = (weight_pairs(odd, slabs, weights) for odd in (0, 1))
     slab_even, slab_odd = (slab_pairs(odd, slabs, weights) for odd in (0, 1))
     even, odd = swap(key_value, weight_even), swap(key_value, weight_odd)
-    even, odd, turned = lax.optimization_barrier((even, odd, turned))
+    query, cotangent = call(
+        query_kernel,
+        [((count, HD), BF), ((count, HD), BF)],
+        [tokens, grad_out, full_qkv, full_proj],
+    )
+    even, odd, turned, query, cotangent = lax.optimization_barrier(
+        (even, odd, turned, query, cotangent)
+    )
     columns = jnp.stack([key_value, even, odd])
     across_even, across_odd = swap(columns, slab_even), swap(columns, slab_odd)
     pair = (3, count, 2 * HD)
@@ -287,9 +280,9 @@
     )
     parts_even, parts_odd = swap(parts_even, slab_even), swap(parts_odd, slab_odd)
     (mixed,) = call(
-        functools.partial(mixed_kernel, split),
+        mixed_kernel,
         [((count, features), BF)],
-        [attended, full],
+        [attended, full_proj],
         final=True,
     )
     parts_even, parts_odd, mixed = lax.optimization_barrier((parts_even, parts_odd, mixed))
@@ -319,9 +312,9 @@
         got = swap(send, step_pairs(step, slabs, weights))
         if step == steps[-1]:
             (grad_tokens,) = call(
-                functools.partial(grad_tokens_kernel, split),
+                grad_tokens_kernel,
                 [((count, features), BF)],
-                [grad_rows, full],
+                [grad_rows, full_qkv],
                 final=True,
             )
             got, grad_tokens = lax.optimization_barrier((got, grad_tokens))

time: 102 us -> 101 us (level)
  Pallas kernels: 14.1 us -> 12.4 us
    pallas_call x7 -> x8, Pallas kernels: 13 us -> 11.4 us  [call(): pl.pallas_call(kernel, out_shape=[make(shape, kind) for shape, kind in ou...]
where the time goes in v4:
time: 101 us
  starting transfers between devices  44.5 us (44%)
  waiting for transfers between devices  42.3 us (42%)
  Pallas kernels  12.4 us (12%)
    ppermute x18, starting transfers between devices, swap(): return lax.ppermute(values, AXES, pairs)  44.5 us
    ppermute x18, waiting for transfers between devices, swap(): return lax.ppermute(values, AXES, pairs)  42.3 us
    pallas_call x8, Pallas kernels, call(): pl.pallas_call(kernel, out_shape=[make(shape, kind) for shape, kind in ou...  11.4 us
  transfers between devices with their start and end apart: 18, of which 13 were waited for; matrix products, arithmetic and copies ran while one was open for 0% of the time, Pallas kernels for 4%

profile of v4, /device:TPU:0, one launch (start us, length us, event | category | flops | bytes accessed | tf_op | source)
XLA Modules:
  0.0 100.8 jit_solution(15694520613561482490)
XLA Ops:
  0.6 1.0 %shard_map.75 = bf16[1,192,128]{2,1,0:T(8,128)(2,1)S(1)} custom-call(bf16[192,96]{1,0:T(8,128)(2,1)} %qkv_hbm.1, bf16[32,192]{1,0:T(8,128)(2,1)} %proj_hbm.1), custom_call_target="tpu_custom_call" | custom-call | tf_op jit(solution)/shard_map/pallas_call | solution.py:236
  1.7 4.1 %collective-permute-start = (bf16[1,192,128]{2,1,0:T(8,128)(2,1)S(1)}, bf16[1,192,128]{2,1,0:T(8,128)(2,1)S(1)}, u32[]{:S(2)}, u32[]{:S(2)}) collective-permute-start(bf16[1,192,128]{2,1,0:T(8,128)(2,1)S(1)} %shard_map.75), channel_id=1, source_target_pairs={{0,4},{1,5},{2,6},{3,7},{4,0},{5,1},{6,2},{7,3},{8,12},{9,13},{10,... | collective-permute-start | bytes 147464 | tf_op jit(solution)/shard_map/ppermute | solution.py:234
  5.8 2.6 %collective-permute-done = bf16[1,192,128]{2,1,0:T(8,128)(2,1)S(1)} collective-permute-done((bf16[1,192,128]{2,1,0:T(8,128)(2,1)S(1)}, bf16[1,192,128]{2,1,0:T(8,128)(2,1)S(1)}, u32[]{:S(2)}, u32[]{:S(2)}) %collective-permute-start) | collective-permute-done | bytes 49184 | tf_op jit(solution)/shard_map/ppermute | solution.py:234
  8.4 1.8 %collective-permute-start.1 = (bf16[2,192,128]{2,1,0:T(8,128)(2,1)S(1)}, bf16[2,192,128]{2,1,0:T(8,128)(2,1)S(1)}, u32[]{:S(2)}, u32[]{:S(2)}) collective-permute-start(bf16[2,192,128]{2,1,0:T(8,128)(2,1)S(1)} %pad_maximum_fusion.3), channel_id=1, source_target_pairs={{0,16},{1,17},{2,18},{3,19},{4,20},{5,21},{6,22},{7,23},{8,9},{9,8... | collective-permute-start | bytes 294920 | tf_op jit(solution)/shard_map/ppermute | solution.py:234
  10.2 2.9 %collective-permute-done.1 = bf16[2,192,128]{2,1,0:T(8,128)(2,1)S(1)} collective-permute-done((bf16[2,192,128]{2,1,0:T(8,128)(2,1)S(1)}, bf16[2,192,128]{2,1,0:T(8,128)(2,1)S(1)}, u32[]{:S(2)}, u32[]{:S(2)}) %collective-permute-start.1) | collective-permute-done | bytes 98336 | tf_op jit(solution)/shard_map/ppermute | solution.py:234
  13.1 1.8 %collective-permute-start.2 = (bf16[4,192,128]{2,1,0:T(8,128)(2,1)S(1)}, bf16[4,192,128]{2,1,0:T(8,128)(2,1)S(1)}, u32[]{:S(2)}, u32[]{:S(2)}) collective-permute-start(bf16[4,192,128]{2,1,0:T(8,128)(2,1)S(1)} %pad_maximum_fusion.2), channel_id=1, source_target_pairs={{0,1},{1,0},{2,3},{3,2},{4,5},{5,4},{6,7},{7,6},{8,10},{9,11},{10,... | collective-permute-start | bytes 589832 | tf_op jit(solution)/shard_map/ppermute | solution.py:234
  14.9 3.9 %collective-permute-done.2 = bf16[4,192,128]{2,1,0:T(8,128)(2,1)S(1)} collective-permute-done((bf16[4,192,128]{2,1,0:T(8,128)(2,1)S(1)}, bf16[4,192,128]{2,1,0:T(8,128)(2,1)S(1)}, u32[]{:S(2)}, u32[]{:S(2)}) %collective-permute-start.2) | collective-permute-done | bytes 196640 | tf_op jit(solution)/shard_map/ppermute | solution.py:234
  18.9 1.4 %collective-permute-start.3 = (bf16[8,192,128]{2,1,0:T(8,128)(2,1)S(1)}, bf16[8,192,128]{2,1,0:T(8,128)(2,1)S(1)}, u32[]{:S(2)}, u32[]{:S(2)}) collective-permute-start(bf16[8,192,128]{2,1,0:T(8,128)(2,1)S(1)} %pad_maximum_fusion), channel_id=1, source_target_pairs={{0,2},{1,3},{2,0},{3,1},{4,6},{5,7},{6,4},{7,5},{8,24},{9,25},{10,... | collective-permute-start | bytes 1179656 | tf_op jit(solution)/shard_map/ppermute | solution.py:234
  20.4 6.3 %collective-permute-done.3 = bf16[8,192,128]{2,1,0:T(8,128)(2,1)S(1)} collective-permute-done((bf16[8,192,128]{2,1,0:T(8,128)(2,1)S(1)}, bf16[8,192,128]{2,1,0:T(8,128)(2,1)S(1)}, u32[]{:S(2)}, u32[]{:S(2)}) %collective-permute-start.3) | collective-permute-done | bytes 393248 | tf_op jit(solution)/shard_map/ppermute | solution.py:234
  27.0 2.2 %collective-permute-done.4.got = bf16[16,192,128]{2,1,0:T(8,128)(2,1)S(1)} collective-permute-done((bf16[16,192,128]{2,1,0:T(8,128)(2,1)S(1)}, bf16[16,192,128]{2,1,0:T(8,128)(2,1)S(1)}, u32[]{:S(2)}, u32[]{:S(2)}) %collective-permute-start.4) | collective-permute-done | bytes 786464 | tf_op jit(solution)/shard_map/ppermute | solution.py:234
  29.2 1.4 %shard_map.76 = (bf16[256,256]{1,0:T(8,128)(2,1)S(1)}, bf16[1536,384]{1,0:T(8,128)(2,1)S(1)}, bf16[1536,128]{1,0:T(8,128)(2,1)S(1)}) custom-call(s32[2]{0:T(128)S(1)} %pad_add_fusion.index, bf16[16,192,128]{2,1,0:T(8,128)(2,1)S(1)} %constant_dynamic-update-slice_fusion.own, bf16[16,192,128]{2,1,0:T(8,128)(2,1)S(1)} %collective-permute-done.4.got, ...), custom_call_target="tpu_custom_call" | custom-call | tf_op jit(solution)/shard_map/pallas_call | solution.py:216
  31.2 4.1 %collective-permute-start.5 = (bf16[256,256]{1,0:T(8,128)(2,1)S(1)}, bf16[256,256]{1,0:T(8,128)(2,1)S(1)}, u32[]{:S(2)}, u32[]{:S(2)}) collective-permute-start(bf16[256,256]{1,0:T(8,128)(2,1)S(1)} %get-tuple-element.29.own), channel_id=1, source_target_pairs={{0,1},{1,0},{2,3},{3,2},{4,5},{5,4},{6,7},{7,6},{8,9},{9,8},{10,11... | collective-permute-start | bytes 393224 | tf_op jit(solution)/shard_map/ppermute | solution.py:234
  36.4 4.5 %collective-permute-done.5.even = bf16[256,256]{1,0:T(8,128)(2,1)S(1)} collective-permute-done((bf16[256,256]{1,0:T(8,128)(2,1)S(1)}, bf16[256,256]{1,0:T(8,128)(2,1)S(1)}, u32[]{:S(2)}, u32[]{:S(2)}) %collective-permute-start.5) | collective-permute-done | bytes 131104 | tf_op jit(solution)/shard_map/ppermute | solution.py:234
  41.7 2.9 %collective-permute-start.7 = (bf16[3,256,256]{2,1,0:T(8,128)(2,1)S(1)}, bf16[3,256,256]{2,1,0:T(8,128)(2,1)S(1)}, u32[]{:S(2)}, u32[]{:S(2)}) collective-permute-start(bf16[3,256,256]{2,1,0:T(8,128)(2,1)S(1)} %pad_maximum_fusion.1), channel_id=1, source_target_pairs={{0,8},{1,9},{2,10},{3,11},{4,12},{5,13},{6,14},{7,15},{8,0},{9,1},... | collective-permute-start | bytes 1179656 | tf_op jit(solution)/shard_map/ppermute | solution.py:234
  44.6 1.3 %collective-permute-done.7.slab_even = bf16[3,256,256]{2,1,0:T(8,128)(2,1)S(1)} collective-permute-done((bf16[3,256,256]{2,1,0:T(8,128)(2,1)S(1)}, bf16[3,256,256]{2,1,0:T(8,128)(2,1)S(1)}, u32[]{:S(2)}, u32[]{:S(2)}) %collective-permute-start.7) | collective-permute-done | bytes 393248 | tf_op jit(solution)/shard_map/ppermute | solution.py:234
  45.9 3.7 %shard_map.79 = (bf16[256,128]{1,0:T(8,128)(2,1)S(1)}, bf16[256,128]{1,0:T(8,128)(2,1)S(1)}, bf16[3,256,256]{2,1,0:T(8,128)(2,1)S(1)}, bf16[3,256,256]{2,1,0:T(8,128)(2,1)S(1)}, bf16[3,256,256]{2,1,0:T(8,128)(2,1)S(1)}) custom-call(s32[2]{0:T(128)S(1)} %pad_add_fusion.index, bf16[256,128]{1,0:T(8,128)(2,1)S(1)} %get-tuple-element.34.q_ref, ...), custom_call_target="tpu_custom_call" | custom-call | tf_op jit(solution)/shard_map/pallas_call | solution.py:216
  49.6 4.2 %collective-permute-start.9 = (bf16[3,256,256]{2,1,0:T(8,128)(2,1)S(1)}, bf16[3,256,256]{2,1,0:T(8,128)(2,1)S(1)}, u32[]{:S(2)}, u32[]{:S(2)}) collective-permute-start(bf16[3,256,256]{2,1,0:T(8,128)(2,1)S(1)} %get-tuple-element.38), channel_id=1, source_target_pairs={{0,8},{1,9},{2,10},{3,11},{4,12},{5,13},{6,14},{7,15},{8,0},{9,1},... | collective-permute-start | bytes 1179656 | tf_op jit(solution)/shard_map/ppermute | solution.py:234
  54.5 1.2 %shard_map.80 = bf16[256,1536]{1,0:T(8,128)(2,1)} custom-call(bf16[256,128]{1,0:T(8,128)(2,1)S(1)} %get-tuple-element.40.att_ref, bf16[1536,128]{1,0:T(8,128)(2,1)S(1)} %get-tuple-element.31.proj_ref), custom_call_target="tpu_custom_call" | custom-call | tf_op jit(solution)/shard_map/pallas_call | solution.py:216
  56.6 4.9 %collective-permute-start.11 = (bf16[256,256]{1,0:T(8,128)(2,1)S(1)}, bf16[256,256]{1,0:T(8,128)(2,1)S(1)}, u32[]{:S(2)}, u32[]{:S(2)}) collective-permute-start(bf16[256,256]{1,0:T(8,128)(2,1)S(1)} %get-tuple-element.59), channel_id=1, source_target_pairs={{0,1},{1,0},{2,3},{3,2},{4,5},{5,4},{6,7},{7,6},{8,9},{9,8},{10,11... | collective-permute-start | bytes 393224 | tf_op jit(solution)/shard_map/ppermute | solution.py:234
  61.5 3.6 %collective-permute-done.11.even = bf16[256,256]{1,0:T(8,128)(2,1)S(1)} collective-permute-done((bf16[256,256]{1,0:T(8,128)(2,1)S(1)}, bf16[256,256]{1,0:T(8,128)(2,1)S(1)}, u32[]{:S(2)}, u32[]{:S(2)}) %collective-permute-start.11) | collective-permute-done | bytes 131104 | tf_op jit(solution)/shard_map/ppermute | solution.py:234
  65.1 1.8 %shard_map.81 = (bf16[256,384]{1,0:T(8,128)(2,1)S(1)}, bf16[16,192,128]{2,1,0:T(8,128)(2,1)S(1)}, bf16[16,192,128]{2,1,0:T(8,128)(2,1)S(1)}) custom-call(s32[2]{0:T(128)S(1)} %pad_add_fusion.index, bf16[1536,512]{1,0:T(8,128)(2,1)S(1)} %shard_map.77.turned, bf16[256,128]{1,0:T(8,128)(2,1)S(1)} %get-tuple-element.43.dq, ...), custom_call_target="tpu_custom_call" | custom-call | tf_op jit(solution)/shard_map/pallas_call | solution.py:216
  66.9 6.7 %collective-permute-start.13 = (bf16[16,192,128]{2,1,0:T(8,128)(2,1)S(1)}, bf16[16,192,128]{2,1,0:T(8,128)(2,1)S(1)}, u32[]{:S(2)}, u32[]{:S(2)}) collective-permute-start(bf16[16,192,128]{2,1,0:T(8,128)(2,1)S(1)} %get-tuple-element.48), channel_id=1, source_target_pairs={{0,8},{1,9},{2,10},{3,11},{4,12},{5,13},{6,14},{7,15},{8,0},{9,1},... | collective-permute-start | bytes 2359304 | tf_op jit(solution)/shard_map/ppermute | solution.py:234
  73.6 1.9 %collective-permute-done.13 = bf16[16,192,128]{2,1,0:T(8,128)(2,1)S(1)} collective-permute-done((bf16[16,192,128]{2,1,0:T(8,128)(2,1)S(1)}, bf16[16,192,128]{2,1,0:T(8,128)(2,1)S(1)}, u32[]{:S(2)}, u32[]{:S(2)}) %collective-permute-start.13) | collective-permute-done | bytes 786464 | tf_op jit(solution)/shard_map/ppermute | solution.py:234
  75.7 1.9 %collective-permute-start.14 = (bf16[8,192,128]{2,1,0:T(8,128)(2,1)S(1)}, bf16[8,192,128]{2,1,0:T(8,128)(2,1)S(1)}, u32[]{:S(2)}, u32[]{:S(2)}) collective-permute-start(bf16[8,192,128]{2,1,0:T(8,128)(2,1)S(1)} %get-tuple-element.55), channel_id=1, source_target_pairs={{0,2},{1,3},{2,0},{3,1},{4,6},{5,7},{6,4},{7,5},{8,24},{9,25},{10,... | collective-permute-start | bytes 1179656 | tf_op jit(solution)/shard_map/ppermute | solution.py:234
  77.6 1.5 %shard_map.82 = bf16[256,1536]{1,0:T(8,128)(2,1)} custom-call(bf16[256,384]{1,0:T(8,128)(2,1)S(1)} %get-tuple-element.49.rows_ref, bf16[1536,384]{1,0:T(8,128)(2,1)S(1)} %get-tuple-element.30.qkv_ref), custom_call_target="tpu_custom_call" | custom-call | tf_op jit(solution)/shard_map/pallas_call | solution.py:216
  79.1 4.5 %collective-permute-done.14 = bf16[8,192,128]{2,1,0:T(8,128)(2,1)S(1)} collective-permute-done((bf16[8,192,128]{2,1,0:T(8,128)(2,1)S(1)}, bf16[8,192,128]{2,1,0:T(8,128)(2,1)S(1)}, u32[]{:S(2)}, u32[]{:S(2)}) %collective-permute-start.14) | collective-permute-done | bytes 393248 | tf_op jit(solution)/shard_map/ppermute | solution.py:234
  83.6 2.2 %collective-permute-start.15 = (bf16[4,192,128]{2,1,0:T(8,128)(2,1)S(1)}, bf16[4,192,128]{2,1,0:T(8,128)(2,1)S(1)}, u32[]{:S(2)}, u32[]{:S(2)}) collective-permute-start(bf16[4,192,128]{2,1,0:T(8,128)(2,1)S(1)} %get-tuple-element.56), channel_id=1, source_target_pairs={{0,1},{1,0},{2,3},{3,2},{4,5},{5,4},{6,7},{7,6},{8,10},{9,11},{10,... | collective-permute-start | bytes 589832 | tf_op jit(solution)/shard_map/ppermute | solution.py:234
  85.9 3.6 %collective-permute-done.15 = bf16[4,192,128]{2,1,0:T(8,128)(2,1)S(1)} collective-permute-done((bf16[4,192,128]{2,1,0:T(8,128)(2,1)S(1)}, bf16[4,192,128]{2,1,0:T(8,128)(2,1)S(1)}, u32[]{:S(2)}, u32[]{:S(2)}) %collective-permute-start.15) | collective-permute-done | bytes 196640 | tf_op jit(solution)/shard_map/ppermute | solution.py:234
  89.6 2.8 %collective-permute-start.16 = (bf16[2,192,128]{2,1,0:T(8,128)(2,1)S(1)}, bf16[2,192,128]{2,1,0:T(8,128)(2,1)S(1)}, u32[]{:S(2)}, u32[]{:S(2)}) collective-permute-start(bf16[2,192,128]{2,1,0:T(8,128)(2,1)S(1)} %get-tuple-element.61), channel_id=1, source_target_pairs={{0,16},{1,17},{2,18},{3,19},{4,20},{5,21},{6,22},{7,23},{8,9},{9,8... | collective-permute-start | bytes 294920 | tf_op jit(solution)/shard_map/ppermute | solution.py:234
  92.3 2.6 %collective-permute-done.16 = bf16[2,192,128]{2,1,0:T(8,128)(2,1)S(1)} collective-permute-done((bf16[2,192,128]{2,1,0:T(8,128)(2,1)S(1)}, bf16[2,192,128]{2,1,0:T(8,128)(2,1)S(1)}, u32[]{:S(2)}, u32[]{:S(2)}) %collective-permute-start.16) | collective-permute-done | bytes 98336 | tf_op jit(solution)/shard_map/ppermute | solution.py:234
  95.0 2.8 %collective-permute-start.17 = (bf16[1,192,128]{2,1,0:T(8,128)(2,1)S(1)}, bf16[1,192,128]{2,1,0:T(8,128)(2,1)S(1)}, u32[]{:S(2)}, u32[]{:S(2)}) collective-permute-start(bf16[1,192,128]{2,1,0:T(8,128)(2,1)S(1)} %get-tuple-element.63), channel_id=1, source_target_pairs={{0,4},{1,5},{2,6},{3,7},{4,0},{5,1},{6,2},{7,3},{8,12},{9,13},{10,... | collective-permute-start | bytes 147464 | tf_op jit(solution)/shard_map/ppermute | solution.py:234
  97.8 2.3 %collective-permute-done.17.got = bf16[1,192,128]{2,1,0:T(8,128)(2,1)S(1)} collective-permute-done((bf16[1,192,128]{2,1,0:T(8,128)(2,1)S(1)}, bf16[1,192,128]{2,1,0:T(8,128)(2,1)S(1)}, u32[]{:S(2)}, u32[]{:S(2)}) %collective-permute-start.17) | collective-permute-done | bytes 49184 | tf_op jit(solution)/shard_map/ppermute | solution.py:234
  (32 shorter events, 5.4 us)
Async XLA Ops:
  0.6 28.5 %copy-start = (bf16[256,1536]{1,0:T(8,128)(2,1)S(1)}, bf16[256,1536]{1,0:T(8,128)(2,1)}, u32[]{:S(2)}) copy-start(bf16[256,1536]{1,0:T(8,128)(2,1)} %tokens.5) | copy-start | bytes 2359300
  1.7 6.7 %collective-permute-start = (bf16[1,192,128]{2,1,0:T(8,128)(2,1)S(1)}, bf16[1,192,128]{2,1,0:T(8,128)(2,1)S(1)}, u32[]{:S(2)}, u32[]{:S(2)}) collective-permute-start(bf16[1,192,128]{2,1,0:T(8,128)(2,1)S(1)} %shard_map.75), channel_id=1, source_target_pairs={{0,4},{1,5},{2,6},{3,7},{4,0},{5,1},{6,2},{7,3},{8,12},{9,13},{10,... | collective-permute-start | bytes 147464 | tf_op jit(solution)/shard_map/ppermute | solution.py:234
  8.4 4.7 %collective-permute-start.1 = (bf16[2,192,128]{2,1,0:T(8,128)(2,1)S(1)}, bf16[2,192,128]{2,1,0:T(8,128)(2,1)S(1)}, u32[]{:S(2)}, u32[]{:S(2)}) collective-permute-start(bf16[2,192,128]{2,1,0:T(8,128)(2,1)S(1)} %pad_maximum_fusion.3), channel_id=1, source_target_pairs={{0,16},{1,17},{2,18},{3,19},{4,20},{5,21},{6,22},{7,23},{8,9},{9,8... | collective-permute-start | bytes 294920 | tf_op jit(solution)/shard_map/ppermute | solution.py:234
  13.1 5.7 %collective-permute-start.2 = (bf16[4,192,128]{2,1,0:T(8,128)(2,1)S(1)}, bf16[4,192,128]{2,1,0:T(8,128)(2,1)S(1)}, u32[]{:S(2)}, u32[]{:S(2)}) collective-permute-start(bf16[4,192,128]{2,1,0:T(8,128)(2,1)S(1)} %pad_maximum_fusion.2), channel_id=1, source_target_pairs={{0,1},{1,0},{2,3},{3,2},{4,5},{5,4},{6,7},{7,6},{8,10},{9,11},{10,... | collective-permute-start | bytes 589832 | tf_op jit(solution)/shard_map/ppermute | solution.py:234
  18.9 7.8 %collective-permute-start.3 = (bf16[8,192,128]{2,1,0:T(8,128)(2,1)S(1)}, bf16[8,192,128]{2,1,0:T(8,128)(2,1)S(1)}, u32[]{:S(2)}, u32[]{:S(2)}) collective-permute-start(bf16[8,192,128]{2,1,0:T(8,128)(2,1)S(1)} %pad_maximum_fusion), channel_id=1, source_target_pairs={{0,2},{1,3},{2,0},{3,1},{4,6},{5,7},{6,4},{7,5},{8,24},{9,25},{10,... | collective-permute-start | bytes 1179656 | tf_op jit(solution)/shard_map/ppermute | solution.py:234
  20.4 14.9 %copy-start.1 = (bf16[256,1536]{1,0:T(8,128)(2,1)S(1)}, bf16[256,1536]{1,0:T(8,128)(2,1)}, u32[]{:S(2)}) copy-start(bf16[256,1536]{1,0:T(8,128)(2,1)} %grad_out.3) | copy-start | bytes 2359300
  26.8 2.4 %collective-permute-start.4 = (bf16[16,192,128]{2,1,0:T(8,128)(2,1)S(1)}, bf16[16,192,128]{2,1,0:T(8,128)(2,1)S(1)}, u32[]{:S(2)}, u32[]{:S(2)}) collective-permute-start(bf16[16,192,128]{2,1,0:T(8,128)(2,1)S(1)} %constant_dynamic-update-slice_fusion.own), channel_id=1, source_target_pairs={{0,8},{1,9},{2,10},{3,11},{4,12},{5,13},{6,14},{7,15},{8,0},{9,1},... | collective-permute-start | bytes 2359304 | tf_op jit(solution)/shard_map/ppermute | solution.py:234
  30.5 5.9 %collective-permute-start.6 = (bf16[256,256]{1,0:T(8,128)(2,1)S(1)}, bf16[256,256]{1,0:T(8,128)(2,1)S(1)}, u32[]{:S(2)}, u32[]{:S(2)}) collective-permute-start(bf16[256,256]{1,0:T(8,128)(2,1)S(1)} %get-tuple-element.29.own), channel_id=1, source_target_pairs={{1,2},{2,1},{3,4},{4,3},{5,6},{6,5},{9,10},{10,9},{11,12},{12,11},... | collective-permute-start | bytes 393224 | tf_op jit(solution)/shard_map/ppermute | solution.py:234
  31.2 9.7 %collective-permute-start.5 = (bf16[256,256]{1,0:T(8,128)(2,1)S(1)}, bf16[256,256]{1,0:T(8,128)(2,1)S(1)}, u32[]{:S(2)}, u32[]{:S(2)}) collective-permute-start(bf16[256,256]{1,0:T(8,128)(2,1)S(1)} %get-tuple-element.29.own), channel_id=1, source_target_pairs={{0,1},{1,0},{2,3},{3,2},{4,5},{5,4},{6,7},{7,6},{8,9},{9,8},{10,11... | collective-permute-start | bytes 393224 | tf_op jit(solution)/shard_map/ppermute | solution.py:234
  41.0 3.6 %collective-permute-start.8 = (bf16[3,256,256]{2,1,0:T(8,128)(2,1)S(1)}, bf16[3,256,256]{2,1,0:T(8,128)(2,1)S(1)}, u32[]{:S(2)}, u32[]{:S(2)}) collective-permute-start(bf16[3,256,256]{2,1,0:T(8,128)(2,1)S(1)} %pad_maximum_fusion.1), channel_id=1, source_target_pairs={{8,16},{9,17},{10,18},{11,19},{12,20},{13,21},{14,22},{15,23},{16,... | collective-permute-start | bytes 1179656 | tf_op jit(solution)/shard_map/ppermute | solution.py:234
  41.7 4.2 %collective-permute-start.7 = (bf16[3,256,256]{2,1,0:T(8,128)(2,1)S(1)}, bf16[3,256,256]{2,1,0:T(8,128)(2,1)S(1)}, u32[]{:S(2)}, u32[]{:S(2)}) collective-permute-start(bf16[3,256,256]{2,1,0:T(8,128)(2,1)S(1)} %pad_maximum_fusion.1), channel_id=1, source_target_pairs={{0,8},{1,9},{2,10},{3,11},{4,12},{5,13},{6,14},{7,15},{8,0},{9,1},... | collective-permute-start | bytes 1179656 | tf_op jit(solution)/shard_map/ppermute | solution.py:234
  49.6 6.2 %collective-permute-start.9 = (bf16[3,256,256]{2,1,0:T(8,128)(2,1)S(1)}, bf16[3,256,256]{2,1,0:T(8,128)(2,1)S(1)}, u32[]{:S(2)}, u32[]{:S(2)}) collective-permute-start(bf16[3,256,256]{2,1,0:T(8,128)(2,1)S(1)} %get-tuple-element.38), channel_id=1, source_target_pairs={{0,8},{1,9},{2,10},{3,11},{4,12},{5,13},{6,14},{7,15},{8,0},{9,1},... | collective-permute-start | bytes 1179656 | tf_op jit(solution)/shard_map/ppermute | solution.py:234
  53.8 1.9 %collective-permute-start.10 = (bf16[3,256,256]{2,1,0:T(8,128)(2,1)S(1)}, bf16[3,256,256]{2,1,0:T(8,128)(2,1)S(1)}, u32[]{:S(2)}, u32[]{:S(2)}) collective-permute-start(bf16[3,256,256]{2,1,0:T(8,128)(2,1)S(1)} %get-tuple-element.39), channel_id=1, source_target_pairs={{8,16},{9,17},{10,18},{11,19},{12,20},{13,21},{14,22},{15,23},{16,... | collective-permute-start | bytes 1179656 | tf_op jit(solution)/shard_map/ppermute | solution.py:234
  55.9 5.6 %collective-permute-start.12 = (bf16[256,256]{1,0:T(8,128)(2,1)S(1)}, bf16[256,256]{1,0:T(8,128)(2,1)S(1)}, u32[]{:S(2)}, u32[]{:S(2)}) collective-permute-start(bf16[256,256]{1,0:T(8,128)(2,1)S(1)} %get-tuple-element.58), channel_id=1, source_target_pairs={{1,2},{2,1},{3,4},{4,3},{5,6},{6,5},{9,10},{10,9},{11,12},{12,11},... | collective-permute-start | bytes 393224 | tf_op jit(solution)/shard_map/ppermute | solution.py:234
  56.6 8.5 %collective-permute-start.11 = (bf16[256,256]{1,0:T(8,128)(2,1)S(1)}, bf16[256,256]{1,0:T(8,128)(2,1)S(1)}, u32[]{:S(2)}, u32[]{:S(2)}) collective-permute-start(bf16[256,256]{1,0:T(8,128)(2,1)S(1)} %get-tuple-element.59), channel_id=1, source_target_pairs={{0,1},{1,0},{2,3},{3,2},{4,5},{5,4},{6,7},{7,6},{8,9},{9,8},{10,11... | collective-permute-start | bytes 393224 | tf_op jit(solution)/shard_map/ppermute | solution.py:234
  66.9 8.6 %collective-permute-start.13 = (bf16[16,192,128]{2,1,0:T(8,128)(2,1)S(1)}, bf16[16,192,128]{2,1,0:T(8,128)(2,1)S(1)}, u32[]{:S(2)}, u32[]{:S(2)}) collective-permute-start(bf16[16,192,128]{2,1,0:T(8,128)(2,1)S(1)} %get-tuple-element.48), channel_id=1, source_target_pairs={{0,8},{1,9},{2,10},{3,11},{4,12},{5,13},{6,14},{7,15},{8,0},{9,1},... | collective-permute-start | bytes 2359304 | tf_op jit(solution)/shard_map/ppermute | solution.py:234
  75.7 7.8 %collective-permute-start.14 = (bf16[8,192,128]{2,1,0:T(8,128)(2,1)S(1)}, bf16[8,192,128]{2,1,0:T(8,128)(2,1)S(1)}, u32[]{:S(2)}, u32[]{:S(2)}) collective-permute-start(bf16[8,192,128]{2,1,0:T(8,128)(2,1)S(1)} %get-tuple-element.55), channel_id=1, source_target_pairs={{0,2},{1,3},{2,0},{3,1},{4,6},{5,7},{6,4},{7,5},{8,24},{9,25},{10,... | collective-permute-start | bytes 1179656 | tf_op jit(solution)/shard_map/ppermute | solution.py:234
  83.6 5.9 %collective-permute-start.15 = (bf16[4,192,128]{2,1,0:T(8,128)(2,1)S(1)}, bf16[4,192,128]{2,1,0:T(8,128)(2,1)S(1)}, u32[]{:S(2)}, u32[]{:S(2)}) collective-permute-start(bf16[4,192,128]{2,1,0:T(8,128)(2,1)S(1)} %get-tuple-element.56), channel_id=1, source_target_pairs={{0,1},{1,0},{2,3},{3,2},{4,5},{5,4},{6,7},{7,6},{8,10},{9,11},{10,... | collective-permute-start | bytes 589832 | tf_op jit(solution)/shard_map/ppermute | solution.py:234
  89.6 5.4 %collective-permute-start.16 = (bf16[2,192,128]{2,1,0:T(8,128)(2,1)S(1)}, bf16[2,192,128]{2,1,0:T(8,128)(2,1)S(1)}, u32[]{:S(2)}, u32[]{:S(2)}) collective-permute-start(bf16[2,192,128]{2,1,0:T(8,128)(2,1)S(1)} %get-tuple-element.61), channel_id=1, source_target_pairs={{0,16},{1,17},{2,18},{3,19},{4,20},{5,21},{6,22},{7,23},{8,9},{9,8... | collective-permute-start | bytes 294920 | tf_op jit(solution)/shard_map/ppermute | solution.py:234
  95.0 5.1 %collective-permute-start.17 = (bf16[1,192,128]{2,1,0:T(8,128)(2,1)S(1)}, bf16[1,192,128]{2,1,0:T(8,128)(2,1)S(1)}, u32[]{:S(2)}, u32[]{:S(2)}) collective-permute-start(bf16[1,192,128]{2,1,0:T(8,128)(2,1)S(1)} %get-tuple-element.63), channel_id=1, source_target_pairs={{0,4},{1,5},{2,6},{3,7},{4,0},{5,1},{6,2},{7,3},{8,12},{9,13},{10,... | collective-permute-start | bytes 147464 | tf_op jit(solution)/shard_map/ppermute | solution.py:234

commit v5 on v4

--- a/solution.py
+++ b/solution.py
@@ -110,70 +110,109 @@
     co_ref[...] = dot(grad_out[...], proj_ref[...]).astype(BF)
 
 
+def block_grads(refs, delta, scale, scores, halves, blocks, outs, total):
+    query, cotangent = (ref[...] for ref in refs)
+    turned_query = query.T
+    turned_cotangent = (cotangent.astype(F32) * scale).astype(BF).T
+    for j, (block, out) in enumerate(zip(blocks, outs)):
+        grad = dot(cotangent, block[:, HD:], ((1,), (1,)))
+        grad = (scores[j] * ((grad - delta) * scale)).astype(BF)
+        step = dot(grad, block[:, :HD])
+        total = step if total is None else total + step
+        out[:HD, :] = (dot(turned_query, grad) * HD ** (-0.5)).astype(BF)
+        out[HD:, :] = dot(turned_cotangent, halves[j]).astype(BF)
+    return total
+
+
 def attention_kernel(
-    sizes, index, q_ref, co_ref, own, even, odd, slab_even, slab_odd,
-    att_ref, dq_ref, parts_own, parts_even, parts_odd, scores, halves,
+    sizes, index, q_ref, co_ref, own, even, odd, side_even, side_odd, far_even, far_odd,
+    att_ref, delta_ref, scale_ref, dq_ref, parts_even, parts_odd, near_scores, near_halves,
+    side_scores, side_halves, scores, halves,
 ):
     slab, weight = index[0], index[1]
     slabs, weights = sizes
-    root = HD ** (-0.5)
-    binary = root * math.log2(math.e)
+    binary = HD ** (-0.5) * math.log2(math.e)
     slab_inside = (slab > 0) & (slab < slabs - 1)
     weight_inside = (weight > 0) & (weight < weights - 1)
-    blocks = [own, even, odd]
-    blocks += [slab_even.at[i] for i in range(3)] + [slab_odd.at[i] for i in range(3)]
-    outs = [parts.at[i] for parts in (parts_own, parts_even, parts_odd) for i in range(3)]
-    query, cotangent = q_ref[...], co_ref[...]
+    far = [far_even.at[0], far_even.at[1], far_odd.at[0], far_odd.at[1]]
+    blocks = far + [own, even, odd, side_even, side_odd]
+    inside = [None, weight_inside, slab_inside, slab_inside & weight_inside]
+    inside += [None, None, weight_inside, None, slab_inside]
+    groups = ((scores, halves, 4), (near_scores, near_halves, 3), (side_scores, side_halves, 2))
+    kept = [ref.at[i] for ref, _, size in groups for i in range(size)]
+    kept_halves = [ref.at[i] for _, ref, size in groups for i in range(size)]
+    query = q_ref[...]
     highest = None
-    for j, block in enumerate(blocks):
+    for block, present, place in zip(blocks, inside, kept):
         part = dot(query, block[:, :HD], ((1,), (1,)))
-        present = None
-        if j % 3 == 2:
-            present = weight_inside
-        if j >= 6:
-            present = slab_inside if present is None else present & slab_inside
         if present is not None:
             part = part + jnp.where(present, 0.0, -jnp.inf)
-        scores[j] = part
+        place[...] = part
         highest = part if highest is None else jnp.maximum(highest, part)
     highest = jnp.max(highest, axis=1, keepdims=True) * binary
     total, attended = None, None
-    for j, block in enumerate(blocks):
-        part = jnp.exp2(scores[j] * binary - highest)
+    for block, place, half_place in zip(blocks, kept, kept_halves):
+        part = jnp.exp2(place[...] * binary - highest)
         total = part if total is None else total + part
         half = part.astype(BF)
-        scores[j] = part
-        halves[j] = half
+        place[...] = part
+        half_place[...] = half
         weighted = dot(half, block[:, HD:])
         attended = weighted if attended is None else attended + weighted
     scale = 1.0 / jnp.sum(total, axis=1, keepdims=True)
     attended = (attended * scale).astype(BF)
     att_ref[...] = attended
-    delta = jnp.sum(cotangent.astype(F32) * attended.astype(F32), axis=1, keepdims=True)
-    turned_query = query.T
-    turned_cotangent = (cotangent.astype(F32) * scale).astype(BF).T
-    grad_query = None
-    for j, (block, out) in enumerate(zip(blocks, outs)):
-        grad = dot(cotangent, block[:, HD:], ((1,), (1,)))
-        grad = (scores[j] * ((grad - delta) * scale)).astype(BF)
-        step = dot(grad, block[:, :HD])
-        grad_query = step if grad_query is None else grad_query + step
-        out[:HD, :] = (dot(turned_query, grad) * root).astype(BF)
-        out[HD:, :] = dot(turned_cotangent, halves[j]).astype(BF)
-    dq_ref[...] = (grad_query * root).astype(BF)
+    cotangent = co_ref[...].astype(F32)
+    delta = jnp.sum(cotangent * attended.astype(F32), axis=1, keepdims=True)
+    delta_ref[...] = delta
+    scale_ref[...] = scale
+    outs = [parts_even.at[0], parts_even.at[1], parts_odd.at[0], parts_odd.at[1]]
+    dq_ref[...] = block_grads((q_ref, co_ref), delta, scale, scores, halves, far, outs, None)
+
+
+def near_grads_kernel(
+    q_ref, co_ref, own, even, odd, delta, scale, dq_part, scores, halves, dq_ref, parts,
+):
+    outs = [parts.at[i] for i in range(3)]
+    dq_ref[...] = block_grads(
+        (q_ref, co_ref), delta[...], scale[...], scores, halves, [own, even, odd], outs, dq_part[...]
+    )
+
+
+def side_grads_kernel(
+    q_ref, co_ref, even, odd, delta, scale, dq_part, scores, halves, dq_ref, part_even, part_odd,
+):
+    outs = [part_even, part_odd]
+    total = block_grads(
+        (q_ref, co_ref), delta[...], scale[...], scores, halves, [even, odd], outs, dq_part[...]
+    )
+    dq_ref[...] = (total * HD ** (-0.5)).astype(BF)
 
 
 def mixed_kernel(att_ref, proj_ref, out_ref):
     out_ref[...] = dot(att_ref[...], proj_ref[...], ((1,), (1,))).astype(BF)
 
 
-def weight_grads_kernel(
-    steps, slabs, split, index, turned, dq, own, even, odd, att_ref,
-    rows_ref, keep, send, full,
+def half_grads(steps, index, away, turned, factors, target, full):
+    slab, weight = index[0], index[1]
+    lanes = target.shape[2]
+    grads = dot(turned[...], factors[...])
+    for i in range(full.shape[0]):
+        full[i] = grads[:, i * lanes : (i + 1) * lanes].astype(BF)
+    size = target.shape[1]
+    parity = slab & 1
+    parity = 1 - parity if away else parity
+    for block in range(target.shape[0]):
+        s, w = block_owner(block, steps, slab ^ away, weight, parity)
+        target[block] = full[s >> 1, pl.ds(pl.multiple_of(w * size, size), size), :]
+
+
+def away_grads_kernel(
+    steps, slabs, split, index, turned, even, odd, dq, own, side_even, side_odd, att_ref,
+    rows_ref, kept, send, sent, full,
 ):
-    slab, weight = index[0], index[1]
-    parity = slab & 1
-    pairs = own[...] + even[...].astype(F32) + odd[...].astype(F32)
+    pairs = own[0].astype(F32) + side_even[...].astype(F32) + side_odd[...].astype(F32)
+    pairs = pairs + even[...].astype(F32) + odd[...].astype(F32)
     rows = jnp.concatenate([dq[...], pairs.astype(BF).T], axis=1)
     rows_ref[...] = rows
     attended = att_ref[...]
@@ -181,20 +220,29 @@
     count = rows.shape[0]
     left_zeros = jnp.zeros((count, width), BF)
     right_zeros = jnp.zeros((count, split), BF)
-    left, right = [], []
-    for s in range(slabs):
-        left += [rows[:, s * split : (s + 1) * split], left_zeros]
-        right += [right_zeros, attended[:, s * width : (s + 1) * width]]
-    left, right = jnp.concatenate(left, axis=1), jnp.concatenate(right, axis=1)
-    grads = dot(turned[...], jnp.concatenate([left, right], axis=0))
-    lanes = split + width
-    for s in range(slabs):
-        full[s] = grads[:, s * lanes : (s + 1) * lanes].astype(BF)
-    size = keep.shape[1]
-    for target, where, odd_core in ((send, slab ^ 1, 1 - parity), (keep, slab, parity)):
-        for block in range(keep.shape[0]):
-            s, w = block_owner(block, steps, where, weight, odd_core)
-            target[block] = full[s, pl.ds(pl.multiple_of(w * size, size), size), :]
+    halves = []
+    for first in range(2):
+        left, right = [], []
+        for s in range(first, slabs, 2):
+            left += [rows[:, s * split : (s + 1) * split], left_zeros]
+            right += [right_zeros, attended[:, s * width : (s + 1) * width]]
+        left, right = jnp.concatenate(left, axis=1), jnp.concatenate(right, axis=1)
+        halves.append(jnp.concatenate([left, right], axis=0))
+    parity = index[0] & 1
+
+    @pl.when(parity == 0)
+    def _():
+        kept[...], sent[...] = halves[0], halves[1]
+
+    @pl.when(parity == 1)
+    def _():
+        kept[...], sent[...] = halves[1], halves[0]
+
+    half_grads(steps, index, 1, turned, sent, send, full)
+
+
+def kept_grads_kernel(steps, index, turned, kept, keep, full):
+    half_grads(steps, index, 0, turned, kept, keep, full)
 
 
 def grad_tokens_kernel(rows_ref, qkv_ref, out_ref):
@@ -259,52 +307,87 @@
 
     weight_even, weight_odd = (weight_pairs(odd, slabs, weights) for odd in (0, 1))
     slab_even, slab_odd = (slab_pairs(odd, slabs, weights) for odd in (0, 1))
+    side_even, side_odd = swap(key_value, slab_even), swap(key_value, slab_odd)
     even, odd = swap(key_value, weight_even), swap(key_value, weight_odd)
     query, cotangent = call(
         query_kernel,
         [((count, HD), BF), ((count, HD), BF)],
         [tokens, grad_out, full_qkv, full_proj],
     )
-    even, odd, turned, query, cotangent = lax.optimization_barrier(
-        (even, odd, turned, query, cotangent)
-    )
-    columns = jnp.stack([key_value, even, odd])
-    across_even, across_odd = swap(columns, slab_even), swap(columns, slab_odd)
-    pair = (3, count, 2 * HD)
-    attended, grad_query, parts_own, parts_even, parts_odd = call(
+    side_even, side_odd, even, odd, turned, query, cotangent = lax.optimization_barrier(
+        (side_even, side_odd, even, odd, turned, query, cotangent)
+    )
+    columns = jnp.stack([even, odd])
+    far_even, far_odd = swap(columns, slab_even), swap(columns, slab_odd)
+    one = (count, 2 * HD)
+    square = (count, count)
+    (
+        attended, delta, scale, grad_query, parts_even, parts_odd,
+        scores, halves, side_scores, side_halves,
+    ) = call(
         functools.partial(attention_kernel, (slabs, weights)),
-        [((count, HD), BF), ((count, HD), BF), (pair, BF), (pair, BF), (pair, BF)],
-        [index, query, cotangent, key_value, even, odd, across_even, across_odd],
-        scratch=[pltpu.VMEM((9, count, count), F32), pltpu.VMEM((9, count, count), BF)],
+        [
+            ((count, HD), BF), ((count, 1), F32), ((count, 1), F32), ((count, HD), F32),
+            ((2, *one), BF), ((2, *one), BF), ((3, *square), F32), ((3, *square), BF),
+            ((2, *square), F32), ((2, *square), BF),
+        ],
+        [
+            index, query, cotangent, key_value, even, odd,
+            side_even, side_odd, far_even, far_odd,
+        ],
+        scratch=[pltpu.VMEM((4, *square), F32), pltpu.VMEM((4, *square), BF)],
         scalars=1,
     )
     parts_even, parts_odd = swap(parts_even, slab_even), swap(parts_odd, slab_odd)
+    grad_query, parts_own = call(
+        near_grads_kernel,
+        [((count, HD), F32), ((3, *one), BF)],
+        [query, cotangent, key_value, even, odd, delta, scale, grad_query, scores, halves],
+    )
     (mixed,) = call(
         mixed_kernel,
         [((count, features), BF)],
         [attended, full_proj],
         final=True,
     )
-    parts_even, parts_odd, mixed = lax.optimization_barrier((parts_even, parts_odd, mixed))
+    parts_even, parts_odd, parts_own, mixed = lax.optimization_barrier(
+        (parts_even, parts_odd, parts_own, mixed)
+    )
 
     def summed(column):
-        return (
-            parts_own[column].astype(F32)
-            + parts_even[column].astype(F32)
-            + parts_odd[column].astype(F32)
-        )
-
-    even = swap(summed(1).astype(BF), weight_even)
-    odd = swap(summed(2).astype(BF), weight_odd)
+        total = parts_own[column + 1].astype(F32)
+        total = total + parts_even[column].astype(F32) + parts_odd[column].astype(F32)
+        return total.astype(BF)
+
+    grad_query, even, odd = lax.optimization_barrier((grad_query, summed(0), summed(1)))
+    grad_query, side_even, side_odd = call(
+        side_grads_kernel,
+        [((count, HD), BF), (one, BF), (one, BF)],
+        [
+            query, cotangent, side_even, side_odd, delta, scale, grad_query,
+            side_scores, side_halves,
+        ],
+    )
+    side_even, side_odd = swap(side_even, slab_even), swap(side_odd, slab_odd)
+    even, odd = swap(even, weight_even), swap(odd, weight_odd)
     half = (1 << len(steps), rows, lanes)
-    grad_rows, keep, send = call(
-        functools.partial(weight_grads_kernel, steps, slabs, split),
-        [((count, 3 * HD), BF), (half, BF), (half, BF)],
-        [index, turned, grad_query, summed(0), even, odd, attended],
-        scratch=[pltpu.VMEM((slabs, features, lanes), BF)],
+    factors = (2 * count, slabs // 2 * lanes)
+    grad_rows, kept, send = call(
+        functools.partial(away_grads_kernel, steps, slabs, split),
+        [((count, 3 * HD), BF), (factors, BF), (half, BF)],
+        [index, turned, even, odd, grad_query, parts_own, side_even, side_odd, attended],
+        scratch=[pltpu.VMEM(factors, BF), pltpu.VMEM((slabs // 2, features, lanes), BF)],
         scalars=1,
     )
     got = swap(send, core_pairs(slabs, weights))
+    (keep,) = call(
+        functools.partial(kept_grads_kernel, steps),
+        [(half, BF)],
+        [index, turned, kept],
+        scratch=[pltpu.VMEM((slabs // 2, features, lanes), BF)],
+        scalars=1,
+    )
+    got, keep = lax.optimization_barrier((got, keep))
     for step in reversed(steps):
         near = keep.shape[0] // 2
         send = (keep[near:].astype(F32) + got[near:].astype(F32)).astype(BF)

time: 101 us -> 99.3 us (0.983)
  waiting for transfers between devices: 42.3 us -> 34.5 us
  starting transfers between devices: 44.5 us -> 49.2 us
  Pallas kernels: 12.4 us -> 13.7 us
    ppermute x18 -> x22, waiting for transfers between devices: 42.3 us -> 34.5 us  [swap(): return lax.ppermute(values, AXES, pairs)]
    ppermute x18 -> x22, starting transfers between devices: 44.5 us -> 49.2 us  [swap(): return lax.ppermute(values, AXES, pairs)]
    pallas_call x8 -> x11, Pallas kernels: 11.4 us -> 12.7 us  [call(): pl.pallas_call(kernel, out_shape=[make(shape, kind) for shape, kind in ou...]
  transfers between devices with their start and end apart: 18 -> 22, of which waited for: 13 -> 13; matrix products, arithmetic and copies ran while one was open for 0% -> 0% of each run, Pallas kernels for 4% -> 6%
where the time goes in v5:
time: 99.3 us; the launch traced here: 99 us
  starting transfers between devices  49.2 us (50%)
  waiting for transfers between devices  34.5 us (35%)
  Pallas kernels  13.7 us (14%)
    ppermute x22, starting transfers between devices, swap(): return lax.ppermute(values, AXES, pairs)  49.2 us
    ppermute x22, waiting for transfers between devices, swap(): return lax.ppermute(values, AXES, pairs)  34.5 us
    pallas_call x11, Pallas kernels, call(): pl.pallas_call(kernel, out_shape=[make(shape, kind) for shape, kind in ou...  12.7 us
  transfers between devices with their start and end apart: 22, of which 13 were waited for; matrix products, arithmetic and copies ran while one was open for 0% of the time, Pallas kernels for 6%

profile of v5, /device:TPU:0, one launch (start us, length us, event | category | flops | bytes accessed | tf_op | source)
XLA Modules:
  0.0 99.0 jit_solution(15301998518089371294)
XLA Ops:
  0.6 1.0 %shard_map.75 = bf16[1,192,128]{2,1,0:T(8,128)(2,1)S(1)} custom-call(bf16[192,96]{1,0:T(8,128)(2,1)} %qkv_hbm.1, bf16[32,192]{1,0:T(8,128)(2,1)} %proj_hbm.1), custom_call_target="tpu_custom_call" | custom-call | tf_op jit(solution)/shard_map/pallas_call | solution.py:284
  1.7 4.1 %collective-permute-start = (bf16[1,192,128]{2,1,0:T(8,128)(2,1)S(1)}, bf16[1,192,128]{2,1,0:T(8,128)(2,1)S(1)}, u32[]{:S(2)}, u32[]{:S(2)}) collective-permute-start(bf16[1,192,128]{2,1,0:T(8,128)(2,1)S(1)} %shard_map.75), channel_id=1, source_target_pairs={{0,4},{1,5},{2,6},{3,7},{4,0},{5,1},{6,2},{7,3},{8,12},{9,13},{10,... | collective-permute-start | bytes 147464 | tf_op jit(solution)/shard_map/ppermute | solution.py:282
  5.8 2.6 %collective-permute-done = bf16[1,192,128]{2,1,0:T(8,128)(2,1)S(1)} collective-permute-done((bf16[1,192,128]{2,1,0:T(8,128)(2,1)S(1)}, bf16[1,192,128]{2,1,0:T(8,128)(2,1)S(1)}, u32[]{:S(2)}, u32[]{:S(2)}) %collective-permute-start) | collective-permute-done | bytes 49184 | tf_op jit(solution)/shard_map/ppermute | solution.py:282
  8.4 1.8 %collective-permute-start.1 = (bf16[2,192,128]{2,1,0:T(8,128)(2,1)S(1)}, bf16[2,192,128]{2,1,0:T(8,128)(2,1)S(1)}, u32[]{:S(2)}, u32[]{:S(2)}) collective-permute-start(bf16[2,192,128]{2,1,0:T(8,128)(2,1)S(1)} %pad_maximum_fusion.3), channel_id=1, source_target_pairs={{0,16},{1,17},{2,18},{3,19},{4,20},{5,21},{6,22},{7,23},{8,9},{9,8... | collective-permute-start | bytes 294920 | tf_op jit(solution)/shard_map/ppermute | solution.py:282
  10.2 2.9 %collective-permute-done.1 = bf16[2,192,128]{2,1,0:T(8,128)(2,1)S(1)} collective-permute-done((bf16[2,192,128]{2,1,0:T(8,128)(2,1)S(1)}, bf16[2,192,128]{2,1,0:T(8,128)(2,1)S(1)}, u32[]{:S(2)}, u32[]{:S(2)}) %collective-permute-start.1) | collective-permute-done | bytes 98336 | tf_op jit(solution)/shard_map/ppermute | solution.py:282
  13.1 1.8 %collective-permute-start.2 = (bf16[4,192,128]{2,1,0:T(8,128)(2,1)S(1)}, bf16[4,192,128]{2,1,0:T(8,128)(2,1)S(1)}, u32[]{:S(2)}, u32[]{:S(2)}) collective-permute-start(bf16[4,192,128]{2,1,0:T(8,128)(2,1)S(1)} %pad_maximum_fusion.2), channel_id=1, source_target_pairs={{0,1},{1,0},{2,3},{3,2},{4,5},{5,4},{6,7},{7,6},{8,10},{9,11},{10,... | collective-permute-start | bytes 589832 | tf_op jit(solution)/shard_map/ppermute | solution.py:282
  14.9 3.9 %collective-permute-done.2 = bf16[4,192,128]{2,1,0:T(8,128)(2,1)S(1)} collective-permute-done((bf16[4,192,128]{2,1,0:T(8,128)(2,1)S(1)}, bf16[4,192,128]{2,1,0:T(8,128)(2,1)S(1)}, u32[]{:S(2)}, u32[]{:S(2)}) %collective-permute-start.2) | collective-permute-done | bytes 196640 | tf_op jit(solution)/shard_map/ppermute | solution.py:282
  18.9 1.4 %collective-permute-start.3 = (bf16[8,192,128]{2,1,0:T(8,128)(2,1)S(1)}, bf16[8,192,128]{2,1,0:T(8,128)(2,1)S(1)}, u32[]{:S(2)}, u32[]{:S(2)}) collective-permute-start(bf16[8,192,128]{2,1,0:T(8,128)(2,1)S(1)} %pad_maximum_fusion), channel_id=1, source_target_pairs={{0,2},{1,3},{2,0},{3,1},{4,6},{5,7},{6,4},{7,5},{8,24},{9,25},{10,... | collective-permute-start | bytes 1179656 | tf_op jit(solution)/shard_map/ppermute | solution.py:282
  20.4 6.3 %collective-permute-done.3 = bf16[8,192,128]{2,1,0:T(8,128)(2,1)S(1)} collective-permute-done((bf16[8,192,128]{2,1,0:T(8,128)(2,1)S(1)}, bf16[8,192,128]{2,1,0:T(8,128)(2,1)S(1)}, u32[]{:S(2)}, u32[]{:S(2)}) %collective-permute-start.3) | collective-permute-done | bytes 393248 | tf_op jit(solution)/shard_map/ppermute | solution.py:282
  27.0 2.2 %collective-permute-done.4.got = bf16[16,192,128]{2,1,0:T(8,128)(2,1)S(1)} collective-permute-done((bf16[16,192,128]{2,1,0:T(8,128)(2,1)S(1)}, bf16[16,192,128]{2,1,0:T(8,128)(2,1)S(1)}, u32[]{:S(2)}, u32[]{:S(2)}) %collective-permute-start.4) | collective-permute-done | bytes 786464 | tf_op jit(solution)/shard_map/ppermute | solution.py:282
  29.2 1.4 %shard_map.76 = (bf16[256,256]{1,0:T(8,128)(2,1)S(1)}, bf16[1536,384]{1,0:T(8,128)(2,1)S(1)}, bf16[1536,128]{1,0:T(8,128)(2,1)S(1)}) custom-call(s32[2]{0:T(128)S(1)} %pad_add_fusion.index, bf16[16,192,128]{2,1,0:T(8,128)(2,1)S(1)} %constant_dynamic-update-slice_fusion.own, bf16[16,192,128]{2,1,0:T(8,128)(2,1)S(1)} %collective-permute-done.4.got, ...), custom_call_target="tpu_custom_call" | custom-call | tf_op jit(solution)/shard_map/pallas_call | solution.py:264
  31.2 4.1 %collective-permute-start.7 = (bf16[256,256]{1,0:T(8,128)(2,1)S(1)}, bf16[256,256]{1,0:T(8,128)(2,1)S(1)}, u32[]{:S(2)}, u32[]{:S(2)}) collective-permute-start(bf16[256,256]{1,0:T(8,128)(2,1)S(1)} %get-tuple-element.47.own), channel_id=1, source_target_pairs={{0,1},{1,0},{2,3},{3,2},{4,5},{5,4},{6,7},{7,6},{8,9},{9,8},{10,11... | collective-permute-start | bytes 393224 | tf_op jit(solution)/shard_map/ppermute | solution.py:282
  36.0 2.9 %collective-permute-start.5 = (bf16[256,256]{1,0:T(8,128)(2,1)S(1)}, bf16[256,256]{1,0:T(8,128)(2,1)S(1)}, u32[]{:S(2)}, u32[]{:S(2)}) collective-permute-start(bf16[256,256]{1,0:T(8,128)(2,1)S(1)} %get-tuple-element.47.own), channel_id=1, source_target_pairs={{0,8},{1,9},{2,10},{3,11},{4,12},{5,13},{6,14},{7,15},{8,0},{9,1},... | collective-permute-start | bytes 393224 | tf_op jit(solution)/shard_map/ppermute | solution.py:282
  41.6 3.6 %collective-permute-start.9 = (bf16[2,256,256]{2,1,0:T(8,128)(2,1)S(1)}, bf16[2,256,256]{2,1,0:T(8,128)(2,1)S(1)}, u32[]{:S(2)}, u32[]{:S(2)}) collective-permute-start(bf16[2,256,256]{2,1,0:T(8,128)(2,1)S(1)} %pad_maximum_fusion.1), channel_id=1, source_target_pairs={{0,8},{1,9},{2,10},{3,11},{4,12},{5,13},{6,14},{7,15},{8,0},{9,1},... | collective-permute-start | bytes 786440 | tf_op jit(solution)/shard_map/ppermute | solution.py:282
  45.3 1.2 %collective-permute-done.9.far_even = bf16[2,256,256]{2,1,0:T(8,128)(2,1)S(1)} collective-permute-done((bf16[2,256,256]{2,1,0:T(8,128)(2,1)S(1)}, bf16[2,256,256]{2,1,0:T(8,128)(2,1)S(1)}, u32[]{:S(2)}, u32[]{:S(2)}) %collective-permute-start.9) | collective-permute-done | bytes 262176 | tf_op jit(solution)/shard_map/ppermute | solution.py:282
  46.4 2.6 %shard_map.79 = (bf16[256,128]{1,0:T(8,128)(2,1)S(1)}, f32[256,1]{1,0:T(8,128)S(1)}, f32[256,1]{1,0:T(8,128)S(1)}, f32[256,128]{1,0:T(8,128)S(1)}, bf16[2,256,25...) custom-call(s32[2]{0:T(128)S(1)} %pad_add_fusion.index, ...), custom_call_target="tpu_custom_call" | custom-call | tf_op jit(solution)/shard_map/pallas_call | solution.py:264
  49.0 2.9 %collective-permute-start.11 = (bf16[2,256,256]{2,1,0:T(8,128)(2,1)S(1)}, bf16[2,256,256]{2,1,0:T(8,128)(2,1)S(1)}, u32[]{:S(2)}, u32[]{:S(2)}) collective-permute-start(bf16[2,256,256]{2,1,0:T(8,128)(2,1)S(1)} %get-tuple-element.58), channel_id=1, source_target_pairs={{0,8},{1,9},{2,10},{3,11},{4,12},{5,13},{6,14},{7,15},{8,0},{9,1},... | collective-permute-start | bytes 786440 | tf_op jit(solution)/shard_map/ppermute | solution.py:282
  52.6 1.3 %shard_map.81 = bf16[256,1536]{1,0:T(8,128)(2,1)} custom-call(bf16[256,128]{1,0:T(8,128)(2,1)S(1)} %get-tuple-element.66.att_ref, bf16[1536,128]{1,0:T(8,128)(2,1)S(1)} %get-tuple-element.49.proj_ref), custom_call_target="tpu_custom_call" | custom-call | tf_op jit(solution)/shard_map/pallas_call | solution.py:264
  54.8 2.0 %collective-permute-start.13 = (bf16[256,256]{1,0:T(8,128)(2,1)S(1)}, bf16[256,256]{1,0:T(8,128)(2,1)S(1)}, u32[]{:S(2)}, u32[]{:S(2)}) collective-permute-start(bf16[256,256]{1,0:T(8,128)(2,1)S(1)} %get-tuple-element.73), channel_id=1, source_target_pairs={{0,1},{1,0},{2,3},{3,2},{4,5},{5,4},{6,7},{7,6},{8,9},{9,8},{10,11... | collective-permute-start | bytes 393224 | tf_op jit(solution)/shard_map/ppermute | solution.py:282
  58.1 5.0 %collective-permute-start.15 = (bf16[256,256]{1,0:T(8,128)(2,1)S(1)}, bf16[256,256]{1,0:T(8,128)(2,1)S(1)}, u32[]{:S(2)}, u32[]{:S(2)}) collective-permute-start(bf16[256,256]{1,0:T(8,128)(2,1)S(1)} %get-tuple-element.79), channel_id=1, source_target_pairs={{0,8},{1,9},{2,10},{3,11},{4,12},{5,13},{6,14},{7,15},{8,0},{9,1},... | collective-permute-start | bytes 393224 | tf_op jit(solution)/shard_map/ppermute | solution.py:282
  64.1 1.5 %shard_map.83 = (bf16[256,384]{1,0:T(8,128)(2,1)S(1)}, bf16[512,256]{1,0:T(8,128)(2,1)S(1)}, bf16[16,192,128]{2,1,0:T(8,128)(2,1)S(1)}) custom-call(s32[2]{0:T(128)S(1)} %pad_add_fusion.index, bf16[1536,512]{1,0:T(8,128)(2,1)S(1)} %shard_map.77.turned, bf16[256,256]{1,0:T(8,128)(2,1)S(1)} %collective-permute-done.13.even, ...), custom_call_target="tpu_custom_call" | custom-call | tf_op jit(solution)/shard_map/pallas_call | solution.py:264
  65.6 5.4 %collective-permute-start.17 = (bf16[16,192,128]{2,1,0:T(8,128)(2,1)S(1)}, bf16[16,192,128]{2,1,0:T(8,128)(2,1)S(1)}, u32[]{:S(2)}, u32[]{:S(2)}) collective-permute-start(bf16[16,192,128]{2,1,0:T(8,128)(2,1)S(1)} %get-tuple-element.81), channel_id=1, source_target_pairs={{0,8},{1,9},{2,10},{3,11},{4,12},{5,13},{6,14},{7,15},{8,0},{9,1},... | collective-permute-start | bytes 2359304 | tf_op jit(solution)/shard_map/ppermute | solution.py:282
  71.0 1.2 %shard_map.84 = bf16[16,192,128]{2,1,0:T(8,128)(2,1)S(1)} custom-call(s32[2]{0:T(128)S(1)} %pad_add_fusion.index, bf16[1536,512]{1,0:T(8,128)(2,1)S(1)} %shard_map.77.turned, bf16[512,256]{1,0:T(8,128)(2,1)S(1)} %get-tuple-element.82.kept), custom_call_target="tpu_custom_call" | custom-call | tf_op jit(solution)/shard_map/pallas_call | solution.py:264
  73.1 2.9 %collective-permute-start.18 = (bf16[8,192,128]{2,1,0:T(8,128)(2,1)S(1)}, bf16[8,192,128]{2,1,0:T(8,128)(2,1)S(1)}, u32[]{:S(2)}, u32[]{:S(2)}) collective-permute-start(bf16[8,192,128]{2,1,0:T(8,128)(2,1)S(1)} %get-tuple-element.91), channel_id=1, source_target_pairs={{0,2},{1,3},{2,0},{3,1},{4,6},{5,7},{6,4},{7,5},{8,24},{9,25},{10,... | collective-permute-start | bytes 1179656 | tf_op jit(solution)/shard_map/ppermute | solution.py:282
  76.0 1.5 %shard_map.85 = bf16[256,1536]{1,0:T(8,128)(2,1)} custom-call(bf16[256,384]{1,0:T(8,128)(2,1)S(1)} %get-tuple-element.85.rows_ref, bf16[1536,384]{1,0:T(8,128)(2,1)S(1)} %get-tuple-element.48.qkv_ref), custom_call_target="tpu_custom_call" | custom-call | tf_op jit(solution)/shard_map/pallas_call | solution.py:264
  77.4 4.3 %collective-permute-done.18 = bf16[8,192,128]{2,1,0:T(8,128)(2,1)S(1)} collective-permute-done((bf16[8,192,128]{2,1,0:T(8,128)(2,1)S(1)}, bf16[8,192,128]{2,1,0:T(8,128)(2,1)S(1)}, u32[]{:S(2)}, u32[]{:S(2)}) %collective-permute-start.18) | collective-permute-done | bytes 393248 | tf_op jit(solution)/shard_map/ppermute | solution.py:282
  81.8 3.0 %collective-permute-start.19 = (bf16[4,192,128]{2,1,0:T(8,128)(2,1)S(1)}, bf16[4,192,128]{2,1,0:T(8,128)(2,1)S(1)}, u32[]{:S(2)}, u32[]{:S(2)}) collective-permute-start(bf16[4,192,128]{2,1,0:T(8,128)(2,1)S(1)} %get-tuple-element.92), channel_id=1, source_target_pairs={{0,1},{1,0},{2,3},{3,2},{4,5},{5,4},{6,7},{7,6},{8,10},{9,11},{10,... | collective-permute-start | bytes 589832 | tf_op jit(solution)/shard_map/ppermute | solution.py:282
  84.8 3.6 %collective-permute-done.19 = bf16[4,192,128]{2,1,0:T(8,128)(2,1)S(1)} collective-permute-done((bf16[4,192,128]{2,1,0:T(8,128)(2,1)S(1)}, bf16[4,192,128]{2,1,0:T(8,128)(2,1)S(1)}, u32[]{:S(2)}, u32[]{:S(2)}) %collective-permute-start.19) | collective-permute-done | bytes 196640 | tf_op jit(solution)/shard_map/ppermute | solution.py:282
  88.5 2.1 %collective-permute-start.20 = (bf16[2,192,128]{2,1,0:T(8,128)(2,1)S(1)}, bf16[2,192,128]{2,1,0:T(8,128)(2,1)S(1)}, u32[]{:S(2)}, u32[]{:S(2)}) collective-permute-start(bf16[2,192,128]{2,1,0:T(8,128)(2,1)S(1)} %get-tuple-element.96), channel_id=1, source_target_pairs={{0,16},{1,17},{2,18},{3,19},{4,20},{5,21},{6,22},{7,23},{8,9},{9,8... | collective-permute-start | bytes 294920 | tf_op jit(solution)/shard_map/ppermute | solution.py:282
  90.6 2.6 %collective-permute-done.20 = bf16[2,192,128]{2,1,0:T(8,128)(2,1)S(1)} collective-permute-done((bf16[2,192,128]{2,1,0:T(8,128)(2,1)S(1)}, bf16[2,192,128]{2,1,0:T(8,128)(2,1)S(1)}, u32[]{:S(2)}, u32[]{:S(2)}) %collective-permute-start.20) | collective-permute-done | bytes 98336 | tf_op jit(solution)/shard_map/ppermute | solution.py:282
  93.2 2.2 %collective-permute-start.21 = (bf16[1,192,128]{2,1,0:T(8,128)(2,1)S(1)}, bf16[1,192,128]{2,1,0:T(8,128)(2,1)S(1)}, u32[]{:S(2)}, u32[]{:S(2)}) collective-permute-start(bf16[1,192,128]{2,1,0:T(8,128)(2,1)S(1)} %get-tuple-element.98), channel_id=1, source_target_pairs={{0,4},{1,5},{2,6},{3,7},{4,0},{5,1},{6,2},{7,3},{8,12},{9,13},{10,... | collective-permute-start | bytes 147464 | tf_op jit(solution)/shard_map/ppermute | solution.py:282
  95.4 2.8 %collective-permute-done.21.got = bf16[1,192,128]{2,1,0:T(8,128)(2,1)S(1)} collective-permute-done((bf16[1,192,128]{2,1,0:T(8,128)(2,1)S(1)}, bf16[1,192,128]{2,1,0:T(8,128)(2,1)S(1)}, u32[]{:S(2)}, u32[]{:S(2)}) %collective-permute-start.21) | collective-permute-done | bytes 49184 | tf_op jit(solution)/shard_map/ppermute | solution.py:282
  (43 shorter events, 10.1 us)
Async XLA Ops:
  0.6 28.5 %copy-start = (bf16[256,1536]{1,0:T(8,128)(2,1)S(1)}, bf16[256,1536]{1,0:T(8,128)(2,1)}, u32[]{:S(2)}) copy-start(bf16[256,1536]{1,0:T(8,128)(2,1)} %tokens.5) | copy-start | bytes 2359300
  1.7 6.7 %collective-permute-start = (bf16[1,192,128]{2,1,0:T(8,128)(2,1)S(1)}, bf16[1,192,128]{2,1,0:T(8,128)(2,1)S(1)}, u32[]{:S(2)}, u32[]{:S(2)}) collective-permute-start(bf16[1,192,128]{2,1,0:T(8,128)(2,1)S(1)} %shard_map.75), channel_id=1, source_target_pairs={{0,4},{1,5},{2,6},{3,7},{4,0},{5,1},{6,2},{7,3},{8,12},{9,13},{10,... | collective-permute-start | bytes 147464 | tf_op jit(solution)/shard_map/ppermute | solution.py:282
  8.4 4.7 %collective-permute-start.1 = (bf16[2,192,128]{2,1,0:T(8,128)(2,1)S(1)}, bf16[2,192,128]{2,1,0:T(8,128)(2,1)S(1)}, u32[]{:S(2)}, u32[]{:S(2)}) collective-permute-start(bf16[2,192,128]{2,1,0:T(8,128)(2,1)S(1)} %pad_maximum_fusion.3), channel_id=1, source_target_pairs={{0,16},{1,17},{2,18},{3,19},{4,20},{5,21},{6,22},{7,23},{8,9},{9,8... | collective-permute-start | bytes 294920 | tf_op jit(solution)/shard_map/ppermute | solution.py:282
  13.1 5.7 %collective-permute-start.2 = (bf16[4,192,128]{2,1,0:T(8,128)(2,1)S(1)}, bf16[4,192,128]{2,1,0:T(8,128)(2,1)S(1)}, u32[]{:S(2)}, u32[]{:S(2)}) collective-permute-start(bf16[4,192,128]{2,1,0:T(8,128)(2,1)S(1)} %pad_maximum_fusion.2), channel_id=1, source_target_pairs={{0,1},{1,0},{2,3},{3,2},{4,5},{5,4},{6,7},{7,6},{8,10},{9,11},{10,... | collective-permute-start | bytes 589832 | tf_op jit(solution)/shard_map/ppermute | solution.py:282
  18.9 7.8 %collective-permute-start.3 = (bf16[8,192,128]{2,1,0:T(8,128)(2,1)S(1)}, bf16[8,192,128]{2,1,0:T(8,128)(2,1)S(1)}, u32[]{:S(2)}, u32[]{:S(2)}) collective-permute-start(bf16[8,192,128]{2,1,0:T(8,128)(2,1)S(1)} %pad_maximum_fusion), channel_id=1, source_target_pairs={{0,2},{1,3},{2,0},{3,1},{4,6},{5,7},{6,4},{7,5},{8,24},{9,25},{10,... | collective-permute-start | bytes 1179656 | tf_op jit(solution)/shard_map/ppermute | solution.py:282
  20.4 18.5 %copy-start.1 = (bf16[256,1536]{1,0:T(8,128)(2,1)S(1)}, bf16[256,1536]{1,0:T(8,128)(2,1)}, u32[]{:S(2)}) copy-start(bf16[256,1536]{1,0:T(8,128)(2,1)} %grad_out.3) | copy-start | bytes 2359300
  26.8 2.4 %collective-permute-start.4 = (bf16[16,192,128]{2,1,0:T(8,128)(2,1)S(1)}, bf16[16,192,128]{2,1,0:T(8,128)(2,1)S(1)}, u32[]{:S(2)}, u32[]{:S(2)}) collective-permute-start(bf16[16,192,128]{2,1,0:T(8,128)(2,1)S(1)} %constant_dynamic-update-slice_fusion.own), channel_id=1, source_target_pairs={{0,8},{1,9},{2,10},{3,11},{4,12},{5,13},{6,14},{7,15},{8,0},{9,1},... | collective-permute-start | bytes 2359304 | tf_op jit(solution)/shard_map/ppermute | solution.py:282
  30.5 9.4 %collective-permute-start.8 = (bf16[256,256]{1,0:T(8,128)(2,1)S(1)}, bf16[256,256]{1,0:T(8,128)(2,1)S(1)}, u32[]{:S(2)}, u32[]{:S(2)}) collective-permute-start(bf16[256,256]{1,0:T(8,128)(2,1)S(1)} %get-tuple-element.47.own), channel_id=1, source_target_pairs={{1,2},{2,1},{3,4},{4,3},{5,6},{6,5},{9,10},{10,9},{11,12},{12,11},... | collective-permute-start | bytes 393224 | tf_op jit(solution)/shard_map/ppermute | solution.py:282
  31.2 9.7 %collective-permute-start.7 = (bf16[256,256]{1,0:T(8,128)(2,1)S(1)}, bf16[256,256]{1,0:T(8,128)(2,1)S(1)}, u32[]{:S(2)}, u32[]{:S(2)}) collective-permute-start(bf16[256,256]{1,0:T(8,128)(2,1)S(1)} %get-tuple-element.47.own), channel_id=1, source_target_pairs={{0,1},{1,0},{2,3},{3,2},{4,5},{5,4},{6,7},{7,6},{8,9},{9,8},{10,11... | collective-permute-start | bytes 393224 | tf_op jit(solution)/shard_map/ppermute | solution.py:282
  35.4 5.6 %collective-permute-start.6 = (bf16[256,256]{1,0:T(8,128)(2,1)S(1)}, bf16[256,256]{1,0:T(8,128)(2,1)S(1)}, u32[]{:S(2)}, u32[]{:S(2)}) collective-permute-start(bf16[256,256]{1,0:T(8,128)(2,1)S(1)} %get-tuple-element.47.own), channel_id=1, source_target_pairs={{8,16},{9,17},{10,18},{11,19},{12,20},{13,21},{14,22},{15,23},{16,... | collective-permute-start | bytes 393224 | tf_op jit(solution)/shard_map/ppermute | solution.py:282
  36.0 4.9 %collective-permute-start.5 = (bf16[256,256]{1,0:T(8,128)(2,1)S(1)}, bf16[256,256]{1,0:T(8,128)(2,1)S(1)}, u32[]{:S(2)}, u32[]{:S(2)}) collective-permute-start(bf16[256,256]{1,0:T(8,128)(2,1)S(1)} %get-tuple-element.47.own), channel_id=1, source_target_pairs={{0,8},{1,9},{2,10},{3,11},{4,12},{5,13},{6,14},{7,15},{8,0},{9,1},... | collective-permute-start | bytes 393224 | tf_op jit(solution)/shard_map/ppermute | solution.py:282
  41.0 4.3 %collective-permute-start.10 = (bf16[2,256,256]{2,1,0:T(8,128)(2,1)S(1)}, bf16[2,256,256]{2,1,0:T(8,128)(2,1)S(1)}, u32[]{:S(2)}, u32[]{:S(2)}) collective-permute-start(bf16[2,256,256]{2,1,0:T(8,128)(2,1)S(1)} %pad_maximum_fusion.1), channel_id=1, source_target_pairs={{8,16},{9,17},{10,18},{11,19},{12,20},{13,21},{14,22},{15,23},{16,... | collective-permute-start | bytes 786440 | tf_op jit(solution)/shard_map/ppermute | solution.py:282
  41.6 4.8 %collective-permute-start.9 = (bf16[2,256,256]{2,1,0:T(8,128)(2,1)S(1)}, bf16[2,256,256]{2,1,0:T(8,128)(2,1)S(1)}, u32[]{:S(2)}, u32[]{:S(2)}) collective-permute-start(bf16[2,256,256]{2,1,0:T(8,128)(2,1)S(1)} %pad_maximum_fusion.1), channel_id=1, source_target_pairs={{0,8},{1,9},{2,10},{3,11},{4,12},{5,13},{6,14},{7,15},{8,0},{9,1},... | collective-permute-start | bytes 786440 | tf_op jit(solution)/shard_map/ppermute | solution.py:282
  49.0 5.7 %collective-permute-start.11 = (bf16[2,256,256]{2,1,0:T(8,128)(2,1)S(1)}, bf16[2,256,256]{2,1,0:T(8,128)(2,1)S(1)}, u32[]{:S(2)}, u32[]{:S(2)}) collective-permute-start(bf16[2,256,256]{2,1,0:T(8,128)(2,1)S(1)} %get-tuple-element.58), channel_id=1, source_target_pairs={{0,8},{1,9},{2,10},{3,11},{4,12},{5,13},{6,14},{7,15},{8,0},{9,1},... | collective-permute-start | bytes 786440 | tf_op jit(solution)/shard_map/ppermute | solution.py:282
  51.9 2.8 %collective-permute-start.12 = (bf16[2,256,256]{2,1,0:T(8,128)(2,1)S(1)}, bf16[2,256,256]{2,1,0:T(8,128)(2,1)S(1)}, u32[]{:S(2)}, u32[]{:S(2)}) collective-permute-start(bf16[2,256,256]{2,1,0:T(8,128)(2,1)S(1)} %get-tuple-element.59), channel_id=1, source_target_pairs={{8,16},{9,17},{10,18},{11,19},{12,20},{13,21},{14,22},{15,23},{16,... | collective-permute-start | bytes 786440 | tf_op jit(solution)/shard_map/ppermute | solution.py:282
  54.8 8.9 %collective-permute-start.13 = (bf16[256,256]{1,0:T(8,128)(2,1)S(1)}, bf16[256,256]{1,0:T(8,128)(2,1)S(1)}, u32[]{:S(2)}, u32[]{:S(2)}) collective-permute-start(bf16[256,256]{1,0:T(8,128)(2,1)S(1)} %get-tuple-element.73), channel_id=1, source_target_pairs={{0,1},{1,0},{2,3},{3,2},{4,5},{5,4},{6,7},{7,6},{8,9},{9,8},{10,11... | collective-permute-start | bytes 393224 | tf_op jit(solution)/shard_map/ppermute | solution.py:282
  56.8 7.0 %collective-permute-start.14 = (bf16[256,256]{1,0:T(8,128)(2,1)S(1)}, bf16[256,256]{1,0:T(8,128)(2,1)S(1)}, u32[]{:S(2)}, u32[]{:S(2)}) collective-permute-start(bf16[256,256]{1,0:T(8,128)(2,1)S(1)} %get-tuple-element.74), channel_id=1, source_target_pairs={{1,2},{2,1},{3,4},{4,3},{5,6},{6,5},{9,10},{10,9},{11,12},{12,11},... | collective-permute-start | bytes 393224 | tf_op jit(solution)/shard_map/ppermute | solution.py:282
  58.1 6.0 %collective-permute-start.15 = (bf16[256,256]{1,0:T(8,128)(2,1)S(1)}, bf16[256,256]{1,0:T(8,128)(2,1)S(1)}, u32[]{:S(2)}, u32[]{:S(2)}) collective-permute-start(bf16[256,256]{1,0:T(8,128)(2,1)S(1)} %get-tuple-element.79), channel_id=1, source_target_pairs={{0,8},{1,9},{2,10},{3,11},{4,12},{5,13},{6,14},{7,15},{8,0},{9,1},... | collective-permute-start | bytes 393224 | tf_op jit(solution)/shard_map/ppermute | solution.py:282
  63.1 1.0 collective-permute-start.16
  65.6 7.3 %collective-permute-start.17 = (bf16[16,192,128]{2,1,0:T(8,128)(2,1)S(1)}, bf16[16,192,128]{2,1,0:T(8,128)(2,1)S(1)}, u32[]{:S(2)}, u32[]{:S(2)}) collective-permute-start(bf16[16,192,128]{2,1,0:T(8,128)(2,1)S(1)} %get-tuple-element.81), channel_id=1, source_target_pairs={{0,8},{1,9},{2,10},{3,11},{4,12},{5,13},{6,14},{7,15},{8,0},{9,1},... | collective-permute-start | bytes 2359304 | tf_op jit(solution)/shard_map/ppermute | solution.py:282
  73.1 8.6 %collective-permute-start.18 = (bf16[8,192,128]{2,1,0:T(8,128)(2,1)S(1)}, bf16[8,192,128]{2,1,0:T(8,128)(2,1)S(1)}, u32[]{:S(2)}, u32[]{:S(2)}) collective-permute-start(bf16[8,192,128]{2,1,0:T(8,128)(2,1)S(1)} %get-tuple-element.91), channel_id=1, source_target_pairs={{0,2},{1,3},{2,0},{3,1},{4,6},{5,7},{6,4},{7,5},{8,24},{9,25},{10,... | collective-permute-start | bytes 1179656 | tf_op jit(solution)/shard_map/ppermute | solution.py:282
  81.8 6.7 %collective-permute-start.19 = (bf16[4,192,128]{2,1,0:T(8,128)(2,1)S(1)}, bf16[4,192,128]{2,1,0:T(8,128)(2,1)S(1)}, u32[]{:S(2)}, u32[]{:S(2)}) collective-permute-start(bf16[4,192,128]{2,1,0:T(8,128)(2,1)S(1)} %get-tuple-element.92), channel_id=1, source_target_pairs={{0,1},{1,0},{2,3},{3,2},{4,5},{5,4},{6,7},{7,6},{8,10},{9,11},{10,... | collective-permute-start | bytes 589832 | tf_op jit(solution)/shard_map/ppermute | solution.py:282
  88.5 4.7 %collective-permute-start.20 = (bf16[2,192,128]{2,1,0:T(8,128)(2,1)S(1)}, bf16[2,192,128]{2,1,0:T(8,128)(2,1)S(1)}, u32[]{:S(2)}, u32[]{:S(2)}) collective-permute-start(bf16[2,192,128]{2,1,0:T(8,128)(2,1)S(1)} %get-tuple-element.96), channel_id=1, source_target_pairs={{0,16},{1,17},{2,18},{3,19},{4,20},{5,21},{6,22},{7,23},{8,9},{9,8... | collective-permute-start | bytes 294920 | tf_op jit(solution)/shard_map/ppermute | solution.py:282
  93.2 5.1 %collective-permute-start.21 = (bf16[1,192,128]{2,1,0:T(8,128)(2,1)S(1)}, bf16[1,192,128]{2,1,0:T(8,128)(2,1)S(1)}, u32[]{:S(2)}, u32[]{:S(2)}) collective-permute-start(bf16[1,192,128]{2,1,0:T(8,128)(2,1)S(1)} %get-tuple-element.98), channel_id=1, source_target_pairs={{0,4},{1,5},{2,6},{3,7},{4,0},{5,1},{6,2},{7,3},{8,12},{9,13},{10,... | collective-permute-start | bytes 147464 | tf_op jit(solution)/shard_map/ppermute | solution.py:282

commit v6 on v5

--- a/solution.py
+++ b/solution.py
@@ -9,6 +9,7 @@
 from jax.sharding import PartitionSpec as P
 
 HD = 128
+BINARY = HD ** (-0.5) * math.log2(math.e)
 AXES = ("slab", "weight")
 BF = jnp.bfloat16
 F32 = jnp.float32
@@ -124,24 +125,7 @@
     return total
 
 
-def attention_kernel(
-    sizes, index, q_ref, co_ref, own, even, odd, side_even, side_odd, far_even, far_odd,
-    att_ref, delta_ref, scale_ref, dq_ref, parts_even, parts_odd, near_scores, near_halves,
-    side_scores, side_halves, scores, halves,
-):
-    slab, weight = index[0], index[1]
-    slabs, weights = sizes
-    binary = HD ** (-0.5) * math.log2(math.e)
-    slab_inside = (slab > 0) & (slab < slabs - 1)
-    weight_inside = (weight > 0) & (weight < weights - 1)
-    far = [far_even.at[0], far_even.at[1], far_odd.at[0], far_odd.at[1]]
-    blocks = far + [own, even, odd, side_even, side_odd]
-    inside = [None, weight_inside, slab_inside, slab_inside & weight_inside]
-    inside += [None, None, weight_inside, None, slab_inside]
-    groups = ((scores, halves, 4), (near_scores, near_halves, 3), (side_scores, side_halves, 2))
-    kept = [ref.at[i] for ref, _, size in groups for i in range(size)]
-    kept_halves = [ref.at[i] for _, ref, size in groups for i in range(size)]
-    query = q_ref[...]
+def window_scores(query, blocks, inside, kept):
     highest = None
     for block, present, place in zip(blocks, inside, kept):
         part = dot(query, block[:, :HD], ((1,), (1,)))
@@ -149,25 +133,60 @@
             part = part + jnp.where(present, 0.0, -jnp.inf)
         place[...] = part
         highest = part if highest is None else jnp.maximum(highest, part)
-    highest = jnp.max(highest, axis=1, keepdims=True) * binary
+    return jnp.max(highest, axis=1, keepdims=True) * BINARY
+
+
+def window_values(highest, blocks, kept, kept_halves):
     total, attended = None, None
     for block, place, half_place in zip(blocks, kept, kept_halves):
-        part = jnp.exp2(place[...] * binary - highest)
+        part = jnp.exp2(place[...] * BINARY - highest)
         total = part if total is None else total + part
         half = part.astype(BF)
         place[...] = part
         half_place[...] = half
         weighted = dot(half, block[:, HD:])
         attended = weighted if attended is None else attended + weighted
-    scale = 1.0 / jnp.sum(total, axis=1, keepdims=True)
-    attended = (attended * scale).astype(BF)
+    return jnp.sum(total, axis=1, keepdims=True), attended
+
+
+def inner(index, axis, size):
+    return (index[axis] > 0) & (index[axis] < size - 1)
+
+
+def near_kernel(
+    sizes, index, q_ref, own, even, odd, side_even, side_odd,
+    high_ref, total_ref, sum_ref, near_scores, near_halves, side_scores, side_halves,
+):
+    blocks = [own, even, odd, side_even, side_odd]
+    inside = [None, None, inner(index, 1, sizes[1]), None, inner(index, 0, sizes[0])]
+    kept = [near_scores.at[i] for i in range(3)] + [side_scores.at[i] for i in range(2)]
+    halves = [near_halves.at[i] for i in range(3)] + [side_halves.at[i] for i in range(2)]
+    highest = window_scores(q_ref[...], blocks, inside, kept)
+    high_ref[...] = highest
+    total_ref[...], sum_ref[...] = window_values(highest, blocks, kept, halves)
+
+
+def attention_kernel(
+    sizes, index, q_ref, co_ref, far_even, far_odd, near_high, near_total, near_sum,
+    att_ref, delta_ref, scale_ref, dq_ref, parts_even, parts_odd, scores, halves,
+):
+    slab_inside, weight_inside = inner(index, 0, sizes[0]), inner(index, 1, sizes[1])
+    blocks = [far_even.at[0], far_even.at[1], far_odd.at[0], far_odd.at[1]]
+    inside = [None, weight_inside, slab_inside, slab_inside & weight_inside]
+    kept, kept_halves = ([ref.at[i] for i in range(4)] for ref in (scores, halves))
+    highest = window_scores(q_ref[...], blocks, inside, kept)
+    highest = jnp.maximum(highest, near_high[...])
+    shrink = jnp.exp2(near_high[...] - highest)
+    total, attended = window_values(highest, blocks, kept, kept_halves)
+    scale = 1.0 / (total + near_total[...] * shrink)
+    attended = ((attended + near_sum[...] * shrink) * scale).astype(BF)
     att_ref[...] = attended
     cotangent = co_ref[...].astype(F32)
     delta = jnp.sum(cotangent * attended.astype(F32), axis=1, keepdims=True)
     delta_ref[...] = delta
-    scale_ref[...] = scale
+    scale_ref[...] = scale * shrink
     outs = [parts_even.at[0], parts_even.at[1], parts_odd.at[0], parts_odd.at[1]]
-    dq_ref[...] = block_grads((q_ref, co_ref), delta, scale, scores, halves, far, outs, None)
+    dq_ref[...] = block_grads((q_ref, co_ref), delta, scale, scores, halves, blocks, outs, None)
 
 
 def near_grads_kernel(
@@ -321,20 +340,24 @@
     far_even, far_odd = swap(columns, slab_even), swap(columns, slab_odd)
     one = (count, 2 * HD)
     square = (count, count)
-    (
-        attended, delta, scale, grad_query, parts_even, parts_odd,
-        scores, halves, side_scores, side_halves,
-    ) = call(
+    column = (count, 1)
+    high, total, partial, scores, halves, side_scores, side_halves = call(
+        functools.partial(near_kernel, (slabs, weights)),
+        [
+            (column, F32), (column, F32), ((count, HD), F32), ((3, *square), F32),
+            ((3, *square), BF), ((2, *square), F32), ((2, *square), BF),
+        ],
+        [index, query, key_value, even, odd, side_even, side_odd],
+        scalars=1,
+    )
+    far_even, far_odd, partial = lax.optimization_barrier((far_even, far_odd, partial))
+    attended, delta, scale, grad_query, parts_even, parts_odd = call(
         functools.partial(attention_kernel, (slabs, weights)),
         [
-            ((count, HD), BF), ((count, 1), F32), ((count, 1), F32), ((count, HD), F32),
-            ((2, *one), BF), ((2, *one), BF), ((3, *square), F32), ((3, *square), BF),
-            ((2, *square), F32), ((2, *square), BF),
+            ((count, HD), BF), (column, F32), (column, F32), ((count, HD), F32),
+            ((2, *one), BF), ((2, *one), BF),
         ],
-        [
-            index, query, cotangent, key_value, even, odd,
-            side_even, side_odd, far_even, far_odd,
-        ],
+        [index, query, cotangent, far_even, far_odd, high, total, partial],
         scratch=[pltpu.VMEM((4, *square), F32), pltpu.VMEM((4, *square), BF)],
         scalars=1,
     )
@@ -344,22 +367,6 @@
         [((count, HD), F32), ((3, *one), BF)],
         [query, cotangent, key_value, even, odd, delta, scale, grad_query, scores, halves],
     )
-    (mixed,) = call(
-        mixed_kernel,
-        [((count, features), BF)],
-        [attended, full_proj],
-        final=True,
-    )
-    parts_even, parts_odd, parts_own, mixed = lax.optimization_barrier(
-        (parts_even, parts_odd, parts_own, mixed)
-    )
-
-    def summed(column):
-        total = parts_own[column + 1].astype(F32)
-        total = total + parts_even[column].astype(F32) + parts_odd[column].astype(F32)
-        return total.astype(BF)
-
-    grad_query, even, odd = lax.optimization_barrier((grad_query, summed(0), summed(1)))
     grad_query, side_even, side_odd = call(
         side_grads_kernel,
         [((count, HD), BF), (one, BF), (one, BF)],
@@ -369,7 +376,22 @@
         ],
     )
     side_even, side_odd = swap(side_even, slab_even), swap(side_odd, slab_odd)
-    even, odd = swap(even, weight_even), swap(odd, weight_odd)
+    (mixed,) = call(
+        mixed_kernel,
+        [((count, features), BF)],
+        [attended, full_proj],
+        final=True,
+    )
+    parts_even, parts_odd, parts_own, grad_query, mixed = lax.optimization_barrier(
+        (parts_even, parts_odd, parts_own, grad_query, mixed)
+    )
+
+    def summed(column):
+        total = parts_own[column + 1].astype(F32)
+        total = total + parts_even[column].astype(F32) + parts_odd[column].astype(F32)
+        return total.astype(BF)
+
+    even, odd = swap(summed(0), weight_even), swap(summed(1), weight_odd)
     half = (1 << len(steps), rows, lanes)
     factors = (2 * count, slabs // 2 * lanes)
     grad_rows, kept, send = call(

time: 99.3 us -> 99.3 us (level)
  starting transfers between devices: 49.2 us -> 42.2 us
  waiting for transfers between devices: 34.5 us -> 40.6 us
    ppermute x22, starting transfers between devices: 49.2 us -> 42.2 us  [swap(): return lax.ppermute(values, AXES, pairs)]
    ppermute x22, waiting for transfers between devices: 34.5 us -> 40.6 us  [swap(): return lax.ppermute(values, AXES, pairs)]
    pallas_call x11 -> x12, Pallas kernels: 12.7 us -> 13.6 us  [call(): pl.pallas_call(kernel, out_shape=[make(shape, kind) for shape, kind in ou...]
  transfers between devices with their start and end apart: 22 -> 22, of which waited for: 13 -> 12; matrix products, arithmetic and copies ran while one was open for 0% -> 0% of each run, Pallas kernels for 6% -> 8%
where the time goes in v6:
time: 99.3 us; the launch traced here: 99 us
  starting transfers between devices  42.2 us (42%)
  waiting for transfers between devices  40.6 us (41%)
  Pallas kernels  14.6 us (15%)
    ppermute x22, starting transfers between devices, swap(): return lax.ppermute(values, AXES, pairs)  42.2 us
    ppermute x22, waiting for transfers between devices, swap(): return lax.ppermute(values, AXES, pairs)  40.6 us
    pallas_call x12, Pallas kernels, call(): pl.pallas_call(kernel, out_shape=[make(shape, kind) for shape, kind in ou...  13.6 us
  transfers between devices with their start and end apart: 22, of which 12 were waited for; matrix products, arithmetic and copies ran while one was open for 0% of the time, Pallas kernels for 8%

profile of v6, /device:TPU:0, one launch (start us, length us, event | category | flops | bytes accessed | tf_op | source)
XLA Modules:
  0.0 99.0 jit_solution(1409323858097525135)
XLA Ops:
  0.6 1.0 %shard_map.75 = bf16[1,192,128]{2,1,0:T(8,128)(2,1)S(1)} custom-call(bf16[192,96]{1,0:T(8,128)(2,1)} %qkv_hbm.1, bf16[32,192]{1,0:T(8,128)(2,1)} %proj_hbm.1), custom_call_target="tpu_custom_call" | custom-call | tf_op jit(solution)/shard_map/pallas_call | solution.py:303
  1.7 4.1 %collective-permute-start = (bf16[1,192,128]{2,1,0:T(8,128)(2,1)S(1)}, bf16[1,192,128]{2,1,0:T(8,128)(2,1)S(1)}, u32[]{:S(2)}, u32[]{:S(2)}) collective-permute-start(bf16[1,192,128]{2,1,0:T(8,128)(2,1)S(1)} %shard_map.75), channel_id=1, source_target_pairs={{0,4},{1,5},{2,6},{3,7},{4,0},{5,1},{6,2},{7,3},{8,12},{9,13},{10,... | collective-permute-start | bytes 147464 | tf_op jit(solution)/shard_map/ppermute | solution.py:301
  5.8 2.6 %collective-permute-done = bf16[1,192,128]{2,1,0:T(8,128)(2,1)S(1)} collective-permute-done((bf16[1,192,128]{2,1,0:T(8,128)(2,1)S(1)}, bf16[1,192,128]{2,1,0:T(8,128)(2,1)S(1)}, u32[]{:S(2)}, u32[]{:S(2)}) %collective-permute-start) | collective-permute-done | bytes 49184 | tf_op jit(solution)/shard_map/ppermute | solution.py:301
  8.4 1.8 %collective-permute-start.1 = (bf16[2,192,128]{2,1,0:T(8,128)(2,1)S(1)}, bf16[2,192,128]{2,1,0:T(8,128)(2,1)S(1)}, u32[]{:S(2)}, u32[]{:S(2)}) collective-permute-start(bf16[2,192,128]{2,1,0:T(8,128)(2,1)S(1)} %pad_maximum_fusion.3), channel_id=1, source_target_pairs={{0,16},{1,17},{2,18},{3,19},{4,20},{5,21},{6,22},{7,23},{8,9},{9,8... | collective-permute-start | bytes 294920 | tf_op jit(solution)/shard_map/ppermute | solution.py:301
  10.2 2.9 %collective-permute-done.1 = bf16[2,192,128]{2,1,0:T(8,128)(2,1)S(1)} collective-permute-done((bf16[2,192,128]{2,1,0:T(8,128)(2,1)S(1)}, bf16[2,192,128]{2,1,0:T(8,128)(2,1)S(1)}, u32[]{:S(2)}, u32[]{:S(2)}) %collective-permute-start.1) | collective-permute-done | bytes 98336 | tf_op jit(solution)/shard_map/ppermute | solution.py:301
  13.1 1.8 %collective-permute-start.2 = (bf16[4,192,128]{2,1,0:T(8,128)(2,1)S(1)}, bf16[4,192,128]{2,1,0:T(8,128)(2,1)S(1)}, u32[]{:S(2)}, u32[]{:S(2)}) collective-permute-start(bf16[4,192,128]{2,1,0:T(8,128)(2,1)S(1)} %pad_maximum_fusion.2), channel_id=1, source_target_pairs={{0,1},{1,0},{2,3},{3,2},{4,5},{5,4},{6,7},{7,6},{8,10},{9,11},{10,... | collective-permute-start | bytes 589832 | tf_op jit(solution)/shard_map/ppermute | solution.py:301
  14.9 3.9 %collective-permute-done.2 = bf16[4,192,128]{2,1,0:T(8,128)(2,1)S(1)} collective-permute-done((bf16[4,192,128]{2,1,0:T(8,128)(2,1)S(1)}, bf16[4,192,128]{2,1,0:T(8,128)(2,1)S(1)}, u32[]{:S(2)}, u32[]{:S(2)}) %collective-permute-start.2) | collective-permute-done | bytes 196640 | tf_op jit(solution)/shard_map/ppermute | solution.py:301
  18.9 1.4 %collective-permute-start.3 = (bf16[8,192,128]{2,1,0:T(8,128)(2,1)S(1)}, bf16[8,192,128]{2,1,0:T(8,128)(2,1)S(1)}, u32[]{:S(2)}, u32[]{:S(2)}) collective-permute-start(bf16[8,192,128]{2,1,0:T(8,128)(2,1)S(1)} %pad_maximum_fusion), channel_id=1, source_target_pairs={{0,2},{1,3},{2,0},{3,1},{4,6},{5,7},{6,4},{7,5},{8,24},{9,25},{10,... | collective-permute-start | bytes 1179656 | tf_op jit(solution)/shard_map/ppermute | solution.py:301
  20.4 6.3 %collective-permute-done.3 = bf16[8,192,128]{2,1,0:T(8,128)(2,1)S(1)} collective-permute-done((bf16[8,192,128]{2,1,0:T(8,128)(2,1)S(1)}, bf16[8,192,128]{2,1,0:T(8,128)(2,1)S(1)}, u32[]{:S(2)}, u32[]{:S(2)}) %collective-permute-start.3) | collective-permute-done | bytes 393248 | tf_op jit(solution)/shard_map/ppermute | solution.py:301
  27.0 2.2 %collective-permute-done.4.got = bf16[16,192,128]{2,1,0:T(8,128)(2,1)S(1)} collective-permute-done((bf16[16,192,128]{2,1,0:T(8,128)(2,1)S(1)}, bf16[16,192,128]{2,1,0:T(8,128)(2,1)S(1)}, u32[]{:S(2)}, u32[]{:S(2)}) %collective-permute-start.4) | collective-permute-done | bytes 786464 | tf_op jit(solution)/shard_map/ppermute | solution.py:301
  29.2 1.4 %shard_map.76 = (bf16[256,256]{1,0:T(8,128)(2,1)S(1)}, bf16[1536,384]{1,0:T(8,128)(2,1)S(1)}, bf16[1536,128]{1,0:T(8,128)(2,1)S(1)}) custom-call(s32[2]{0:T(128)S(1)} %pad_add_fusion.index, bf16[16,192,128]{2,1,0:T(8,128)(2,1)S(1)} %constant_dynamic-update-slice_fusion.own, bf16[16,192,128]{2,1,0:T(8,128)(2,1)S(1)} %collective-permute-done.4.got, ...), custom_call_target="tpu_custom_call" | custom-call | tf_op jit(solution)/shard_map/pallas_call | solution.py:283
  31.2 4.1 %collective-permute-start.7 = (bf16[256,256]{1,0:T(8,128)(2,1)S(1)}, bf16[256,256]{1,0:T(8,128)(2,1)S(1)}, u32[]{:S(2)}, u32[]{:S(2)}) collective-permute-start(bf16[256,256]{1,0:T(8,128)(2,1)S(1)} %get-tuple-element.51.own), channel_id=1, source_target_pairs={{0,1},{1,0},{2,3},{3,2},{4,5},{5,4},{6,7},{7,6},{8,9},{9,8},{10,11... | collective-permute-start | bytes 393224 | tf_op jit(solution)/shard_map/ppermute | solution.py:301
  36.0 2.9 %collective-permute-start.5 = (bf16[256,256]{1,0:T(8,128)(2,1)S(1)}, bf16[256,256]{1,0:T(8,128)(2,1)S(1)}, u32[]{:S(2)}, u32[]{:S(2)}) collective-permute-start(bf16[256,256]{1,0:T(8,128)(2,1)S(1)} %get-tuple-element.51.own), channel_id=1, source_target_pairs={{0,8},{1,9},{2,10},{3,11},{4,12},{5,13},{6,14},{7,15},{8,0},{9,1},... | collective-permute-start | bytes 393224 | tf_op jit(solution)/shard_map/ppermute | solution.py:301
  41.6 3.6 %collective-permute-start.9 = (bf16[2,256,256]{2,1,0:T(8,128)(2,1)S(1)}, bf16[2,256,256]{2,1,0:T(8,128)(2,1)S(1)}, u32[]{:S(2)}, u32[]{:S(2)}) collective-permute-start(bf16[2,256,256]{2,1,0:T(8,128)(2,1)S(1)} %pad_maximum_fusion.1), channel_id=1, source_target_pairs={{0,8},{1,9},{2,10},{3,11},{4,12},{5,13},{6,14},{7,15},{8,0},{9,1},... | collective-permute-start | bytes 786440 | tf_op jit(solution)/shard_map/ppermute | solution.py:301
  45.3 1.4 %shard_map.79 = (f32[256,1]{1,0:T(8,128)S(1)}, f32[256,1]{1,0:T(8,128)S(1)}, f32[256,128]{1,0:T(8,128)S(1)}, f32[3,256,256]{2,1,0:T(8,128)S(1)}, bf16[3,256,256]...) custom-call(s32[2]{0:T(128)S(1)} %pad_add_fusion.index, ...), custom_call_target="tpu_custom_call" | custom-call | tf_op jit(solution)/shard_map/pallas_call | solution.py:283
  46.7 2.1 %shard_map.80 = (bf16[256,128]{1,0:T(8,128)(2,1)S(1)}, f32[256,1]{1,0:T(8,128)S(1)}, f32[256,1]{1,0:T(8,128)S(1)}, f32[256,128]{1,0:T(8,128)S(1)}, bf16[2,256,25...) custom-call(s32[2]{0:T(128)S(1)} %pad_add_fusion.index, bf16[256,128]{1,0:T(8,128)(2,1)S(1)} %get-tuple-element.56.q_ref, ...), custom_call_target="tpu_custom_call" | custom-call | tf_op jit(solution)/shard_map/pallas_call | solution.py:283
  48.8 2.6 %collective-permute-start.11 = (bf16[2,256,256]{2,1,0:T(8,128)(2,1)S(1)}, bf16[2,256,256]{2,1,0:T(8,128)(2,1)S(1)}, u32[]{:S(2)}, u32[]{:S(2)}) collective-permute-start(bf16[2,256,256]{2,1,0:T(8,128)(2,1)S(1)} %get-tuple-element.68), channel_id=1, source_target_pairs={{0,8},{1,9},{2,10},{3,11},{4,12},{5,13},{6,14},{7,15},{8,0},{9,1},... | collective-permute-start | bytes 786440 | tf_op jit(solution)/shard_map/ppermute | solution.py:301
  53.5 3.1 %collective-permute-start.15 = (bf16[256,256]{1,0:T(8,128)(2,1)S(1)}, bf16[256,256]{1,0:T(8,128)(2,1)S(1)}, u32[]{:S(2)}, u32[]{:S(2)}) collective-permute-start(bf16[256,256]{1,0:T(8,128)(2,1)S(1)} %get-tuple-element.87), channel_id=1, source_target_pairs={{0,8},{1,9},{2,10},{3,11},{4,12},{5,13},{6,14},{7,15},{8,0},{9,1},... | collective-permute-start | bytes 393224 | tf_op jit(solution)/shard_map/ppermute | solution.py:301
  57.3 1.2 %shard_map.83 = bf16[256,1536]{1,0:T(8,128)(2,1)} custom-call(bf16[256,128]{1,0:T(8,128)(2,1)S(1)} %get-tuple-element.80.att_ref, bf16[1536,128]{1,0:T(8,128)(2,1)S(1)} %get-tuple-element.53.proj_ref), custom_call_target="tpu_custom_call" | custom-call | tf_op jit(solution)/shard_map/pallas_call | solution.py:283
  59.3 4.4 %collective-permute-start.13 = (bf16[256,256]{1,0:T(8,128)(2,1)S(1)}, bf16[256,256]{1,0:T(8,128)(2,1)S(1)}, u32[]{:S(2)}, u32[]{:S(2)}) collective-permute-start(bf16[256,256]{1,0:T(8,128)(2,1)S(1)} %get-tuple-element.103), channel_id=1, source_target_pairs={{0,1},{1,0},{2,3},{3,2},{4,5},{5,4},{6,7},{7,6},{8,9},{9,8},{10,11... | collective-permute-start | bytes 393224 | tf_op jit(solution)/shard_map/ppermute | solution.py:301
  63.7 6.2 %collective-permute-done.13.even = bf16[256,256]{1,0:T(8,128)(2,1)S(1)} collective-permute-done((bf16[256,256]{1,0:T(8,128)(2,1)S(1)}, bf16[256,256]{1,0:T(8,128)(2,1)S(1)}, u32[]{:S(2)}, u32[]{:S(2)}) %collective-permute-start.13) | collective-permute-done | bytes 131104 | tf_op jit(solution)/shard_map/ppermute | solution.py:301
  69.9 1.5 %shard_map.84 = (bf16[256,384]{1,0:T(8,128)(2,1)S(1)}, bf16[512,256]{1,0:T(8,128)(2,1)S(1)}, bf16[16,192,128]{2,1,0:T(8,128)(2,1)S(1)}) custom-call(s32[2]{0:T(128)S(1)} %pad_add_fusion.index, bf16[1536,512]{1,0:T(8,128)(2,1)S(1)} %shard_map.77.turned, bf16[256,256]{1,0:T(8,128)(2,1)S(1)} %collective-permute-done.13.even, ...), custom_call_target="tpu_custom_call" | custom-call | tf_op jit(solution)/shard_map/pallas_call | solution.py:283
  71.6 1.2 %shard_map.85 = bf16[16,192,128]{2,1,0:T(8,128)(2,1)S(1)} custom-call(s32[2]{0:T(128)S(1)} %pad_add_fusion.index, bf16[1536,512]{1,0:T(8,128)(2,1)S(1)} %shard_map.77.turned, bf16[512,256]{1,0:T(8,128)(2,1)S(1)} %get-tuple-element.90.kept), custom_call_target="tpu_custom_call" | custom-call | tf_op jit(solution)/shard_map/pallas_call | solution.py:283
  72.8 1.0 %collective-permute-done.17 = bf16[16,192,128]{2,1,0:T(8,128)(2,1)S(1)} collective-permute-done((bf16[16,192,128]{2,1,0:T(8,128)(2,1)S(1)}, bf16[16,192,128]{2,1,0:T(8,128)(2,1)S(1)}, u32[]{:S(2)}, u32[]{:S(2)}) %collective-permute-start.17) | collective-permute-done | bytes 786464 | tf_op jit(solution)/shard_map/ppermute | solution.py:301
  73.9 2.4 %collective-permute-start.18 = (bf16[8,192,128]{2,1,0:T(8,128)(2,1)S(1)}, bf16[8,192,128]{2,1,0:T(8,128)(2,1)S(1)}, u32[]{:S(2)}, u32[]{:S(2)}) collective-permute-start(bf16[8,192,128]{2,1,0:T(8,128)(2,1)S(1)} %get-tuple-element.99), channel_id=1, source_target_pairs={{0,2},{1,3},{2,0},{3,1},{4,6},{5,7},{6,4},{7,5},{8,24},{9,25},{10,... | collective-permute-start | bytes 1179656 | tf_op jit(solution)/shard_map/ppermute | solution.py:301
  76.3 1.5 %shard_map.86 = bf16[256,1536]{1,0:T(8,128)(2,1)} custom-call(bf16[256,384]{1,0:T(8,128)(2,1)S(1)} %get-tuple-element.93.rows_ref, bf16[1536,384]{1,0:T(8,128)(2,1)S(1)} %get-tuple-element.52.qkv_ref), custom_call_target="tpu_custom_call" | custom-call | tf_op jit(solution)/shard_map/pallas_call | solution.py:283
  77.8 4.3 %collective-permute-done.18 = bf16[8,192,128]{2,1,0:T(8,128)(2,1)S(1)} collective-permute-done((bf16[8,192,128]{2,1,0:T(8,128)(2,1)S(1)}, bf16[8,192,128]{2,1,0:T(8,128)(2,1)S(1)}, u32[]{:S(2)}, u32[]{:S(2)}) %collective-permute-start.18) | collective-permute-done | bytes 393248 | tf_op jit(solution)/shard_map/ppermute | solution.py:301
  82.2 2.2 %collective-permute-start.19 = (bf16[4,192,128]{2,1,0:T(8,128)(2,1)S(1)}, bf16[4,192,128]{2,1,0:T(8,128)(2,1)S(1)}, u32[]{:S(2)}, u32[]{:S(2)}) collective-permute-start(bf16[4,192,128]{2,1,0:T(8,128)(2,1)S(1)} %get-tuple-element.100), channel_id=1, source_target_pairs={{0,1},{1,0},{2,3},{3,2},{4,5},{5,4},{6,7},{7,6},{8,10},{9,11},{10,... | collective-permute-start | bytes 589832 | tf_op jit(solution)/shard_map/ppermute | solution.py:301
  84.4 3.6 %collective-permute-done.19 = bf16[4,192,128]{2,1,0:T(8,128)(2,1)S(1)} collective-permute-done((bf16[4,192,128]{2,1,0:T(8,128)(2,1)S(1)}, bf16[4,192,128]{2,1,0:T(8,128)(2,1)S(1)}, u32[]{:S(2)}, u32[]{:S(2)}) %collective-permute-start.19) | collective-permute-done | bytes 196640 | tf_op jit(solution)/shard_map/ppermute | solution.py:301
  88.3 4.5 %collective-permute-done.20 = bf16[2,192,128]{2,1,0:T(8,128)(2,1)S(1)} collective-permute-done((bf16[2,192,128]{2,1,0:T(8,128)(2,1)S(1)}, bf16[2,192,128]{2,1,0:T(8,128)(2,1)S(1)}, u32[]{:S(2)}, u32[]{:S(2)}) %collective-permute-start.20) | collective-permute-done | bytes 98336 | tf_op jit(solution)/shard_map/ppermute | solution.py:301
  92.8 3.3 %collective-permute-start.21 = (bf16[1,192,128]{2,1,0:T(8,128)(2,1)S(1)}, bf16[1,192,128]{2,1,0:T(8,128)(2,1)S(1)}, u32[]{:S(2)}, u32[]{:S(2)}) collective-permute-start(bf16[1,192,128]{2,1,0:T(8,128)(2,1)S(1)} %get-tuple-element.106), channel_id=1, source_target_pairs={{0,4},{1,5},{2,6},{3,7},{4,0},{5,1},{6,2},{7,3},{8,12},{9,13},{10,... | collective-permute-start | bytes 147464 | tf_op jit(solution)/shard_map/ppermute | solution.py:301
  96.1 2.1 %collective-permute-done.21.got = bf16[1,192,128]{2,1,0:T(8,128)(2,1)S(1)} collective-permute-done((bf16[1,192,128]{2,1,0:T(8,128)(2,1)S(1)}, bf16[1,192,128]{2,1,0:T(8,128)(2,1)S(1)}, u32[]{:S(2)}, u32[]{:S(2)}) %collective-permute-start.21) | collective-permute-done | bytes 49184 | tf_op jit(solution)/shard_map/ppermute | solution.py:301
  (44 shorter events, 9.4 us)
Async XLA Ops:
  0.6 28.5 %copy-start = (bf16[256,1536]{1,0:T(8,128)(2,1)S(1)}, bf16[256,1536]{1,0:T(8,128)(2,1)}, u32[]{:S(2)}) copy-start(bf16[256,1536]{1,0:T(8,128)(2,1)} %tokens.5) | copy-start | bytes 2359300
  1.7 6.7 %collective-permute-start = (bf16[1,192,128]{2,1,0:T(8,128)(2,1)S(1)}, bf16[1,192,128]{2,1,0:T(8,128)(2,1)S(1)}, u32[]{:S(2)}, u32[]{:S(2)}) collective-permute-start(bf16[1,192,128]{2,1,0:T(8,128)(2,1)S(1)} %shard_map.75), channel_id=1, source_target_pairs={{0,4},{1,5},{2,6},{3,7},{4,0},{5,1},{6,2},{7,3},{8,12},{9,13},{10,... | collective-permute-start | bytes 147464 | tf_op jit(solution)/shard_map/ppermute | solution.py:301
  8.4 4.7 %collective-permute-start.1 = (bf16[2,192,128]{2,1,0:T(8,128)(2,1)S(1)}, bf16[2,192,128]{2,1,0:T(8,128)(2,1)S(1)}, u32[]{:S(2)}, u32[]{:S(2)}) collective-permute-start(bf16[2,192,128]{2,1,0:T(8,128)(2,1)S(1)} %pad_maximum_fusion.3), channel_id=1, source_target_pairs={{0,16},{1,17},{2,18},{3,19},{4,20},{5,21},{6,22},{7,23},{8,9},{9,8... | collective-permute-start | bytes 294920 | tf_op jit(solution)/shard_map/ppermute | solution.py:301
  13.1 5.7 %collective-permute-start.2 = (bf16[4,192,128]{2,1,0:T(8,128)(2,1)S(1)}, bf16[4,192,128]{2,1,0:T(8,128)(2,1)S(1)}, u32[]{:S(2)}, u32[]{:S(2)}) collective-permute-start(bf16[4,192,128]{2,1,0:T(8,128)(2,1)S(1)} %pad_maximum_fusion.2), channel_id=1, source_target_pairs={{0,1},{1,0},{2,3},{3,2},{4,5},{5,4},{6,7},{7,6},{8,10},{9,11},{10,... | collective-permute-start | bytes 589832 | tf_op jit(solution)/shard_map/ppermute | solution.py:301
  18.9 7.8 %collective-permute-start.3 = (bf16[8,192,128]{2,1,0:T(8,128)(2,1)S(1)}, bf16[8,192,128]{2,1,0:T(8,128)(2,1)S(1)}, u32[]{:S(2)}, u32[]{:S(2)}) collective-permute-start(bf16[8,192,128]{2,1,0:T(8,128)(2,1)S(1)} %pad_maximum_fusion), channel_id=1, source_target_pairs={{0,2},{1,3},{2,0},{3,1},{4,6},{5,7},{6,4},{7,5},{8,24},{9,25},{10,... | collective-permute-start | bytes 1179656 | tf_op jit(solution)/shard_map/ppermute | solution.py:301
  20.4 18.5 %copy-start.1 = (bf16[256,1536]{1,0:T(8,128)(2,1)S(1)}, bf16[256,1536]{1,0:T(8,128)(2,1)}, u32[]{:S(2)}) copy-start(bf16[256,1536]{1,0:T(8,128)(2,1)} %grad_out.3) | copy-start | bytes 2359300
  26.8 2.4 %collective-permute-start.4 = (bf16[16,192,128]{2,1,0:T(8,128)(2,1)S(1)}, bf16[16,192,128]{2,1,0:T(8,128)(2,1)S(1)}, u32[]{:S(2)}, u32[]{:S(2)}) collective-permute-start(bf16[16,192,128]{2,1,0:T(8,128)(2,1)S(1)} %constant_dynamic-update-slice_fusion.own), channel_id=1, source_target_pairs={{0,8},{1,9},{2,10},{3,11},{4,12},{5,13},{6,14},{7,15},{8,0},{9,1},... | collective-permute-start | bytes 2359304 | tf_op jit(solution)/shard_map/ppermute | solution.py:301
  30.5 9.4 %collective-permute-start.8 = (bf16[256,256]{1,0:T(8,128)(2,1)S(1)}, bf16[256,256]{1,0:T(8,128)(2,1)S(1)}, u32[]{:S(2)}, u32[]{:S(2)}) collective-permute-start(bf16[256,256]{1,0:T(8,128)(2,1)S(1)} %get-tuple-element.51.own), channel_id=1, source_target_pairs={{1,2},{2,1},{3,4},{4,3},{5,6},{6,5},{9,10},{10,9},{11,12},{12,11},... | collective-permute-start | bytes 393224 | tf_op jit(solution)/shard_map/ppermute | solution.py:301
  31.2 9.7 %collective-permute-start.7 = (bf16[256,256]{1,0:T(8,128)(2,1)S(1)}, bf16[256,256]{1,0:T(8,128)(2,1)S(1)}, u32[]{:S(2)}, u32[]{:S(2)}) collective-permute-start(bf16[256,256]{1,0:T(8,128)(2,1)S(1)} %get-tuple-element.51.own), channel_id=1, source_target_pairs={{0,1},{1,0},{2,3},{3,2},{4,5},{5,4},{6,7},{7,6},{8,9},{9,8},{10,11... | collective-permute-start | bytes 393224 | tf_op jit(solution)/shard_map/ppermute | solution.py:301
  35.4 5.6 %collective-permute-start.6 = (bf16[256,256]{1,0:T(8,128)(2,1)S(1)}, bf16[256,256]{1,0:T(8,128)(2,1)S(1)}, u32[]{:S(2)}, u32[]{:S(2)}) collective-permute-start(bf16[256,256]{1,0:T(8,128)(2,1)S(1)} %get-tuple-element.51.own), channel_id=1, source_target_pairs={{8,16},{9,17},{10,18},{11,19},{12,20},{13,21},{14,22},{15,23},{16,... | collective-permute-start | bytes 393224 | tf_op jit(solution)/shard_map/ppermute | solution.py:301
  36.0 4.9 %collective-permute-start.5 = (bf16[256,256]{1,0:T(8,128)(2,1)S(1)}, bf16[256,256]{1,0:T(8,128)(2,1)S(1)}, u32[]{:S(2)}, u32[]{:S(2)}) collective-permute-start(bf16[256,256]{1,0:T(8,128)(2,1)S(1)} %get-tuple-element.51.own), channel_id=1, source_target_pairs={{0,8},{1,9},{2,10},{3,11},{4,12},{5,13},{6,14},{7,15},{8,0},{9,1},... | collective-permute-start | bytes 393224 | tf_op jit(solution)/shard_map/ppermute | solution.py:301
  41.0 5.8 %collective-permute-start.10 = (bf16[2,256,256]{2,1,0:T(8,128)(2,1)S(1)}, bf16[2,256,256]{2,1,0:T(8,128)(2,1)S(1)}, u32[]{:S(2)}, u32[]{:S(2)}) collective-permute-start(bf16[2,256,256]{2,1,0:T(8,128)(2,1)S(1)} %pad_maximum_fusion.1), channel_id=1, source_target_pairs={{8,16},{9,17},{10,18},{11,19},{12,20},{13,21},{14,22},{15,23},{16,... | collective-permute-start | bytes 786440 | tf_op jit(solution)/shard_map/ppermute | solution.py:301
  41.6 5.1 %collective-permute-start.9 = (bf16[2,256,256]{2,1,0:T(8,128)(2,1)S(1)}, bf16[2,256,256]{2,1,0:T(8,128)(2,1)S(1)}, u32[]{:S(2)}, u32[]{:S(2)}) collective-permute-start(bf16[2,256,256]{2,1,0:T(8,128)(2,1)S(1)} %pad_maximum_fusion.1), channel_id=1, source_target_pairs={{0,8},{1,9},{2,10},{3,11},{4,12},{5,13},{6,14},{7,15},{8,0},{9,1},... | collective-permute-start | bytes 786440 | tf_op jit(solution)/shard_map/ppermute | solution.py:301
  48.8 9.7 %collective-permute-start.11 = (bf16[2,256,256]{2,1,0:T(8,128)(2,1)S(1)}, bf16[2,256,256]{2,1,0:T(8,128)(2,1)S(1)}, u32[]{:S(2)}, u32[]{:S(2)}) collective-permute-start(bf16[2,256,256]{2,1,0:T(8,128)(2,1)S(1)} %get-tuple-element.68), channel_id=1, source_target_pairs={{0,8},{1,9},{2,10},{3,11},{4,12},{5,13},{6,14},{7,15},{8,0},{9,1},... | collective-permute-start | bytes 786440 | tf_op jit(solution)/shard_map/ppermute | solution.py:301
  51.4 7.1 %collective-permute-start.12 = (bf16[2,256,256]{2,1,0:T(8,128)(2,1)S(1)}, bf16[2,256,256]{2,1,0:T(8,128)(2,1)S(1)}, u32[]{:S(2)}, u32[]{:S(2)}) collective-permute-start(bf16[2,256,256]{2,1,0:T(8,128)(2,1)S(1)} %get-tuple-element.69), channel_id=1, source_target_pairs={{8,16},{9,17},{10,18},{11,19},{12,20},{13,21},{14,22},{15,23},{16,... | collective-permute-start | bytes 786440 | tf_op jit(solution)/shard_map/ppermute | solution.py:301
  53.5 10.2 %collective-permute-start.15 = (bf16[256,256]{1,0:T(8,128)(2,1)S(1)}, bf16[256,256]{1,0:T(8,128)(2,1)S(1)}, u32[]{:S(2)}, u32[]{:S(2)}) collective-permute-start(bf16[256,256]{1,0:T(8,128)(2,1)S(1)} %get-tuple-element.87), channel_id=1, source_target_pairs={{0,8},{1,9},{2,10},{3,11},{4,12},{5,13},{6,14},{7,15},{8,0},{9,1},... | collective-permute-start | bytes 393224 | tf_op jit(solution)/shard_map/ppermute | solution.py:301
  56.6 7.1 %collective-permute-start.16 = (bf16[256,256]{1,0:T(8,128)(2,1)S(1)}, bf16[256,256]{1,0:T(8,128)(2,1)S(1)}, u32[]{:S(2)}, u32[]{:S(2)}) collective-permute-start(bf16[256,256]{1,0:T(8,128)(2,1)S(1)} %get-tuple-element.88), channel_id=1, source_target_pairs={{8,16},{9,17},{10,18},{11,19},{12,20},{13,21},{14,22},{15,23},{16,... | collective-permute-start | bytes 393224 | tf_op jit(solution)/shard_map/ppermute | solution.py:301
  58.6 5.1 %collective-permute-start.14 = (bf16[256,256]{1,0:T(8,128)(2,1)S(1)}, bf16[256,256]{1,0:T(8,128)(2,1)S(1)}, u32[]{:S(2)}, u32[]{:S(2)}) collective-permute-start(bf16[256,256]{1,0:T(8,128)(2,1)S(1)} %get-tuple-element.102), channel_id=1, source_target_pairs={{1,2},{2,1},{3,4},{4,3},{5,6},{6,5},{9,10},{10,9},{11,12},{12,11},... | collective-permute-start | bytes 393224 | tf_op jit(solution)/shard_map/ppermute | solution.py:301
  59.3 10.6 %collective-permute-start.13 = (bf16[256,256]{1,0:T(8,128)(2,1)S(1)}, bf16[256,256]{1,0:T(8,128)(2,1)S(1)}, u32[]{:S(2)}, u32[]{:S(2)}) collective-permute-start(bf16[256,256]{1,0:T(8,128)(2,1)S(1)} %get-tuple-element.103), channel_id=1, source_target_pairs={{0,1},{1,0},{2,3},{3,2},{4,5},{5,4},{6,7},{7,6},{8,9},{9,8},{10,11... | collective-permute-start | bytes 393224 | tf_op jit(solution)/shard_map/ppermute | solution.py:301
  71.4 2.4 %collective-permute-start.17 = (bf16[16,192,128]{2,1,0:T(8,128)(2,1)S(1)}, bf16[16,192,128]{2,1,0:T(8,128)(2,1)S(1)}, u32[]{:S(2)}, u32[]{:S(2)}) collective-permute-start(bf16[16,192,128]{2,1,0:T(8,128)(2,1)S(1)} %get-tuple-element.89), channel_id=1, source_target_pairs={{0,8},{1,9},{2,10},{3,11},{4,12},{5,13},{6,14},{7,15},{8,0},{9,1},... | collective-permute-start | bytes 2359304 | tf_op jit(solution)/shard_map/ppermute | solution.py:301
  73.9 8.1 %collective-permute-start.18 = (bf16[8,192,128]{2,1,0:T(8,128)(2,1)S(1)}, bf16[8,192,128]{2,1,0:T(8,128)(2,1)S(1)}, u32[]{:S(2)}, u32[]{:S(2)}) collective-permute-start(bf16[8,192,128]{2,1,0:T(8,128)(2,1)S(1)} %get-tuple-element.99), channel_id=1, source_target_pairs={{0,2},{1,3},{2,0},{3,1},{4,6},{5,7},{6,4},{7,5},{8,24},{9,25},{10,... | collective-permute-start | bytes 1179656 | tf_op jit(solution)/shard_map/ppermute | solution.py:301
  82.2 5.9 %collective-permute-start.19 = (bf16[4,192,128]{2,1,0:T(8,128)(2,1)S(1)}, bf16[4,192,128]{2,1,0:T(8,128)(2,1)S(1)}, u32[]{:S(2)}, u32[]{:S(2)}) collective-permute-start(bf16[4,192,128]{2,1,0:T(8,128)(2,1)S(1)} %get-tuple-element.100), channel_id=1, source_target_pairs={{0,1},{1,0},{2,3},{3,2},{4,5},{5,4},{6,7},{7,6},{8,10},{9,11},{10,... | collective-permute-start | bytes 589832 | tf_op jit(solution)/shard_map/ppermute | solution.py:301
  88.1 4.7 %collective-permute-start.20 = (bf16[2,192,128]{2,1,0:T(8,128)(2,1)S(1)}, bf16[2,192,128]{2,1,0:T(8,128)(2,1)S(1)}, u32[]{:S(2)}, u32[]{:S(2)}) collective-permute-start(bf16[2,192,128]{2,1,0:T(8,128)(2,1)S(1)} %get-tuple-element.104), channel_id=1, source_target_pairs={{0,16},{1,17},{2,18},{3,19},{4,20},{5,21},{6,22},{7,23},{8,9},{9,8... | collective-permute-start | bytes 294920 | tf_op jit(solution)/shard_map/ppermute | solution.py:301
  92.8 5.4 %collective-permute-start.21 = (bf16[1,192,128]{2,1,0:T(8,128)(2,1)S(1)}, bf16[1,192,128]{2,1,0:T(8,128)(2,1)S(1)}, u32[]{:S(2)}, u32[]{:S(2)}) collective-permute-start(bf16[1,192,128]{2,1,0:T(8,128)(2,1)S(1)} %get-tuple-element.106), channel_id=1, source_target_pairs={{0,4},{1,5},{2,6},{3,7},{4,0},{5,1},{6,2},{7,3},{8,12},{9,13},{10,... | collective-permute-start | bytes 147464 | tf_op jit(solution)/shard_map/ppermute | solution.py:301
